TPU v7x, 1024 devices: a whole 4x4x32 slice. The times are simulated.
1024 devices in a mesh: seq: 64 (over x, z_lo, core), head: 16 (over y, z_hi).
Axes of the slice: x: 4, y: 4, z: 32 (z_hi: 4, z_lo: 8; z = z_hi * 8 + z_lo), core: 2. Of those that a mesh axis runs over, the one named last changes fastest.
Arguments:
- queries: bfloat16 [16384, 64, 128], P('seq', 'head'), may hold values from -100 to 100
- key_states: bfloat16 [16384, 4, 128], P('seq'), may hold values from -6.7 to 6.7
- values: bfloat16 [16384, 4, 128], P('seq'), may hold values from -6 to 6
- grad_out: bfloat16 [16384, 64, 128], P('seq', 'head'), may hold values from -6 to 6
- picked_blocks: int32 [256, 4, 16], P('seq'), may hold values from -1 to 255, as said below
Outputs:
- grad_queries: float32 [16384, 64, 128], P('seq', 'head')
- grad_keys: float32 [16384, 4, 128], P(('seq', 'head'))
- grad_values: float32 [16384, 4, 128], P(('seq', 'head'))
Inputs may be any that keep to these rules, and one draw needn't show every extreme that they name: picked_blocks[b, g, 0] = b. The query blocks come in runs of 256 / 64 (run s holds blocks s * 4 onward); for each run s and group g, the entries j >= 1 of the run's blocks that are not -1 name blocks of distinct runs, all lower than s, and there are exactly min(s, 60) of them.
All inputs are finite; a program needn't handle non-finite values.
Results may differ from a plain program's by a relative error of at most 0.02.
Values may be sent and summed in bfloat16 or wider, within the bound.
No kernel may reach another device: no remote copies, remote signals or barrier semaphores. Data moves between devices by JAX's collectives and lax.ppermute only.
A program may use at most 64 MiB of HBM per device.

v0:
```python
import jax
import jax.numpy as jnp
from jax import lax
from jax.sharding import PartitionSpec as P

G = 4
HPG = 16
BLK = 64
KSEL = 16


NEG = -1e30


def block_grads(operands):
    query_pair, grad_pair, key_pair, value_pair, live_pair = operands
    block_len = query_pair.shape[1]
    factor = query_pair.shape[3] ** (-0.5)
    scores = (
        jnp.einsum("athd,ajkd->ahtjk", query_pair, key_pair, preferred_element_type=jnp.float32)
        * factor
    )
    offsets = jnp.arange(block_len, dtype=jnp.int32)
    causal = offsets[None, :] <= offsets[:, None]
    leading = jnp.arange(key_pair.shape[1], dtype=jnp.int32) == 0
    visible = live_pair[:, None, None, :, None] & (
        jnp.logical_not(leading)[None, None, None, :, None] | causal[None, None, :, None, :]
    )
    scores = jnp.where(visible, scores, NEG)
    maxima = jnp.max(scores, axis=(3, 4), keepdims=True)
    weights = jnp.where(visible, jnp.exp(scores - maxima), 0.0)
    attend = weights / jnp.sum(weights, axis=(3, 4), keepdims=True)
    attend_low = attend.astype(jnp.bfloat16)
    grad_prob = jnp.einsum(
        "athe,ajke->ahtjk", grad_pair, value_pair, preferred_element_type=jnp.float32
    )
    row_dot = jnp.sum(attend * grad_prob, axis=(3, 4), keepdims=True)
    dscore = (attend * (grad_prob - row_dot)).astype(jnp.bfloat16)
    grad_query = (
        jnp.einsum("ahtjk,ajkd->athd", dscore, key_pair, preferred_element_type=jnp.float32)
        * factor
    )
    grad_key = (
        jnp.einsum("ahtjk,athd->ajkd", dscore, query_pair, preferred_element_type=jnp.float32)
        * factor
    )
    grad_value = jnp.einsum(
        "ahtjk,athe->ajke", attend_low, grad_pair, preferred_element_type=jnp.float32
    )
    return (grad_query, grad_key, grad_value)


def on_device(queries, key_states, values, grad_out, picked_blocks):
    tokens_dev, heads_dev, width_qk = queries.shape
    width_v = grad_out.shape[2]
    block_count = tokens_dev // BLK
    shard_count = lax.axis_size("seq")
    head_index = lax.axis_index("head")
    run_total = HPG // heads_dev
    group_id = head_index // run_total
    own_keys = lax.dynamic_index_in_dim(key_states, group_id, 1, keepdims=False)
    own_values = lax.dynamic_index_in_dim(values, group_id, 1, keepdims=False)
    own_picks = lax.dynamic_index_in_dim(picked_blocks, group_id, 1, keepdims=False)
    first_keys = own_keys.reshape(block_count, 1, BLK, width_qk)
    first_values = own_values.reshape(block_count, 1, BLK, width_v)
    remote = own_picks[:, 1:]
    owner_shard = jnp.where(remote >= 0, remote // block_count, -1)
    local_slot = jnp.where(remote >= 0, remote % block_count, -1)
    shard_ids = jnp.arange(shard_count, dtype=jnp.int32)
    owner_match = owner_shard[:, :, None] == shard_ids[None, None, :]
    wanted = jnp.max(jnp.where(owner_match, local_slot[:, :, None], -1), axis=(0, 1))
    asked_block = lax.all_to_all(wanted[:, None], "seq", split_axis=0, concat_axis=0, tiled=True)[
        :, 0
    ]
    chosen = (asked_block[:, None] == jnp.arange(block_count, dtype=jnp.int32)[None, :]).astype(
        jnp.bfloat16
    )
    key_rows = own_keys.reshape(block_count, BLK * width_qk)
    value_rows = own_values.reshape(block_count, BLK * width_v)
    send_keys = (
        jnp.dot(chosen, key_rows, preferred_element_type=jnp.float32)
        .astype(jnp.bfloat16)
        .reshape(shard_count, BLK, width_qk)
    )
    send_values = (
        jnp.dot(chosen, value_rows, preferred_element_type=jnp.float32)
        .astype(jnp.bfloat16)
        .reshape(shard_count, BLK, width_v)
    )
    got_keys, got_values = (
        lax.all_to_all(send_keys, "seq", split_axis=0, concat_axis=0, tiled=True),
        lax.all_to_all(send_values, "seq", split_axis=0, concat_axis=0, tiled=True),
    )
    safe_owner = jnp.maximum(owner_shard, 0)
    far_keys = jnp.take(got_keys, safe_owner, axis=0)
    far_values = jnp.take(got_values, safe_owner, axis=0)
    all_keys = jnp.concatenate([first_keys, far_keys], axis=1)
    all_values = jnp.concatenate([first_values, far_values], axis=1)
    live_slots = jnp.concatenate([jnp.ones((block_count, 1), dtype=bool), remote >= 0], axis=1)
    back_select = owner_match.reshape(block_count * (KSEL - 1), shard_count)
    pair_count = block_count // 2
    query_pairs = queries.reshape(pair_count, 2, BLK, heads_dev, width_qk)
    grad_pairs = grad_out.reshape(pair_count, 2, BLK, heads_dev, width_v)
    key_pairs = all_keys.reshape(pair_count, 2, KSEL, BLK, width_qk)
    value_pairs = all_values.reshape(pair_count, 2, KSEL, BLK, width_v)
    live_pairs = live_slots.reshape(pair_count, 2, KSEL)
    grad_query, grad_key, grad_value = lax.map(
        block_grads, (query_pairs, grad_pairs, key_pairs, value_pairs, live_pairs)
    )
    grad_queries = grad_query.reshape(tokens_dev, heads_dev, width_qk)
    grad_key = grad_key.reshape(block_count, KSEL, BLK, width_qk)
    grad_value = grad_value.reshape(block_count, KSEL, BLK, width_v)
    select_low = back_select.astype(jnp.bfloat16)
    far_key_parts = (
        grad_key[:, 1:].astype(jnp.bfloat16).reshape(block_count * (KSEL - 1), BLK * width_qk)
    )
    far_value_parts = (
        grad_value[:, 1:].astype(jnp.bfloat16).reshape(block_count * (KSEL - 1), BLK * width_v)
    )
    back_keys = (
        jnp.einsum("ps,px->sx", select_low, far_key_parts, preferred_element_type=jnp.float32)
        .astype(jnp.bfloat16)
        .reshape(shard_count, BLK, width_qk)
    )
    back_values = (
        jnp.einsum("ps,px->sx", select_low, far_value_parts, preferred_element_type=jnp.float32)
        .astype(jnp.bfloat16)
        .reshape(shard_count, BLK, width_v)
    )
    returned_keys, returned_values = (
        lax.all_to_all(back_keys, "seq", split_axis=0, concat_axis=0, tiled=True),
        lax.all_to_all(back_values, "seq", split_axis=0, concat_axis=0, tiled=True),
    )
    key_total = jnp.einsum(
        "rq,rx->qx",
        chosen,
        returned_keys.reshape(shard_count, BLK * width_qk),
        preferred_element_type=jnp.float32,
    )
    value_total = jnp.einsum(
        "rq,rx->qx",
        chosen,
        returned_values.reshape(shard_count, BLK * width_v),
        preferred_element_type=jnp.float32,
    )
    key_total = key_total + grad_key[:, 0].reshape(block_count, BLK * width_qk)
    value_total = value_total + grad_value[:, 0].reshape(block_count, BLK * width_v)
    key_total = key_total.reshape(tokens_dev, width_qk)
    value_total = value_total.reshape(tokens_dev, width_v)
    group_mask = (jnp.arange(G, dtype=jnp.int32) == group_id).astype(jnp.float32)
    key_term = key_total[:, None, :] * group_mask[None, :, None]
    value_term = value_total[:, None, :] * group_mask[None, :, None]
    grad_keys, grad_values = (
        lax.psum_scatter(key_term, "head", scatter_dimension=0, tiled=True),
        lax.psum_scatter(value_term, "head", scatter_dimension=0, tiled=True),
    )
    return (grad_queries, grad_keys, grad_values)


def solution(mesh):
    placed = (
        P("seq", "head", None),
        P("seq", None, None),
        P("seq", None, None),
        P("seq", "head", None),
        P("seq", None, None),
    )
    return jax.shard_map(
        on_device,
        mesh=mesh,
        in_specs=placed,
        out_specs=(
            P("seq", "head", None),
            P(("seq", "head"), None, None),
            P(("seq", "head"), None, None),
        ),
        check_vma=False,
    )
```

profile of v0, /device:TPU:244, one launch (start us, length us, event | category | flops | bytes accessed | tf_op | source)
XLA Modules:
  0.0 700.8 jit_solution(4428994895063365288)
XLA Ops:
  8.3 0.7 copy.54
  9.1 13.1 %all-to-all-start = ((s32[64,1,1]{2,1,0:T(1,128)}), s32[64,1,1]{2,1,0:T(1,128)S(1)}, u32[]{:S(2)}, u32[]{:S(2)}) async-start(s32[64,1,1]{2,1,0:T(1,128)} %copy.54), calls=%async_computation | async-start | bytes 65536 | tf_op jit(solution)/shard_map/all_to_all | solution.py:72
  22.1 1.3 constant_dynamic-slice_fusion.5
  23.5 2.0 all-to-all-done
  25.4 1.2 reduce
  27.2 1.3 copy.88
  28.4 13.7 %all-to-all-start.2 = ((bf16[64,64,128]{2,1,0:T(8,128)(2,1)}), bf16[64,64,128]{2,1,0:T(8,128)(2,1)S(1)}, u32[]{:S(2)}, u32[]{:S(2)}) async-start(bf16[64,64,128]{2,1,0:T(8,128)(2,1)} %bitcast.62), calls=%async_computation.2 | async-start | bytes 2097152 | tf_op jit(solution)/shard_map/all_to_all | solution.py:92
  42.6 1.2 copy.87
  43.9 44.2 %all-to-all-done.2 = bf16[64,64,128]{2,1,0:T(8,128)(2,1)S(1)} async-done(((bf16[64,64,128]{2,1,0:T(8,128)(2,1)}), bf16[64,64,128]{2,1,0:T(8,128)(2,1)S(1)}, u32[]{:S(2)}, u32[]{:S(2)}) %all-to-all-start.2) | async-done | bytes 1048608 | tf_op jit(solution)/shard_map/all_to_all | solution.py:92
  88.1 13.5 %all-to-all-start.1 = ((bf16[64,64,128]{2,1,0:T(8,128)(2,1)}), bf16[64,64,128]{2,1,0:T(8,128)(2,1)S(1)}, u32[]{:S(2)}, u32[]{:S(2)}) async-start(bf16[64,64,128]{2,1,0:T(8,128)(2,1)} %bitcast.59), calls=%async_computation.1 | async-start | bytes 2097152 | tf_op jit(solution)/shard_map/all_to_all | solution.py:91
  101.9 0.7 gather_fusion.1
  102.6 44.9 %all-to-all-done.1 = bf16[64,64,128]{2,1,0:T(8,128)(2,1)S(1)} async-done(((bf16[64,64,128]{2,1,0:T(8,128)(2,1)}), bf16[64,64,128]{2,1,0:T(8,128)(2,1)S(1)}, u32[]{:S(2)}, u32[]{:S(2)}) %all-to-all-start.1) | async-done | bytes 1048608 | tf_op jit(solution)/shard_map/all_to_all | solution.py:91
  147.5 0.7 gather_fusion
  149.2 23.8 %while.14 = (s32[]{:T(128)}, f32[2,2,64,4,128]{4,3,2,1,0:T(4,128)}, f32[2,2,16,64,128]{4,3,2,1,0:T(8,128)}, f32[2,2,16,64,128]{4,3,2,1,0:T(8,128)}, bf16[2,2,16,...) while((s32[]{:T(128)}, f32[2,2,64,4,128]{4,3,2,1,0:T(4,128)}, ...), condition=%wide.region_5.7_spmd, body=%wide.region_1.6_spmd.sunk | while | flops 686819840 | bytes 46700868 | solution.py:107
  149.6 1.0 constant_dynamic-slice_fusion.9
  150.6 0.9 fusion.73
  151.5 1.4 fusion.74
  152.9 1.7 fusion.79
  154.6 1.7 fusion.75
  156.3 1.6 fusion.76
  157.9 0.8 fusion.77
  158.7 1.5 fusion.78
  160.2 0.9 copy_dynamic-update-slice_fusion.2
  161.5 1.0 constant_dynamic-slice_fusion.9
  162.5 0.9 fusion.73
  163.4 1.4 fusion.74
  164.8 1.7 fusion.79
  166.4 1.8 fusion.75
  168.2 1.6 fusion.76
  169.8 0.8 fusion.77
  170.6 1.6 fusion.78
  172.2 0.9 copy_dynamic-update-slice_fusion.2
  173.0 1.7 slice.46
  176.1 1.3 copy.94
  177.4 13.5 %all-to-all-start.4 = ((bf16[64,64,128]{2,1,0:T(8,128)(2,1)}), bf16[64,64,128]{2,1,0:T(8,128)(2,1)S(1)}, u32[]{:S(2)}, u32[]{:S(2)}) async-start(bf16[64,64,128]{2,1,0:T(8,128)(2,1)} %bitcast.80), calls=%async_computation.4 | async-start | bytes 2097152 | tf_op jit(solution)/shard_map/all_to_all | solution.py:132
  191.0 1.7 slice.47
  194.1 1.2 copy.90
  195.3 41.6 %all-to-all-done.4 = bf16[64,64,128]{2,1,0:T(8,128)(2,1)S(1)} async-done(((bf16[64,64,128]{2,1,0:T(8,128)(2,1)}), bf16[64,64,128]{2,1,0:T(8,128)(2,1)S(1)}, u32[]{:S(2)}, u32[]{:S(2)}) %all-to-all-start.4) | async-done | bytes 1048608 | tf_op jit(solution)/shard_map/all_to_all | solution.py:132
  236.9 13.5 %all-to-all-start.3 = ((bf16[64,64,128]{2,1,0:T(8,128)(2,1)}), bf16[64,64,128]{2,1,0:T(8,128)(2,1)S(1)}, u32[]{:S(2)}, u32[]{:S(2)}) async-start(bf16[64,64,128]{2,1,0:T(8,128)(2,1)} %bitcast.68), calls=%async_computation.3 | async-start | bytes 2097152 | tf_op jit(solution)/shard_map/all_to_all | solution.py:131
  250.5 0.9 slice_bitcast_fusion
  251.4 0.9 slice_bitcast_fusion.1
  252.3 0.7 convolution_add_fusion
  253.1 43.2 %all-to-all-done.3 = bf16[64,64,128]{2,1,0:T(8,128)(2,1)S(1)} async-done(((bf16[64,64,128]{2,1,0:T(8,128)(2,1)}), bf16[64,64,128]{2,1,0:T(8,128)(2,1)S(1)}, u32[]{:S(2)}, u32[]{:S(2)}) %all-to-all-start.3) | async-done | bytes 1048608 | tf_op jit(solution)/shard_map/all_to_all | solution.py:131
  297.2 1.3 broadcast_multiply_fusion
  298.5 1.3 dynamic-slice
  300.4 390.8 %all-reduce.6.cloned.1.call-done = (f32[256,4,128]{2,1,0:T(4,128)}, f32[256,4,128]{2,1,0:T(4,128)}) async-done(((f32[256,4,128]{2,1,0:T(4,128)}, f32[256,4,128]{2,1,0:T(4,128)}), (f32[256,4,128]{2,1,0:T(4,128)}, f32[256,4,128]{2,1,0:T(4,128)})) %all-reduce.6.cloned.1.call-update) | async-done | bytes 1048592
  691.2 1.4 constant_dynamic-slice_fusion.4
  692.6 1.4 constant_dynamic-slice_fusion.3
  (57 shorter events, 7.7 us)
Async XLA Ops:
  7.2 0.7 copy-start
  9.1 16.4 %all-to-all-start = ((s32[64,1,1]{2,1,0:T(1,128)}), s32[64,1,1]{2,1,0:T(1,128)S(1)}, u32[]{:S(2)}, u32[]{:S(2)}) async-start(s32[64,1,1]{2,1,0:T(1,128)} %copy.54), calls=%async_computation | async-start | bytes 65536 | tf_op jit(solution)/shard_map/all_to_all | solution.py:72
  28.4 59.7 %all-to-all-start.2 = ((bf16[64,64,128]{2,1,0:T(8,128)(2,1)}), bf16[64,64,128]{2,1,0:T(8,128)(2,1)S(1)}, u32[]{:S(2)}, u32[]{:S(2)}) async-start(bf16[64,64,128]{2,1,0:T(8,128)(2,1)} %bitcast.62), calls=%async_computation.2 | async-start | bytes 2097152 | tf_op jit(solution)/shard_map/all_to_all | solution.py:92
  88.1 59.5 %all-to-all-start.1 = ((bf16[64,64,128]{2,1,0:T(8,128)(2,1)}), bf16[64,64,128]{2,1,0:T(8,128)(2,1)S(1)}, u32[]{:S(2)}, u32[]{:S(2)}) async-start(bf16[64,64,128]{2,1,0:T(8,128)(2,1)} %bitcast.59), calls=%async_computation.1 | async-start | bytes 2097152 | tf_op jit(solution)/shard_map/all_to_all | solution.py:91
  148.3 1.0 copy-start.1
  150.6 2.3 copy-start.2
  154.6 3.4 copy-start.3
  162.5 2.3 copy-start.2
  166.4 3.4 copy-start.3
  177.4 59.5 %all-to-all-start.4 = ((bf16[64,64,128]{2,1,0:T(8,128)(2,1)}), bf16[64,64,128]{2,1,0:T(8,128)(2,1)S(1)}, u32[]{:S(2)}, u32[]{:S(2)}) async-start(bf16[64,64,128]{2,1,0:T(8,128)(2,1)} %bitcast.80), calls=%async_computation.4 | async-start | bytes 2097152 | tf_op jit(solution)/shard_map/all_to_all | solution.py:132
  236.9 59.5 %all-to-all-start.3 = ((bf16[64,64,128]{2,1,0:T(8,128)(2,1)}), bf16[64,64,128]{2,1,0:T(8,128)(2,1)S(1)}, u32[]{:S(2)}, u32[]{:S(2)}) async-start(bf16[64,64,128]{2,1,0:T(8,128)(2,1)} %bitcast.68), calls=%async_computation.3 | async-start | bytes 2097152 | tf_op jit(solution)/shard_map/all_to_all | solution.py:131
  250.4 440.8 %all-reduce.6.cloned.1.call-start = ((), (), s32[]{:S(2)}) async-start(), calls=%async_computation.5 | async-start | bytes 2097152
Sparse Core Ops, SparseCore 0:
  298.6 392.5 all-reduce.5
where the time goes:
time: 702 us; the launch traced here: 701 us
  waiting for transfers between devices  567 us (81%)
  starting transfers between devices  67.3 us (10%)
  local copies, waits for them, and re-layouts  25.1 us (4%)
  matrix products  16.7 us (2%)
  between operations  14.9 us (2%)
  other arithmetic  9.8 us (1%)
    unnamed x2, waiting for transfers between devices  391 us
    all_to_all x1, waiting for transfers between devices, on_device(): lax.all_to_all(send_keys, 'seq', split_axis=0, concat_axis=0, tiled=True)  44.9 us
    all_to_all x1, waiting for transfers between devices, on_device(): lax.all_to_all(send_values, 'seq', split_axis=0, concat_axis=0, tiled=True)  44.2 us
    all_to_all x1, waiting for transfers between devices, on_device(): lax.all_to_all(back_keys, 'seq', split_axis=0, concat_axis=0, tiled=True)  43.2 us
    all_to_all x1, waiting for transfers between devices, on_device(): lax.all_to_all(back_values, 'seq', split_axis=0, concat_axis=0, tiled=True)  41.6 us
  transfers between devices with their start and end apart: 6, of which 6 were waited for; matrix products, arithmetic and copies ran while one was open for 2% of the time, Pallas kernels for 0%

commit v1 on v0

v1 whole, which is shorter than its diff:
```python
import functools

import jax
import jax.numpy as jnp
from jax import lax
from jax.experimental import pallas as pl
from jax.experimental.pallas import tpu as pltpu
from jax.sharding import Mesh
from jax.sharding import PartitionSpec as P

HPG = 16
BLK = 64
KSEL = 16
NEG = -1e30

NX, ZL, NC, NY, ZH = 4, 8, 2, 4, 4
NZ = ZL * ZH
SEQ = ("x", "zl", "c")
HEAD = ("y", "zh")
XC = ("x", "c")
AXES = SEQ + HEAD

F32 = jnp.float32
BF16 = jnp.bfloat16


def ring_pairs(step):
    def number(x, z, c, y):
        return (((x * ZL + z % ZL) * NC + c) * NY + y) * ZH + z // ZL

    return [
        (number(x, z, c, y), number(x, (z + step) % NZ, c, y))
        for x in range(NX)
        for z in range(NZ)
        for c in range(NC)
        for y in range(NY)
    ]


def shift_z(array, step):
    return lax.ppermute(array, AXES, ring_pairs(step))


def attend_body(slot_ref, q_ref, g_ref, own_ref, bias_ref, got_ref, dq_ref, down_ref, back_ref, k_ref, v_ref):
    b = pl.program_id(0)
    rows = q_ref.shape[0]
    width = q_ref.shape[1]
    heads = rows // BLK
    factor = width ** (-0.5)

    @pl.when(b == 0)
    def _():
        back_ref[...] = jnp.zeros_like(back_ref)

    k_ref[0:BLK, :] = own_ref[0, :, :width]
    v_ref[0:BLK, :] = own_ref[0, :, width:]
    for j in range(1, KSEL):
        slot = jnp.maximum(slot_ref[b, j], 0)
        k_ref[j * BLK : (j + 1) * BLK, :] = got_ref[slot, :, :width]
        v_ref[j * BLK : (j + 1) * BLK, :] = got_ref[slot, :, width:]
    q = q_ref[...]
    g = g_ref[...]
    k = k_ref[...]
    v = v_ref[...]
    nt = (((1,), (1,)), ((), ()))
    scores = lax.dot_general(k, q, nt, preferred_element_type=F32) * factor
    key_row = lax.broadcasted_iota(jnp.int32, (BLK, rows), 0)
    token = lax.broadcasted_iota(jnp.int32, (BLK, rows), 1) // heads
    own = jnp.where(key_row <= token, scores[:BLK], NEG)
    far = scores[BLK:].reshape(KSEL - 1, BLK, rows) + bias_ref[0, 1:][:, None, :]
    scores = jnp.concatenate([own, far.reshape((KSEL - 1) * BLK, rows)], axis=0)
    weights = jnp.exp(scores - jnp.max(scores, axis=0, keepdims=True))
    attend = weights * (1.0 / jnp.sum(weights, axis=0, keepdims=True))
    grad_prob = lax.dot_general(v, g, nt, preferred_element_type=F32)
    row_dot = jnp.sum(attend * grad_prob, axis=0, keepdims=True)
    dscore = (attend * (grad_prob - row_dot)).astype(BF16)
    tn = (((0,), (0,)), ((), ()))
    nn = (((1,), (0,)), ((), ()))
    dq = lax.dot_general(k, dscore, tn, preferred_element_type=F32) * factor
    dq_ref[...] = dq.T
    dk = lax.dot_general(dscore, q, nn, preferred_element_type=F32) * factor
    dv = lax.dot_general(attend.astype(BF16), g, nn, preferred_element_type=F32)
    down_ref[0, :, :width] = dk[:BLK]
    down_ref[0, :, width:] = dv[:BLK]
    for j in range(1, KSEL):
        slot = slot_ref[b, j]

        @pl.when(slot >= 0)
        def _():
            back_ref[slot, :, :width] = dk[j * BLK : (j + 1) * BLK].astype(BF16)
            back_ref[slot, :, width:] = dv[j * BLK : (j + 1) * BLK].astype(BF16)


def attend_grads(slots, q_rows, g_rows, own, bias, got):
    blocks = slots.shape[0]
    total, width = q_rows.shape
    rows = total // blocks
    row_spec = pl.BlockSpec((rows, width), lambda b, s: (b, 0))
    own_spec = pl.BlockSpec((1, BLK, 2 * width), lambda b, s: (b, 0, 0))
    whole = pl.BlockSpec(got.shape, lambda b, s: (0, 0, 0))
    return pl.pallas_call(
        attend_body,
        grid_spec=pltpu.PrefetchScalarGridSpec(
            num_scalar_prefetch=1,
            grid=(blocks,),
            in_specs=[row_spec, row_spec, own_spec, pl.BlockSpec((1, KSEL, rows), lambda b, s: (b, 0, 0)), whole],
            out_specs=[row_spec, own_spec, whole],
            scratch_shapes=[pltpu.VMEM((KSEL * BLK, width), BF16), pltpu.VMEM((KSEL * BLK, width), BF16)],
        ),
        out_shape=[
            jax.ShapeDtypeStruct((total, width), F32),
            jax.ShapeDtypeStruct((blocks, BLK, 2 * width), F32),
            jax.ShapeDtypeStruct(got.shape, BF16),
        ],
        compiler_params=pltpu.CompilerParams(dimension_semantics=("arbitrary",), vmem_limit_bytes=48 * 2**20),
        name="attend_grads",
    )(slots, q_rows, g_rows, own, bias, got)


def pick_body(want_ref, home_ref, *refs):
    out_ref = refs[-1]
    for k, near_ref in enumerate(refs[:-1]):
        zl = lax.rem(home_ref[0] + k, ZL)
        for peer in range(NX * NC):
            slot = jnp.maximum(want_ref[peer, zl], 0)
            out_ref[peer, zl] = near_ref[slot]


def pick_blocks(want, home, near):
    blocks, rows, width = near[0].shape
    shape = (NX * NC, ZL, rows, width)
    spec = pl.BlockSpec((blocks, rows, width), lambda i, w, h: (0, 0, 0))
    return pl.pallas_call(
        pick_body,
        grid_spec=pltpu.PrefetchScalarGridSpec(
            num_scalar_prefetch=2,
            grid=(1,),
            in_specs=[spec] * ZL,
            out_specs=pl.BlockSpec(shape, lambda i, w, h: (0, 0, 0, 0)),
        ),
        out_shape=jax.ShapeDtypeStruct(shape, near[0].dtype),
        compiler_params=pltpu.CompilerParams(vmem_limit_bytes=32 * 2**20),
        name="pick_blocks",
    )(want, home, *near)


def gather_body(want_ref, home_ref, in_ref, out_ref, sum_ref):
    zl = lax.rem(home_ref[0] + pl.program_id(0), ZL)
    sum_ref[...] = jnp.zeros_like(sum_ref)
    for peer in range(NX * NC):
        slot = want_ref[peer, zl]

        @pl.when(slot >= 0)
        def _():
            sum_ref[slot] += in_ref[peer, 0].astype(F32)

    out_ref[0] = sum_ref[...].astype(out_ref.dtype)


def sum_parts(want, home, parts, blocks):
    peers, runs, rows, width = parts.shape
    return pl.pallas_call(
        gather_body,
        grid_spec=pltpu.PrefetchScalarGridSpec(
            num_scalar_prefetch=2,
            grid=(runs,),
            in_specs=[
                pl.BlockSpec((peers, 1, rows, width), lambda k, w, h: (0, lax.rem(h[0] + k, ZL), 0, 0)),
            ],
            out_specs=pl.BlockSpec((1, blocks, rows, width), lambda k, w, h: (k, 0, 0, 0)),
            scratch_shapes=[pltpu.VMEM((blocks, rows, width), F32)],
        ),
        out_shape=jax.ShapeDtypeStruct((runs, blocks, rows, width), BF16),
        compiler_params=pltpu.CompilerParams(dimension_semantics=("arbitrary",)),
        name="sum_parts",
    )(want, home, parts)


def on_device(queries, key_states, values, grad_out, picked_blocks):
    tokens, heads, width = queries.shape
    blocks = tokens // BLK
    group = lax.axis_index("y")
    home = lax.axis_index("zl").astype(jnp.int32)[None]
    own_keys = lax.dynamic_index_in_dim(key_states, group, 1, keepdims=False)
    own_values = lax.dynamic_index_in_dim(values, group, 1, keepdims=False)
    own = jnp.concatenate([own_keys, own_values], axis=1).reshape(blocks, BLK, 2 * width)
    picks = lax.dynamic_index_in_dim(picked_blocks, group, 1, keepdims=False)

    near = [None] * ZL
    near[0] = own
    ahead = behind = own
    for step in range(1, ZL // 2 + 1):
        ahead = shift_z(ahead, 1)
        near[ZL - step] = ahead
        if step < ZL // 2:
            behind = shift_z(behind, -1)
            near[step] = behind

    live = picks >= 0
    run = jnp.where(live, picks // blocks, -1)
    run_ids = jnp.arange(NX * ZL * NC, dtype=jnp.int32)
    match = run[:, 1:, None] == run_ids
    wanted = jnp.max(jnp.where(match, (picks % blocks)[:, 1:, None], -1), axis=(0, 1))
    wanted = wanted.reshape(NX, ZL, NC).transpose(0, 2, 1).reshape(NX * NC, ZL)
    asked = lax.all_to_all(wanted, XC, split_axis=0, concat_axis=0, tiled=True)

    sent = pick_blocks(asked, home, near)
    got = lax.all_to_all(sent, XC, split_axis=0, concat_axis=0, tiled=True)
    got = got.reshape(NX * NC * ZL, BLK, 2 * width)
    run_x, run_z, run_c = run // (ZL * NC), run // NC % ZL, run % NC
    slots = jnp.where(live, (run_x * NC + run_c) * ZL + run_z, -1)
    bias = jnp.where(live, 0.0, NEG).astype(F32)
    bias = jnp.broadcast_to(bias[:, :, None], (blocks, KSEL, BLK * heads))
    dq, own_grads, back = attend_grads(
        slots, queries.reshape(tokens * heads, width), grad_out.reshape(tokens * heads, width), own, bias, got
    )
    grad_queries = dq.reshape(tokens, heads, width)

    parts = lax.all_to_all(back.reshape(NX * NC, ZL, BLK, 2 * width), XC, split_axis=0, concat_axis=0, tiled=True)
    sums = sum_parts(asked, home, parts, blocks)

    ahead = sums[ZL // 2]
    behind = None
    for step in range(ZL // 2, 0, -1):
        ahead = shift_z(ahead, 1)
        if step > 1:
            ahead = (ahead.astype(F32) + sums[step - 1].astype(F32)).astype(BF16)
        if step < ZL // 2:
            behind = sums[ZL - step] if behind is None else (behind.astype(F32) + sums[ZL - step].astype(F32)).astype(BF16)
            behind = shift_z(behind, -1)
    total = own_grads + sums[0].astype(F32) + ahead.astype(F32) + behind.astype(F32)

    pieces = total.astype(BF16).reshape(NY * ZH, tokens // (NY * ZH), 2 * width)
    pieces = lax.all_to_all(pieces, HEAD, split_axis=0, concat_axis=0, tiled=True)
    summed = pieces.astype(F32).reshape(NY, ZH, tokens // (NY * ZH), 2 * width).sum(axis=1)
    summed = summed.transpose(1, 0, 2)
    return (grad_queries, summed[:, :, :width], summed[:, :, width:])


def solution(mesh):
    torus = Mesh(mesh.devices.reshape(NX, ZL, NC, NY, ZH), AXES)
    by_head = P(SEQ, HEAD, None)
    by_run = P(SEQ, None, None)
    by_all = P(AXES, None, None)
    return jax.shard_map(
        on_device,
        mesh=torus,
        in_specs=(by_head, by_run, by_run, by_head, by_run),
        out_specs=(by_head, by_all, by_all),
        check_vma=False,
    )
```

time: 702 us -> 217 us (0.31)
  the two profiles are of different devices: /device:TPU:244 before, /device:TPU:96 now
where the time goes in v1:
time: 217 us; the launch traced here: 216 us
  blocking collectives  82.5 us (38%)
  starting transfers between devices  59.1 us (27%)
  waiting for transfers between devices  48.2 us (22%)
  Pallas kernels  15.1 us (7%)
  local copies, waits for them, and re-layouts  6.14 us (3%)
  other arithmetic  4.22 us (2%)
    all_to_all x1, blocking collectives, on_device(): lax.all_to_all(pieces, HEAD, split_axis=0, concat_axis=0, tiled=True)  51.9 us
    ppermute x14, starting transfers between devices, shift_z(): return lax.ppermute(array, AXES, ring_pairs(step))  51.1 us
    all_to_all x1, blocking collectives, on_device(): lax.all_to_all(back.reshape(NX * NC, ZL, BLK, 2 * width), XC, split_axis=...  30.7 us
    all_to_all x1, waiting for transfers between devices, on_device(): got = lax.all_to_all(sent, XC, split_axis=0, concat_axis=0, tiled=True)  27.1 us
    ppermute x14, waiting for transfers between devices, shift_z(): return lax.ppermute(array, AXES, ring_pairs(step))  15.9 us
    pallas_call x1, Pallas kernels, attend_grads(): pl.pallas_call(attend_body, grid_spec=pltpu.PrefetchScalarGridSpec(num_sc...  7.76 us
    pallas_call x1, Pallas kernels, sum_parts(): pl.pallas_call(gather_body, grid_spec=pltpu.PrefetchScalarGridSpec(num_sc...  6.55 us
    all_to_all x1, waiting for transfers between devices, on_device(): asked = lax.all_to_all(wanted, XC, split_axis=0, concat_axis=0, tiled=True)  5.19 us
  transfers between devices with their start and end apart: 16, of which 11 were waited for; matrix products, arithmetic and copies ran while one was open for 1% of the time, Pallas kernels for 0%

profile of v1, /device:TPU:96, one launch (start us, length us, event | category | flops | bytes accessed | tf_op | source)
XLA Modules:
  0.0 216.2 jit_solution(14609972089887886051)
XLA Ops:
  0.7 1.3 constant_dynamic-slice_fusion
  2.0 5.0 %collective-permute-start.3 = (bf16[4,64,256]{2,1,0:T(8,128)(2,1)S(1)}, bf16[4,64,256]{2,1,0:T(8,128)(2,1)S(1)}, u32[]{:S(2)}, u32[]{:S(2)}) collective-permute-start(bf16[4,64,256]{2,1,0:T(8,128)(2,1)S(1)} %pad_maximum_fusion.refs_0_.own_ref), channel_id=1, source_target_pairs={{0,32},{4,36},{8,40},{12,44},{16,48},{20,52},{24,56},{28,60},{32,6... | collective-permute-start | bytes 393224 | tf_op jit(solution)/shard_map/ppermute | solution.py:41
  7.1 1.9 collective-permute-start
  9.0 0.8 collective-permute-done.3.refs_7_
  9.8 5.6 %collective-permute-start.4 = (bf16[4,64,256]{2,1,0:T(8,128)(2,1)S(1)}, bf16[4,64,256]{2,1,0:T(8,128)(2,1)S(1)}, u32[]{:S(2)}, u32[]{:S(2)}) collective-permute-start(bf16[4,64,256]{2,1,0:T(8,128)(2,1)S(1)} %collective-permute-done.3.refs_7_), channel_id=1, source_target_pairs={{0,32},{4,36},{8,40},{12,44},{16,48},{20,52},{24,56},{28,60},{32,6... | collective-permute-start | bytes 393224 | tf_op jit(solution)/shard_map/ppermute | solution.py:41
  15.4 1.9 collective-permute-start.1
  17.3 0.6 collective-permute-done.4.refs_6_
  17.9 5.6 %collective-permute-start.5 = (bf16[4,64,256]{2,1,0:T(8,128)(2,1)S(1)}, bf16[4,64,256]{2,1,0:T(8,128)(2,1)S(1)}, u32[]{:S(2)}, u32[]{:S(2)}) collective-permute-start(bf16[4,64,256]{2,1,0:T(8,128)(2,1)S(1)} %collective-permute-done.4.refs_6_), channel_id=1, source_target_pairs={{0,32},{4,36},{8,40},{12,44},{16,48},{20,52},{24,56},{28,60},{32,6... | collective-permute-start | bytes 393224 | tf_op jit(solution)/shard_map/ppermute | solution.py:41
  23.5 5.0 %collective-permute-start.2 = (bf16[4,64,256]{2,1,0:T(8,128)(2,1)S(1)}, bf16[4,64,256]{2,1,0:T(8,128)(2,1)S(1)}, u32[]{:S(2)}, u32[]{:S(2)}) collective-permute-start(bf16[4,64,256]{2,1,0:T(8,128)(2,1)S(1)} %collective-permute-done.1.refs_2_), channel_id=1, source_target_pairs={{0,227},{4,231},{8,235},{12,239},{16,243},{20,247},{24,251},{28,25... | collective-permute-start | bytes 393224 | tf_op jit(solution)/shard_map/ppermute | solution.py:41
  28.6 1.0 collective-permute-done.5.refs_5_
  29.5 2.0 collective-permute-start.6
  31.6 0.1 slice.36
  31.6 0.1 slice.37
  31.7 0.1 copy.21
  31.8 0.1 copy.20
  31.9 0.1 select_reduce_fusion
  32.0 0.1 reshape.64
  32.1 0.7 copy.22
  32.8 4.3 %all-to-all-start = ((s32[8,1,8]{2,1,0:T(1,128)}), s32[8,1,8]{2,1,0:T(1,128)S(1)}, u32[]{:S(2)}, u32[]{:S(2)}) async-start(s32[8,1,8]{2,1,0:T(1,128)} %bitcast.7), calls=%async_computation | async-start | bytes 8192 | tf_op jit(solution)/shard_map/all_to_all | solution.py:205
  37.1 5.2 %all-to-all-done = s32[8,1,8]{2,1,0:T(1,128)S(1)} async-done(((s32[8,1,8]{2,1,0:T(1,128)}), s32[8,1,8]{2,1,0:T(1,128)S(1)}, u32[]{:S(2)}, u32[]{:S(2)}) %all-to-all-start) | async-done | bytes 288 | tf_op jit(solution)/shard_map/all_to_all | solution.py:205
  42.3 0.8 pick_blocks.1
  43.1 1.3 copy-done.1
  44.4 3.7 %all-to-all-start.1 = ((bf16[8,8,64,256]{3,2,1,0:T(8,128)(2,1)}), bf16[8,8,64,256]{3,2,1,0:T(8,128)(2,1)S(1)}, u32[]{:S(2)}, u32[]{:S(2)}) async-start(bf16[8,8,64,256]{3,2,1,0:T(8,128)(2,1)} %copy-done.1), calls=%async_computation.1 | async-start | bytes 4194304 | tf_op jit(solution)/shard_map/all_to_all | solution.py:208
  48.2 27.1 %all-to-all-done.1 = bf16[8,8,64,256]{3,2,1,0:T(8,128)(2,1)S(1)} async-done(((bf16[8,8,64,256]{3,2,1,0:T(8,128)(2,1)}), bf16[8,8,64,256]{3,2,1,0:T(8,128)(2,1)S(1)}, u32[]{:S(2)}, u32[]{:S(2)}) %all-to-all-start.1) | async-done | bytes 2097184 | tf_op jit(solution)/shard_map/all_to_all | solution.py:208
  75.4 7.8 %attend_grads.1 = (f32[1024,128]{1,0:T(8,128)}, f32[4,64,256]{2,1,0:T(8,128)S(1)}, bf16[64,64,256]{2,1,0:T(8,128)(2,1)S(1)}) custom-call(s32[4,16]{1,0:T(4,128)S(1)} %get-tuple-element.15.slot_ref, bf16[1024,128]{1,0:T(8,128)(2,1)S(1)} %bitcast.55, bf16[1024,128]{1,0:T(8,128)(2,1)S(1)} %bitcast.56, bf16[4,64,256]{2,1,0:T(8,128)(2,1)S(1)} %pad_maximum_fusion.refs_0_.own_ref, ...), custom_call_target="tpu_custom_call" | custom-call | tf_op jit(solution)/shard_map/attend_grads/pallas_call | solution.py:101
  83.1 30.7 %all_to_all.26.in_ref = bf16[8,8,64,256]{3,2,1,0:T(8,128)(2,1)} all-to-all(bf16[8,8,64,256]{3,2,1,0:T(8,128)(2,1)S(1)} %bitcast.54), channel_id=1, replica_groups=mesh['x'=4,'zl'=8,'c'=2,'y'=4,'zh'=4] {'x','c'}, dimensions={0} | all-to-all | bytes 4194304 | tf_op jit(solution)/shard_map/all_to_all | solution.py:219
  113.8 6.6 %sum_parts.1 = bf16[8,4,64,256]{3,2,1,0:T(8,128)(2,1)} custom-call(s32[8,8]{1,0:T(8,128)} %bitcast.58, s32[1]{0:T(128)} %bitcast.9.home_ref, bf16[8,8,64,256]{3,2,1,0:T(8,128)(2,1)} %all_to_all.26.in_ref), custom_call_target="tpu_custom_call" | custom-call | tf_op jit(solution)/shard_map/sum_parts/pallas_call | solution.py:162
  120.3 1.0 slice_bitcast_fusion.6
  121.3 1.9 collective-permute-start.7
  123.3 6.5 %collective-permute-start.11 = (bf16[4,64,256]{2,1,0:T(8,128)(2,1)S(1)}, bf16[4,64,256]{2,1,0:T(8,128)(2,1)S(1)}, u32[]{:S(2)}, u32[]{:S(2)}) collective-permute-start(bf16[4,64,256]{2,1,0:T(8,128)(2,1)S(1)} %get-tuple-element.22), channel_id=1, source_target_pairs={{0,227},{4,231},{8,235},{12,239},{16,243},{20,247},{24,251},{28,25... | collective-permute-start | bytes 393224 | tf_op jit(solution)/shard_map/ppermute | solution.py:41
  129.8 1.2 collective-permute-done.7
  130.9 0.9 fusion.4
  131.9 1.9 collective-permute-start.8
  133.8 6.1 %collective-permute-done.8 = bf16[4,64,256]{2,1,0:T(8,128)(2,1)S(1)} collective-permute-done((bf16[4,64,256]{2,1,0:T(8,128)(2,1)S(1)}, bf16[4,64,256]{2,1,0:T(8,128)(2,1)S(1)}, u32[]{:S(2)}, u32[]{:S(2)}) %collective-permute-start.8) | collective-permute-done | bytes 131104 | tf_op jit(solution)/shard_map/ppermute | solution.py:41
  139.9 1.1 fusion.3
  141.0 1.9 collective-permute-start.9
  142.9 5.1 %collective-permute-start.12 = (bf16[4,64,256]{2,1,0:T(8,128)(2,1)S(1)}, bf16[4,64,256]{2,1,0:T(8,128)(2,1)S(1)}, u32[]{:S(2)}, u32[]{:S(2)}) collective-permute-start(bf16[4,64,256]{2,1,0:T(8,128)(2,1)S(1)} %get-tuple-element.20), channel_id=1, source_target_pairs={{0,227},{4,231},{8,235},{12,239},{16,243},{20,247},{24,251},{28,25... | collective-permute-start | bytes 393224 | tf_op jit(solution)/shard_map/ppermute | solution.py:41
  148.0 1.0 collective-permute-done.9
  149.0 2.0 collective-permute-done.12
  151.0 1.1 fusion.2
  152.1 1.9 collective-permute-start.10
  154.0 4.7 %collective-permute-start.13 = (bf16[4,64,256]{2,1,0:T(8,128)(2,1)S(1)}, bf16[4,64,256]{2,1,0:T(8,128)(2,1)S(1)}, u32[]{:S(2)}, u32[]{:S(2)}) collective-permute-start(bf16[4,64,256]{2,1,0:T(8,128)(2,1)S(1)} %get-tuple-element.18), channel_id=1, source_target_pairs={{0,227},{4,231},{8,235},{12,239},{16,243},{20,247},{24,251},{28,25... | collective-permute-start | bytes 393224 | tf_op jit(solution)/shard_map/ppermute | solution.py:41
  158.8 1.0 collective-permute-done.10
  159.8 2.3 %collective-permute-done.13 = bf16[4,64,256]{2,1,0:T(8,128)(2,1)S(1)} collective-permute-done((bf16[4,64,256]{2,1,0:T(8,128)(2,1)S(1)}, bf16[4,64,256]{2,1,0:T(8,128)(2,1)S(1)}, u32[]{:S(2)}, u32[]{:S(2)}) %collective-permute-start.13) | collective-permute-done | bytes 131104 | tf_op jit(solution)/shard_map/ppermute | solution.py:41
  162.1 1.0 fusion.7
  163.1 51.9 %all_to_all.27 = bf16[16,16,256]{2,1,0:T(8,128)(2,1)S(1)} all-to-all(bf16[16,16,256]{2,1,0:T(8,128)(2,1)S(1)} %bitcast.59), channel_id=1, replica_groups=mesh['x'=4,'zl'=8,'c'=2,'y'=4,'zh'=4] {'y','zh'}, dimensions={0} | all-to-all | bytes 262144 | tf_op jit(solution)/shard_map/all_to_all | solution.py:234
  215.0 0.6 copy.25
  215.6 0.6 copy.24
  (23 shorter events, 0.2 us)
Async XLA Ops:
  0.6 22.8 %copy-start = (s32[4,4,16]{2,1,0:T(4,128)S(1)}, s32[4,4,16]{2,1,0:T(4,128)}, u32[]{:S(2)}) copy-start(s32[4,4,16]{2,1,0:T(4,128)} %param.9) | copy-start | bytes 3076
  2.0 7.8 %collective-permute-start.3 = (bf16[4,64,256]{2,1,0:T(8,128)(2,1)S(1)}, bf16[4,64,256]{2,1,0:T(8,128)(2,1)S(1)}, u32[]{:S(2)}, u32[]{:S(2)}) collective-permute-start(bf16[4,64,256]{2,1,0:T(8,128)(2,1)S(1)} %pad_maximum_fusion.refs_0_.own_ref), channel_id=1, source_target_pairs={{0,32},{4,36},{8,40},{12,44},{16,48},{20,52},{24,56},{28,60},{32,6... | collective-permute-start | bytes 393224 | tf_op jit(solution)/shard_map/ppermute | solution.py:41
  7.1 8.3 %collective-permute-start = (bf16[4,64,256]{2,1,0:T(8,128)(2,1)S(1)}, bf16[4,64,256]{2,1,0:T(8,128)(2,1)S(1)}, u32[]{:S(2)}, u32[]{:S(2)}) collective-permute-start(bf16[4,64,256]{2,1,0:T(8,128)(2,1)S(1)} %pad_maximum_fusion.refs_0_.own_ref), channel_id=1, source_target_pairs={{0,227},{4,231},{8,235},{12,239},{16,243},{20,247},{24,251},{28,25... | collective-permute-start | bytes 393224 | tf_op jit(solution)/shard_map/ppermute | solution.py:41
  9.8 8.1 %collective-permute-start.4 = (bf16[4,64,256]{2,1,0:T(8,128)(2,1)S(1)}, bf16[4,64,256]{2,1,0:T(8,128)(2,1)S(1)}, u32[]{:S(2)}, u32[]{:S(2)}) collective-permute-start(bf16[4,64,256]{2,1,0:T(8,128)(2,1)S(1)} %collective-permute-done.3.refs_7_), channel_id=1, source_target_pairs={{0,32},{4,36},{8,40},{12,44},{16,48},{20,52},{24,56},{28,60},{32,6... | collective-permute-start | bytes 393224 | tf_op jit(solution)/shard_map/ppermute | solution.py:41
  15.4 8.1 %collective-permute-start.1 = (bf16[4,64,256]{2,1,0:T(8,128)(2,1)S(1)}, bf16[4,64,256]{2,1,0:T(8,128)(2,1)S(1)}, u32[]{:S(2)}, u32[]{:S(2)}) collective-permute-start(bf16[4,64,256]{2,1,0:T(8,128)(2,1)S(1)} %collective-permute-done.refs_1_), channel_id=1, source_target_pairs={{0,227},{4,231},{8,235},{12,239},{16,243},{20,247},{24,251},{28,25... | collective-permute-start | bytes 393224 | tf_op jit(solution)/shard_map/ppermute | solution.py:41
  17.9 11.6 %collective-permute-start.5 = (bf16[4,64,256]{2,1,0:T(8,128)(2,1)S(1)}, bf16[4,64,256]{2,1,0:T(8,128)(2,1)S(1)}, u32[]{:S(2)}, u32[]{:S(2)}) collective-permute-start(bf16[4,64,256]{2,1,0:T(8,128)(2,1)S(1)} %collective-permute-done.4.refs_6_), channel_id=1, source_target_pairs={{0,32},{4,36},{8,40},{12,44},{16,48},{20,52},{24,56},{28,60},{32,6... | collective-permute-start | bytes 393224 | tf_op jit(solution)/shard_map/ppermute | solution.py:41
  23.5 18.8 %collective-permute-start.2 = (bf16[4,64,256]{2,1,0:T(8,128)(2,1)S(1)}, bf16[4,64,256]{2,1,0:T(8,128)(2,1)S(1)}, u32[]{:S(2)}, u32[]{:S(2)}) collective-permute-start(bf16[4,64,256]{2,1,0:T(8,128)(2,1)S(1)} %collective-permute-done.1.refs_2_), channel_id=1, source_target_pairs={{0,227},{4,231},{8,235},{12,239},{16,243},{20,247},{24,251},{28,25... | collective-permute-start | bytes 393224 | tf_op jit(solution)/shard_map/ppermute | solution.py:41
  29.5 12.8 %collective-permute-start.6 = (bf16[4,64,256]{2,1,0:T(8,128)(2,1)S(1)}, bf16[4,64,256]{2,1,0:T(8,128)(2,1)S(1)}, u32[]{:S(2)}, u32[]{:S(2)}) collective-permute-start(bf16[4,64,256]{2,1,0:T(8,128)(2,1)S(1)} %collective-permute-done.5.refs_5_), channel_id=1, source_target_pairs={{0,32},{4,36},{8,40},{12,44},{16,48},{20,52},{24,56},{28,60},{32,6... | collective-permute-start | bytes 393224 | tf_op jit(solution)/shard_map/ppermute | solution.py:41
  32.8 9.5 %all-to-all-start = ((s32[8,1,8]{2,1,0:T(1,128)}), s32[8,1,8]{2,1,0:T(1,128)S(1)}, u32[]{:S(2)}, u32[]{:S(2)}) async-start(s32[8,1,8]{2,1,0:T(1,128)} %bitcast.7), calls=%async_computation | async-start | bytes 8192 | tf_op jit(solution)/shard_map/all_to_all | solution.py:205
  42.3 2.1 copy-start.4
  43.1 1.3 copy-start.1
  44.4 30.9 %copy-start.2 = (bf16[256,4,128]{2,1,0:T(4,128)(2,1)S(1)}, bf16[256,4,128]{2,1,0:T(4,128)(2,1)}, u32[]{:S(2)}) copy-start(bf16[256,4,128]{2,1,0:T(4,128)(2,1)} %param.5) | copy-start | bytes 786436
  44.4 30.9 %copy-start.3 = (bf16[256,4,128]{2,1,0:T(4,128)(2,1)S(1)}, bf16[256,4,128]{2,1,0:T(4,128)(2,1)}, u32[]{:S(2)}) copy-start(bf16[256,4,128]{2,1,0:T(4,128)(2,1)} %param.8) | copy-start | bytes 786436
  44.4 30.9 %all-to-all-start.1 = ((bf16[8,8,64,256]{3,2,1,0:T(8,128)(2,1)}), bf16[8,8,64,256]{3,2,1,0:T(8,128)(2,1)S(1)}, u32[]{:S(2)}, u32[]{:S(2)}) async-start(bf16[8,8,64,256]{3,2,1,0:T(8,128)(2,1)} %copy-done.1), calls=%async_computation.1 | async-start | bytes 4194304 | tf_op jit(solution)/shard_map/all_to_all | solution.py:208
  121.3 9.6 %collective-permute-start.7 = (bf16[4,64,256]{2,1,0:T(8,128)(2,1)S(1)}, bf16[4,64,256]{2,1,0:T(8,128)(2,1)S(1)}, u32[]{:S(2)}, u32[]{:S(2)}) collective-permute-start(bf16[4,64,256]{2,1,0:T(8,128)(2,1)S(1)} %get-tuple-element.21), channel_id=1, source_target_pairs={{0,32},{4,36},{8,40},{12,44},{16,48},{20,52},{24,56},{28,60},{32,6... | collective-permute-start | bytes 393224 | tf_op jit(solution)/shard_map/ppermute | solution.py:41
  123.3 10.6 %collective-permute-start.11 = (bf16[4,64,256]{2,1,0:T(8,128)(2,1)S(1)}, bf16[4,64,256]{2,1,0:T(8,128)(2,1)S(1)}, u32[]{:S(2)}, u32[]{:S(2)}) collective-permute-start(bf16[4,64,256]{2,1,0:T(8,128)(2,1)S(1)} %get-tuple-element.22), channel_id=1, source_target_pairs={{0,227},{4,231},{8,235},{12,239},{16,243},{20,247},{24,251},{28,25... | collective-permute-start | bytes 393224 | tf_op jit(solution)/shard_map/ppermute | solution.py:41
  131.9 8.1 %collective-permute-start.8 = (bf16[4,64,256]{2,1,0:T(8,128)(2,1)S(1)}, bf16[4,64,256]{2,1,0:T(8,128)(2,1)S(1)}, u32[]{:S(2)}, u32[]{:S(2)}) collective-permute-start(bf16[4,64,256]{2,1,0:T(8,128)(2,1)S(1)} %fusion.4), channel_id=1, source_target_pairs={{0,32},{4,36},{8,40},{12,44},{16,48},{20,52},{24,56},{28,60},{32,6... | collective-permute-start | bytes 393224 | tf_op jit(solution)/shard_map/ppermute | solution.py:41
  141.0 8.0 %collective-permute-start.9 = (bf16[4,64,256]{2,1,0:T(8,128)(2,1)S(1)}, bf16[4,64,256]{2,1,0:T(8,128)(2,1)S(1)}, u32[]{:S(2)}, u32[]{:S(2)}) collective-permute-start(bf16[4,64,256]{2,1,0:T(8,128)(2,1)S(1)} %get-tuple-element.19), channel_id=1, source_target_pairs={{0,32},{4,36},{8,40},{12,44},{16,48},{20,52},{24,56},{28,60},{32,6... | collective-permute-start | bytes 393224 | tf_op jit(solution)/shard_map/ppermute | solution.py:41
  142.9 8.1 %collective-permute-start.12 = (bf16[4,64,256]{2,1,0:T(8,128)(2,1)S(1)}, bf16[4,64,256]{2,1,0:T(8,128)(2,1)S(1)}, u32[]{:S(2)}, u32[]{:S(2)}) collective-permute-start(bf16[4,64,256]{2,1,0:T(8,128)(2,1)S(1)} %get-tuple-element.20), channel_id=1, source_target_pairs={{0,227},{4,231},{8,235},{12,239},{16,243},{20,247},{24,251},{28,25... | collective-permute-start | bytes 393224 | tf_op jit(solution)/shard_map/ppermute | solution.py:41
  152.1 7.7 %collective-permute-start.10 = (bf16[4,64,256]{2,1,0:T(8,128)(2,1)S(1)}, bf16[4,64,256]{2,1,0:T(8,128)(2,1)S(1)}, u32[]{:S(2)}, u32[]{:S(2)}) collective-permute-start(bf16[4,64,256]{2,1,0:T(8,128)(2,1)S(1)} %get-tuple-element.17), channel_id=1, source_target_pairs={{0,32},{4,36},{8,40},{12,44},{16,48},{20,52},{24,56},{28,60},{32,6... | collective-permute-start | bytes 393224 | tf_op jit(solution)/shard_map/ppermute | solution.py:41
  154.0 8.1 %collective-permute-start.13 = (bf16[4,64,256]{2,1,0:T(8,128)(2,1)S(1)}, bf16[4,64,256]{2,1,0:T(8,128)(2,1)S(1)}, u32[]{:S(2)}, u32[]{:S(2)}) collective-permute-start(bf16[4,64,256]{2,1,0:T(8,128)(2,1)S(1)} %get-tuple-element.18), channel_id=1, source_target_pairs={{0,227},{4,231},{8,235},{12,239},{16,243},{20,247},{24,251},{28,25... | collective-permute-start | bytes 393224 | tf_op jit(solution)/shard_map/ppermute | solution.py:41

commit v2 on v1

v2 whole, which is shorter than its diff:
```python
import functools

import jax
import jax.numpy as jnp
from jax import lax
from jax.experimental import pallas as pl
from jax.experimental.pallas import tpu as pltpu
from jax.sharding import Mesh
from jax.sharding import PartitionSpec as P

BLK = 64
KSEL = 16
NEG = -1e30

NX, ZL, NC, NY, ZH = 4, 8, 2, 4, 4
NZ = ZL * ZH
SEQ = ("x", "zl", "c")
HEAD = ("y", "zh")
XC = ("x", "c")
AXES = SEQ + HEAD
NEAR = ZL // 2
PARTS = 1
PER = NEAR // PARTS

F32 = jnp.float32
BF16 = jnp.bfloat16


def number(x, z, c, y):
    return (((x * ZL + z % ZL) * NC + c) * NY + y) * ZH + z % NZ // ZL


def send(array, move):
    pairs = []
    for x in range(NX):
        for z in range(NZ):
            for c in range(NC):
                for y in range(NY):
                    to = move(c)
                    if to is not None:
                        pairs.append((number(x, z, c, y), number(x, z + to[0], to[1], y)))
    return lax.ppermute(array, AXES, pairs)


def swap_cores(c):
    return (0, 1 - c)


def spread(c):
    return (1 if c == 0 else -1, c)


def spread_last(c):
    return (1, 0) if c == 0 else None


def collect(c):
    return (-1 if c == 0 else 1, c)


def collect_same(c):
    return (-1, 0) if c == 0 else None


def collect_cross(c):
    return (-1, 1) if c == 0 else (0, 0)


def attend_body(slot_ref, q_ref, g_ref, own_ref, bias_ref, *refs):
    got_refs = refs[:PARTS]
    dq_ref, down_ref = refs[PARTS : PARTS + 2]
    back_refs = refs[PARTS + 2 : 2 * PARTS + 2]
    k_ref, v_ref = refs[2 * PARTS + 2 :]
    held = got_refs[0].shape[0]
    b = pl.program_id(0)
    rows = q_ref.shape[0]
    width = q_ref.shape[1]
    heads = rows // BLK
    factor = width ** (-0.5)

    @pl.when(b == 0)
    def _():
        for back_ref in back_refs:
            back_ref[...] = jnp.zeros_like(back_ref)

    k_ref[0:BLK, :] = own_ref[0, :, :width]
    v_ref[0:BLK, :] = own_ref[0, :, width:]
    for j in range(1, KSEL):
        slot = jnp.maximum(slot_ref[b, j], 0)
        for part, got_ref in enumerate(got_refs):

            @pl.when(slot // held == part)
            def _():
                k_ref[j * BLK : (j + 1) * BLK, :] = got_ref[slot - part * held, :, :width]
                v_ref[j * BLK : (j + 1) * BLK, :] = got_ref[slot - part * held, :, width:]

    q = q_ref[...]
    g = g_ref[...]
    k = k_ref[...]
    v = v_ref[...]
    nt = (((1,), (1,)), ((), ()))
    scores = lax.dot_general(k, q, nt, preferred_element_type=F32) * factor
    key_row = lax.broadcasted_iota(jnp.int32, (BLK, rows), 0)
    token = lax.broadcasted_iota(jnp.int32, (BLK, rows), 1) // heads
    own = jnp.where(key_row <= token, scores[:BLK], NEG)
    far = scores[BLK:].reshape(KSEL - 1, BLK, rows) + bias_ref[0, 1:][:, None, :]
    scores = jnp.concatenate([own, far.reshape((KSEL - 1) * BLK, rows)], axis=0)
    weights = jnp.exp(scores - jnp.max(scores, axis=0, keepdims=True))
    attend = weights * (1.0 / jnp.sum(weights, axis=0, keepdims=True))
    grad_prob = lax.dot_general(v, g, nt, preferred_element_type=F32)
    row_dot = jnp.sum(attend * grad_prob, axis=0, keepdims=True)
    dscore = (attend * (grad_prob - row_dot)).astype(BF16)
    tn = (((0,), (0,)), ((), ()))
    nn = (((1,), (0,)), ((), ()))
    dq = lax.dot_general(k, dscore, tn, preferred_element_type=F32) * factor
    dq_ref[...] = dq.T
    dk = lax.dot_general(dscore, q, nn, preferred_element_type=F32) * factor
    dv = lax.dot_general(attend.astype(BF16), g, nn, preferred_element_type=F32)
    down_ref[0, :, :width] = dk[:BLK]
    down_ref[0, :, width:] = dv[:BLK]
    for j in range(1, KSEL):
        slot = slot_ref[b, j]

        for part, back_ref in enumerate(back_refs):

            @pl.when((slot >= part * held) & (slot < (part + 1) * held))
            def _():
                back_ref[slot - part * held, :, :width] = dk[j * BLK : (j + 1) * BLK].astype(BF16)
                back_ref[slot - part * held, :, width:] = dv[j * BLK : (j + 1) * BLK].astype(BF16)


def attend_grads(slots, q_rows, g_rows, own, bias, got):
    blocks = slots.shape[0]
    total, width = q_rows.shape
    rows = total // blocks
    row_spec = pl.BlockSpec((rows, width), lambda b, s: (b, 0))
    own_spec = pl.BlockSpec((1, BLK, 2 * width), lambda b, s: (b, 0, 0))
    whole = pl.BlockSpec(got[0].shape, lambda b, s: (0, 0, 0))
    return pl.pallas_call(
        attend_body,
        grid_spec=pltpu.PrefetchScalarGridSpec(
            num_scalar_prefetch=1,
            grid=(blocks,),
            in_specs=[row_spec, row_spec, own_spec, pl.BlockSpec((1, KSEL, rows), lambda b, s: (b, 0, 0))]
            + [whole] * PARTS,
            out_specs=[row_spec, own_spec] + [whole] * PARTS,
            scratch_shapes=[pltpu.VMEM((KSEL * BLK, width), BF16), pltpu.VMEM((KSEL * BLK, width), BF16)],
        ),
        out_shape=[
            jax.ShapeDtypeStruct((total, width), F32),
            jax.ShapeDtypeStruct((blocks, BLK, 2 * width), F32),
        ]
        + [jax.ShapeDtypeStruct(got[0].shape, BF16)] * PARTS,
        compiler_params=pltpu.CompilerParams(dimension_semantics=("arbitrary",), vmem_limit_bytes=48 * 2**20),
        name="attend_grads",
    )(slots, q_rows, g_rows, own, bias, *got)


def pick_body(part, want_ref, core_ref, *refs):
    out_ref = refs[-1]
    for core in range(NC):

        @pl.when(core_ref[0] == core)
        def _():
            for step in range(PER):
                near_ref = refs[step + 1 - core]
                for which in range(NC):
                    for peer in range(NX * NC):
                        slot = want_ref[peer, (part * PER + step) * NC + which]
                        out_ref[peer, step * NC + which] = near_ref[which, jnp.maximum(slot, 0)]


def pick_blocks(part, want, core, near):
    cores, blocks, rows, width = near[0].shape
    shape = (NX * NC, PER * NC, rows, width)
    spec = pl.BlockSpec(near[0].shape, lambda i, w, h: (0, 0, 0, 0))
    return pl.pallas_call(
        functools.partial(pick_body, part),
        grid_spec=pltpu.PrefetchScalarGridSpec(
            num_scalar_prefetch=2,
            grid=(1,),
            in_specs=[spec] * (PER + 1),
            out_specs=pl.BlockSpec(shape, lambda i, w, h: (0, 0, 0, 0)),
        ),
        out_shape=jax.ShapeDtypeStruct(shape, near[0].dtype),
        compiler_params=pltpu.CompilerParams(vmem_limit_bytes=32 * 2**20),
        name="pick_blocks",
    )(want, core, *near[part * PER : (part + 1) * PER + 1])


def sum_body(part, want_ref, in_ref, *refs):
    sum_ref = refs[-1]
    for step in range(PER):
        for which in range(NC):
            sum_ref[...] = jnp.zeros_like(sum_ref)
            for peer in range(NX * NC):
                slot = jnp.maximum(want_ref[peer, (part * PER + step) * NC + which], 0)
                sum_ref[slot] += in_ref[peer, step * NC + which].astype(F32)
            refs[step][which] = sum_ref[...].astype(BF16)


def sum_parts(part, want, parts, blocks):
    peers, runs, rows, width = parts.shape
    shape = (NC, blocks, rows, width)
    return pl.pallas_call(
        functools.partial(sum_body, part),
        grid_spec=pltpu.PrefetchScalarGridSpec(
            num_scalar_prefetch=1,
            grid=(1,),
            in_specs=[pl.BlockSpec(parts.shape, lambda k, w: (0, 0, 0, 0))],
            out_specs=[pl.BlockSpec(shape, lambda k, w: (0, 0, 0, 0))] * PER,
            scratch_shapes=[pltpu.VMEM((blocks, rows, width), F32)],
        ),
        out_shape=[jax.ShapeDtypeStruct(shape, BF16)] * PER,
        compiler_params=pltpu.CompilerParams(vmem_limit_bytes=32 * 2**20),
        name="sum_parts",
    )(want, parts)


def plus(a, b):
    return (a.astype(F32) + b.astype(F32)).astype(BF16)


def on_device(queries, key_states, values, grad_out, picked_blocks):
    tokens, heads, width = queries.shape
    blocks = tokens // BLK
    group = lax.axis_index("y")
    core = lax.axis_index("c").astype(jnp.int32)
    home = lax.axis_index("zl").astype(jnp.int32)
    own_keys = lax.dynamic_index_in_dim(key_states, group, 1, keepdims=False)
    own_values = lax.dynamic_index_in_dim(values, group, 1, keepdims=False)
    own = jnp.concatenate([own_keys, own_values], axis=1).reshape(1, blocks, BLK, 2 * width)
    picks = lax.dynamic_index_in_dim(picked_blocks, group, 1, keepdims=False)

    live = picks >= 0
    run = picks // blocks
    ahead = lax.rem(run // NC % ZL - home + ZL, ZL)
    holder = (ahead < NEAR).astype(jnp.int32)
    step = jnp.where(holder == 1, ahead, ZL - 1 - ahead)
    which = jnp.where(run % NC == holder, 0, 1)
    peer = run // (ZL * NC) * NC + holder
    place = jnp.where(live, peer * ZL + step * NC + which, -1)
    match = place[:, 1:, None] == jnp.arange(NX * ZL * NC, dtype=jnp.int32)
    wanted = jnp.max(jnp.where(match, (picks % blocks)[:, 1:, None], -1), axis=(0, 1))
    wanted = wanted.reshape(NX * NC, ZL)
    asked = lax.all_to_all(wanted, XC, split_axis=0, concat_axis=0, tiled=True)

    near = [jnp.concatenate([own, send(own, swap_cores)], axis=0)]
    for turn in range(NEAR):
        near.append(send(near[-1], spread if turn < NEAR - 1 else spread_last))

    got = []
    for part in range(PARTS):
        sent = pick_blocks(part, asked, core[None], near)
        arrived = lax.all_to_all(sent, XC, split_axis=0, concat_axis=0, tiled=True)
        got.append(arrived.reshape(NX * NC * PER * NC, BLK, 2 * width))
    slots = (step // PER * (NX * NC) + peer) * (PER * NC) + step % PER * NC + which
    slots = jnp.where(live, slots, -1)
    bias = jnp.where(live, 0.0, NEG).astype(F32)
    bias = jnp.broadcast_to(bias[:, :, None], (blocks, KSEL, BLK * heads))
    dq, own_grads, *back = attend_grads(
        slots, queries.reshape(tokens * heads, width), grad_out.reshape(tokens * heads, width), own[0], bias, got
    )
    grad_queries = dq.reshape(tokens, heads, width)

    sums = [None] * NEAR
    for part in reversed(range(PARTS)):
        parts = back[part].reshape(NX * NC, PER * NC, BLK, 2 * width)
        parts = lax.all_to_all(parts, XC, split_axis=0, concat_axis=0, tiled=True)
        sums[part * PER : (part + 1) * PER] = sum_parts(part, asked, parts, blocks)
    chain = sums[NEAR - 1]
    for turn in range(NEAR - 2, -1, -1):
        chain = plus(send(chain, collect), sums[turn])
    same = send(chain[0], collect_same)
    cross = send(chain[1], collect_cross)
    same = jnp.where(core == 0, same, chain[0])
    total = own_grads + same.astype(F32) + cross.astype(F32)

    pieces = total.astype(BF16).reshape(NY * ZH, tokens // (NY * ZH), 2 * width)
    pieces = lax.all_to_all(pieces, HEAD, split_axis=0, concat_axis=0, tiled=True)
    summed = pieces.astype(F32).reshape(NY, ZH, tokens // (NY * ZH), 2 * width).sum(axis=1)
    summed = summed.transpose(1, 0, 2)
    return (grad_queries, summed[:, :, :width], summed[:, :, width:])


def solution(mesh):
    torus = Mesh(mesh.devices.reshape(NX, ZL, NC, NY, ZH), AXES)
    by_head = P(SEQ, HEAD, None)
    by_run = P(SEQ, None, None)
    by_all = P(AXES, None, None)
    return jax.shard_map(
        on_device,
        mesh=torus,
        in_specs=(by_head, by_run, by_run, by_head, by_run),
        out_specs=(by_head, by_all, by_all),
        check_vma=False,
    )
```

time: 217 us -> 218 us (level)
  the two profiles are of different devices: /device:TPU:96 before, /device:TPU:32 now
where the time goes in v2:
time: 218 us
  waiting for transfers between devices  80.1 us (37%)
  blocking collectives  79.7 us (37%)
  starting transfers between devices  41 us (19%)
  Pallas kernels  10.6 us (5%)
  local copies, waits for them, and re-layouts  5.07 us (2%)
    all_to_all x1, blocking collectives, on_device(): lax.all_to_all(pieces, HEAD, split_axis=0, concat_axis=0, tiled=True)  49.8 us
    ppermute x10, waiting for transfers between devices, send(): return lax.ppermute(array, AXES, pairs)  47.8 us
    ppermute x10, starting transfers between devices, send(): return lax.ppermute(array, AXES, pairs)  33 us
    all_to_all x1, blocking collectives, on_device(): parts = lax.all_to_all(parts, XC, split_axis=0, concat_axis=0, tiled=True)  29.9 us
    all_to_all x1, waiting for transfers between devices, on_device(): arrived = lax.all_to_all(sent, XC, split_axis=0, concat_axis=0, tiled=True)  27.1 us
    pallas_call x1, Pallas kernels, attend_grads(): pl.pallas_call(attend_body, grid_spec=pltpu.PrefetchScalarGridSpec(num_sc...  8.49 us
    all_to_all x1, waiting for transfers between devices, on_device(): asked = lax.all_to_all(wanted, XC, split_axis=0, concat_axis=0, tiled=True)  5.19 us
  transfers between devices with their start and end apart: 12, of which 11 were waited for; matrix products, arithmetic and copies ran while one was open for 0% of the time, Pallas kernels for 0%

profile of v2, /device:TPU:32, one launch (start us, length us, event | category | flops | bytes accessed | tf_op | source)
XLA Modules:
  0.0 217.9 jit_solution(1543740199023343848)
XLA Ops:
  0.6 0.0 copy-start
  0.7 1.3 constant_dynamic-slice_fusion
  2.0 1.9 collective-permute-start
  4.0 1.3 collective-permute-done
  5.3 3.8 %collective-permute-start.1 = (bf16[2,4,64,256]{3,2,1,0:T(8,128)(2,1)S(1)}, bf16[2,4,64,256]{3,2,1,0:T(8,128)(2,1)S(1)}, u32[]{:S(2)}, u32[]{:S(2)}) collective-permute-start(bf16[2,4,64,256]{3,2,1,0:T(8,128)(2,1)S(1)} %pad_maximum_fusion.refs_0_), channel_id=1, source_target_pairs={{0,32},{4,36},{8,40},{12,44},{16,243},{20,247},{24,251},{28,255},{... | collective-permute-start | bytes 786440 | tf_op jit(solution)/shard_map/ppermute | solution.py:42
  9.1 15.2 %collective-permute-done.1.refs_1_ = bf16[2,4,64,256]{3,2,1,0:T(8,128)(2,1)S(1)} collective-permute-done((bf16[2,4,64,256]{3,2,1,0:T(8,128)(2,1)S(1)}, bf16[2,4,64,256]{3,2,1,0:T(8,128)(2,1)S(1)}, u32[]{:S(2)}, u32[]{:S(2)}) %collective-permute-start.1) | collective-permute-done | bytes 262176 | tf_op jit(solution)/shard_map/ppermute | solution.py:42
  24.3 1.9 collective-permute-start.2
  26.2 8.4 %collective-permute-done.2.refs_2_ = bf16[2,4,64,256]{3,2,1,0:T(8,128)(2,1)S(1)} collective-permute-done((bf16[2,4,64,256]{3,2,1,0:T(8,128)(2,1)S(1)}, bf16[2,4,64,256]{3,2,1,0:T(8,128)(2,1)S(1)}, u32[]{:S(2)}, u32[]{:S(2)}) %collective-permute-start.2) | collective-permute-done | bytes 262176 | tf_op jit(solution)/shard_map/ppermute | solution.py:42
  34.7 1.9 collective-permute-start.3
  36.6 0.0 copy-done
  36.7 0.1 slice.19
  36.7 7.4 %collective-permute-done.3.refs_3_ = bf16[2,4,64,256]{3,2,1,0:T(8,128)(2,1)S(1)} collective-permute-done((bf16[2,4,64,256]{3,2,1,0:T(8,128)(2,1)S(1)}, bf16[2,4,64,256]{3,2,1,0:T(8,128)(2,1)S(1)}, u32[]{:S(2)}, u32[]{:S(2)}) %collective-permute-start.3) | collective-permute-done | bytes 262176 | tf_op jit(solution)/shard_map/ppermute | solution.py:42
  44.1 1.9 collective-permute-start.4
  46.1 0.1 slice.20
  46.2 0.1 copy.18
  46.3 0.1 copy.17
  46.3 0.1 select_reduce_fusion
  46.5 0.7 all_to_all.16
  47.1 4.3 %all-to-all-start = ((s32[8,1,8]{2,1,0:T(1,128)}), s32[8,1,8]{2,1,0:T(1,128)S(1)}, u32[]{:S(2)}, u32[]{:S(2)}) async-start(s32[8,1,8]{2,1,0:T(1,128)} %bitcast.5), calls=%async_computation | async-start | bytes 8192 | tf_op jit(solution)/shard_map/all_to_all | solution.py:246
  51.4 5.2 %all-to-all-done = s32[8,1,8]{2,1,0:T(1,128)S(1)} async-done(((s32[8,1,8]{2,1,0:T(1,128)}), s32[8,1,8]{2,1,0:T(1,128)S(1)}, u32[]{:S(2)}, u32[]{:S(2)}) %all-to-all-start) | async-done | bytes 288 | tf_op jit(solution)/shard_map/all_to_all | solution.py:246
  56.6 0.0 collective-permute-done.4.refs_4_
  56.6 0.8 pick_blocks.1
  57.4 0.0 copy-start.1
  57.4 1.3 copy-done.1
  58.7 3.7 %all-to-all-start.1 = ((bf16[8,8,64,256]{3,2,1,0:T(8,128)(2,1)}), bf16[8,8,64,256]{3,2,1,0:T(8,128)(2,1)S(1)}, u32[]{:S(2)}, u32[]{:S(2)}) async-start(bf16[8,8,64,256]{3,2,1,0:T(8,128)(2,1)} %copy-done.1), calls=%async_computation.1 | async-start | bytes 4194304 | tf_op jit(solution)/shard_map/all_to_all | solution.py:255
  62.5 27.1 %all-to-all-done.1 = bf16[8,8,64,256]{3,2,1,0:T(8,128)(2,1)S(1)} async-done(((bf16[8,8,64,256]{3,2,1,0:T(8,128)(2,1)}), bf16[8,8,64,256]{3,2,1,0:T(8,128)(2,1)S(1)}, u32[]{:S(2)}, u32[]{:S(2)}) %all-to-all-start.1) | async-done | bytes 2097184 | tf_op jit(solution)/shard_map/all_to_all | solution.py:255
  89.6 0.1 broadcast_in_dim.41.bias_ref
  89.7 0.0 copy-done.2
  89.7 8.5 %attend_grads.1 = (f32[1024,128]{1,0:T(8,128)}, f32[4,64,256]{2,1,0:T(8,128)S(1)}, bf16[64,64,256]{2,1,0:T(8,128)(2,1)S(1)}) custom-call(s32[4,16]{1,0:T(4,128)S(1)} %get-tuple-element.31.slot_ref, bf16[1024,128]{1,0:T(8,128)(2,1)S(1)} %bitcast.26, bf16[1024,128]{1,0:T(8,128)(2,1)S(1)} %bitcast.27, bf16[4,64,256]{2,1,0:T(8,128)(2,1)S(1)} %pad_maximum_fusion.1.own_ref, ...), custom_call_target="tpu_custom_call" | custom-call | tf_op jit(solution)/shard_map/attend_grads/pallas_call | solution.py:139
  98.2 29.9 %all_to_all.26.in_ref = bf16[8,8,64,256]{3,2,1,0:T(8,128)(2,1)S(1)} all-to-all(bf16[8,8,64,256]{3,2,1,0:T(8,128)(2,1)S(1)} %bitcast.25), channel_id=1, replica_groups=mesh['x'=4,'zl'=8,'c'=2,'y'=4,'zh'=4] {'x','c'}, dimensions={0} | all-to-all | bytes 4194304 | tf_op jit(solution)/shard_map/all_to_all | solution.py:269
  128.1 1.3 sum_parts.1
  129.5 5.1 %collective-permute-start.5 = (bf16[2,4,64,256]{3,2,1,0:T(8,128)(2,1)S(1)}, bf16[2,4,64,256]{3,2,1,0:T(8,128)(2,1)S(1)}, u32[]{:S(2)}, u32[]{:S(2)}) collective-permute-start(bf16[2,4,64,256]{3,2,1,0:T(8,128)(2,1)S(1)} %get-tuple-element.13), channel_id=1, source_target_pairs={{0,227},{4,231},{8,235},{12,239},{16,48},{20,52},{24,56},{28,60},{... | collective-permute-start | bytes 786440 | tf_op jit(solution)/shard_map/ppermute | solution.py:42
  134.6 3.9 %collective-permute-done.5 = bf16[2,4,64,256]{3,2,1,0:T(8,128)(2,1)S(1)} collective-permute-done((bf16[2,4,64,256]{3,2,1,0:T(8,128)(2,1)S(1)}, bf16[2,4,64,256]{3,2,1,0:T(8,128)(2,1)S(1)}, u32[]{:S(2)}, u32[]{:S(2)}) %collective-permute-start.5) | collective-permute-done | bytes 262176 | tf_op jit(solution)/shard_map/ppermute | solution.py:42
  138.5 0.1 add_convert_fusion.2
  138.5 5.2 %collective-permute-start.6 = (bf16[2,4,64,256]{3,2,1,0:T(8,128)(2,1)S(1)}, bf16[2,4,64,256]{3,2,1,0:T(8,128)(2,1)S(1)}, u32[]{:S(2)}, u32[]{:S(2)}) collective-permute-start(bf16[2,4,64,256]{3,2,1,0:T(8,128)(2,1)S(1)} %add_convert_fusion.2), channel_id=1, source_target_pairs={{0,227},{4,231},{8,235},{12,239},{16,48},{20,52},{24,56},{28,60},{... | collective-permute-start | bytes 786440 | tf_op jit(solution)/shard_map/ppermute | solution.py:42
  143.7 3.9 %collective-permute-done.6 = bf16[2,4,64,256]{3,2,1,0:T(8,128)(2,1)S(1)} collective-permute-done((bf16[2,4,64,256]{3,2,1,0:T(8,128)(2,1)S(1)}, bf16[2,4,64,256]{3,2,1,0:T(8,128)(2,1)S(1)}, u32[]{:S(2)}, u32[]{:S(2)}) %collective-permute-start.6) | collective-permute-done | bytes 262176 | tf_op jit(solution)/shard_map/ppermute | solution.py:42
  147.6 0.1 add_convert_fusion.1
  147.7 5.6 %collective-permute-start.7 = (bf16[2,4,64,256]{3,2,1,0:T(8,128)(2,1)S(1)}, bf16[2,4,64,256]{3,2,1,0:T(8,128)(2,1)S(1)}, u32[]{:S(2)}, u32[]{:S(2)}) collective-permute-start(bf16[2,4,64,256]{3,2,1,0:T(8,128)(2,1)S(1)} %add_convert_fusion.1), channel_id=1, source_target_pairs={{0,227},{4,231},{8,235},{12,239},{16,48},{20,52},{24,56},{28,60},{... | collective-permute-start | bytes 786440 | tf_op jit(solution)/shard_map/ppermute | solution.py:42
  153.3 3.9 %collective-permute-done.7 = bf16[2,4,64,256]{3,2,1,0:T(8,128)(2,1)S(1)} collective-permute-done((bf16[2,4,64,256]{3,2,1,0:T(8,128)(2,1)S(1)}, bf16[2,4,64,256]{3,2,1,0:T(8,128)(2,1)S(1)}, u32[]{:S(2)}, u32[]{:S(2)}) %collective-permute-start.7) | collective-permute-done | bytes 262176 | tf_op jit(solution)/shard_map/ppermute | solution.py:42
  157.1 0.1 add_convert_fusion
  157.2 5.6 %collective-permute-start.8 = (bf16[4,64,256]{2,1,0:T(8,128)(2,1)S(1)}, bf16[4,64,256]{2,1,0:T(8,128)(2,1)S(1)}, u32[]{:S(2)}, u32[]{:S(2)}) collective-permute-start(bf16[4,64,256]{2,1,0:T(8,128)(2,1)S(1)} %get-tuple-element.26), channel_id=1, source_target_pairs={{0,227},{4,231},{8,235},{12,239},{32,0},{36,4},{40,8},{44,12},{64,... | collective-permute-start | bytes 393224 | tf_op jit(solution)/shard_map/ppermute | solution.py:42
  162.9 0.0 collective-permute-start.9
  162.9 2.5 %collective-permute-done.8 = bf16[4,64,256]{2,1,0:T(8,128)(2,1)S(1)} collective-permute-done((bf16[4,64,256]{2,1,0:T(8,128)(2,1)S(1)}, bf16[4,64,256]{2,1,0:T(8,128)(2,1)S(1)}, u32[]{:S(2)}, u32[]{:S(2)}) %collective-permute-start.8) | collective-permute-done | bytes 131104 | tf_op jit(solution)/shard_map/ppermute | solution.py:42
  165.4 1.4 collective-permute-done.9
  166.7 0.1 add_convert_fusion.3
  166.8 49.8 %all_to_all.27 = bf16[16,16,256]{2,1,0:T(8,128)(2,1)S(1)} all-to-all(bf16[16,16,256]{2,1,0:T(8,128)(2,1)S(1)} %bitcast.36), channel_id=1, replica_groups=mesh['x'=4,'zl'=8,'c'=2,'y'=4,'zh'=4] {'y','zh'}, dimensions={0} | all-to-all | bytes 262144 | tf_op jit(solution)/shard_map/all_to_all | solution.py:280
  216.6 0.6 copy.21
  217.2 0.6 copy.20
  (15 shorter events, 0.2 us)
Async XLA Ops:
  0.6 36.0 %copy-start = (s32[4,4,16]{2,1,0:T(4,128)S(1)}, s32[4,4,16]{2,1,0:T(4,128)}, u32[]{:S(2)}) copy-start(s32[4,4,16]{2,1,0:T(4,128)} %param.9) | copy-start | bytes 3076
  2.0 3.2 %collective-permute-start = (bf16[1,4,64,256]{3,2,1,0:T(8,128)(2,1)S(1)}, bf16[1,4,64,256]{3,2,1,0:T(8,128)(2,1)S(1)}, u32[]{:S(2)}, u32[]{:S(2)}) collective-permute-start(bf16[1,4,64,256]{3,2,1,0:T(8,128)(2,1)S(1)} %pad_maximum_fusion.2), channel_id=1, source_target_pairs={{0,16},{4,20},{8,24},{12,28},{16,0},{20,4},{24,8},{28,12},{32,48},... | collective-permute-start | bytes 393224 | tf_op jit(solution)/shard_map/ppermute | solution.py:42
  5.3 19.0 %collective-permute-start.1 = (bf16[2,4,64,256]{3,2,1,0:T(8,128)(2,1)S(1)}, bf16[2,4,64,256]{3,2,1,0:T(8,128)(2,1)S(1)}, u32[]{:S(2)}, u32[]{:S(2)}) collective-permute-start(bf16[2,4,64,256]{3,2,1,0:T(8,128)(2,1)S(1)} %pad_maximum_fusion.refs_0_), channel_id=1, source_target_pairs={{0,32},{4,36},{8,40},{12,44},{16,243},{20,247},{24,251},{28,255},{... | collective-permute-start | bytes 786440 | tf_op jit(solution)/shard_map/ppermute | solution.py:42
  24.3 10.4 %collective-permute-start.2 = (bf16[2,4,64,256]{3,2,1,0:T(8,128)(2,1)S(1)}, bf16[2,4,64,256]{3,2,1,0:T(8,128)(2,1)S(1)}, u32[]{:S(2)}, u32[]{:S(2)}) collective-permute-start(bf16[2,4,64,256]{3,2,1,0:T(8,128)(2,1)S(1)} %collective-permute-done.1.refs_1_), channel_id=1, source_target_pairs={{0,32},{4,36},{8,40},{12,44},{16,243},{20,247},{24,251},{28,255},{... | collective-permute-start | bytes 786440 | tf_op jit(solution)/shard_map/ppermute | solution.py:42
  34.7 9.5 %collective-permute-start.3 = (bf16[2,4,64,256]{3,2,1,0:T(8,128)(2,1)S(1)}, bf16[2,4,64,256]{3,2,1,0:T(8,128)(2,1)S(1)}, u32[]{:S(2)}, u32[]{:S(2)}) collective-permute-start(bf16[2,4,64,256]{3,2,1,0:T(8,128)(2,1)S(1)} %collective-permute-done.2.refs_2_), channel_id=1, source_target_pairs={{0,32},{4,36},{8,40},{12,44},{16,243},{20,247},{24,251},{28,255},{... | collective-permute-start | bytes 786440 | tf_op jit(solution)/shard_map/ppermute | solution.py:42
  44.1 12.5 %collective-permute-start.4 = (bf16[2,4,64,256]{3,2,1,0:T(8,128)(2,1)S(1)}, bf16[2,4,64,256]{3,2,1,0:T(8,128)(2,1)S(1)}, u32[]{:S(2)}, u32[]{:S(2)}) collective-permute-start(bf16[2,4,64,256]{3,2,1,0:T(8,128)(2,1)S(1)} %collective-permute-done.3.refs_3_), channel_id=1, source_target_pairs={{0,32},{4,36},{8,40},{12,44},{32,64},{36,68},{40,72},{44,76},{64,9... | collective-permute-start | bytes 786440 | tf_op jit(solution)/shard_map/ppermute | solution.py:42
  47.1 9.5 %all-to-all-start = ((s32[8,1,8]{2,1,0:T(1,128)}), s32[8,1,8]{2,1,0:T(1,128)S(1)}, u32[]{:S(2)}, u32[]{:S(2)}) async-start(s32[8,1,8]{2,1,0:T(1,128)} %bitcast.5), calls=%async_computation | async-start | bytes 8192 | tf_op jit(solution)/shard_map/all_to_all | solution.py:246
  57.4 1.3 copy-start.1
  58.7 30.9 %copy-start.2 = (bf16[256,4,128]{2,1,0:T(4,128)(2,1)S(1)}, bf16[256,4,128]{2,1,0:T(4,128)(2,1)}, u32[]{:S(2)}) copy-start(bf16[256,4,128]{2,1,0:T(4,128)(2,1)} %param.5) | copy-start | bytes 786436
  58.7 30.9 %copy-start.3 = (bf16[256,4,128]{2,1,0:T(4,128)(2,1)S(1)}, bf16[256,4,128]{2,1,0:T(4,128)(2,1)}, u32[]{:S(2)}) copy-start(bf16[256,4,128]{2,1,0:T(4,128)(2,1)} %param.8) | copy-start | bytes 786436
  58.7 30.9 %all-to-all-start.1 = ((bf16[8,8,64,256]{3,2,1,0:T(8,128)(2,1)}), bf16[8,8,64,256]{3,2,1,0:T(8,128)(2,1)S(1)}, u32[]{:S(2)}, u32[]{:S(2)}) async-start(bf16[8,8,64,256]{3,2,1,0:T(8,128)(2,1)} %copy-done.1), calls=%async_computation.1 | async-start | bytes 4194304 | tf_op jit(solution)/shard_map/all_to_all | solution.py:255
  129.5 9.0 %collective-permute-start.5 = (bf16[2,4,64,256]{3,2,1,0:T(8,128)(2,1)S(1)}, bf16[2,4,64,256]{3,2,1,0:T(8,128)(2,1)S(1)}, u32[]{:S(2)}, u32[]{:S(2)}) collective-permute-start(bf16[2,4,64,256]{3,2,1,0:T(8,128)(2,1)S(1)} %get-tuple-element.13), channel_id=1, source_target_pairs={{0,227},{4,231},{8,235},{12,239},{16,48},{20,52},{24,56},{28,60},{... | collective-permute-start | bytes 786440 | tf_op jit(solution)/shard_map/ppermute | solution.py:42
  138.5 9.1 %collective-permute-start.6 = (bf16[2,4,64,256]{3,2,1,0:T(8,128)(2,1)S(1)}, bf16[2,4,64,256]{3,2,1,0:T(8,128)(2,1)S(1)}, u32[]{:S(2)}, u32[]{:S(2)}) collective-permute-start(bf16[2,4,64,256]{3,2,1,0:T(8,128)(2,1)S(1)} %add_convert_fusion.2), channel_id=1, source_target_pairs={{0,227},{4,231},{8,235},{12,239},{16,48},{20,52},{24,56},{28,60},{... | collective-permute-start | bytes 786440 | tf_op jit(solution)/shard_map/ppermute | solution.py:42
  147.7 9.5 %collective-permute-start.7 = (bf16[2,4,64,256]{3,2,1,0:T(8,128)(2,1)S(1)}, bf16[2,4,64,256]{3,2,1,0:T(8,128)(2,1)S(1)}, u32[]{:S(2)}, u32[]{:S(2)}) collective-permute-start(bf16[2,4,64,256]{3,2,1,0:T(8,128)(2,1)S(1)} %add_convert_fusion.1), channel_id=1, source_target_pairs={{0,227},{4,231},{8,235},{12,239},{16,48},{20,52},{24,56},{28,60},{... | collective-permute-start | bytes 786440 | tf_op jit(solution)/shard_map/ppermute | solution.py:42
  157.2 8.1 %collective-permute-start.8 = (bf16[4,64,256]{2,1,0:T(8,128)(2,1)S(1)}, bf16[4,64,256]{2,1,0:T(8,128)(2,1)S(1)}, u32[]{:S(2)}, u32[]{:S(2)}) collective-permute-start(bf16[4,64,256]{2,1,0:T(8,128)(2,1)S(1)} %get-tuple-element.26), channel_id=1, source_target_pairs={{0,227},{4,231},{8,235},{12,239},{32,0},{36,4},{40,8},{44,12},{64,... | collective-permute-start | bytes 393224 | tf_op jit(solution)/shard_map/ppermute | solution.py:42
  162.9 3.9 %collective-permute-start.9 = (bf16[4,64,256]{2,1,0:T(8,128)(2,1)S(1)}, bf16[4,64,256]{2,1,0:T(8,128)(2,1)S(1)}, u32[]{:S(2)}, u32[]{:S(2)}) collective-permute-start(bf16[4,64,256]{2,1,0:T(8,128)(2,1)S(1)} %get-tuple-element.27), channel_id=1, source_target_pairs={{0,243},{4,247},{8,251},{12,255},{16,0},{20,4},{24,8},{28,12},{32,... | collective-permute-start | bytes 393224 | tf_op jit(solution)/shard_map/ppermute | solution.py:42

commit v3 on v2

--- a/solution.py
+++ b/solution.py
@@ -19,7 +19,7 @@
 XC = ("x", "c")
 AXES = SEQ + HEAD
 NEAR = ZL // 2
-PARTS = 1
+PARTS = 2
 PER = NEAR // PARTS
 
 F32 = jnp.float32

time: 218 us -> 204 us (0.936)
  the two profiles are of different devices: /device:TPU:32 before, /device:TPU:34 now
where the time goes in v3:
time: 204 us; the launch traced here: 203 us
  blocking collectives  67.4 us (33%)
  starting transfers between devices  62.4 us (31%)
  waiting for transfers between devices  53.5 us (26%)
  Pallas kernels  14.9 us (7%)
  local copies, waits for them, and re-layouts  3.73 us (2%)
    all_to_all x1, blocking collectives, on_device(): lax.all_to_all(pieces, HEAD, split_axis=0, concat_axis=0, tiled=True)  48.9 us
    ppermute x10, waiting for transfers between devices, send(): return lax.ppermute(array, AXES, pairs)  35.2 us
    ppermute x10, starting transfers between devices, send(): return lax.ppermute(array, AXES, pairs)  31.7 us
    all_to_all x1, blocking collectives, on_device(): parts = lax.all_to_all(parts, XC, split_axis=0, concat_axis=0, tiled=True)  18.5 us
    all_to_all x1, starting transfers between devices, on_device(): asked = lax.all_to_all(wanted, XC, split_axis=0, concat_axis=0, tiled=True)  15.9 us
    all_to_all x2, waiting for transfers between devices, on_device(): arrived = lax.all_to_all(sent, XC, split_axis=0, concat_axis=0, tiled=True)  14.5 us
    all_to_all x2, starting transfers between devices, on_device(): arrived = lax.all_to_all(sent, XC, split_axis=0, concat_axis=0, tiled=True)  9.87 us
    pallas_call x1, Pallas kernels, attend_grads(): pl.pallas_call(attend_body, grid_spec=pltpu.PrefetchScalarGridSpec(num_sc...  9.63 us
  transfers between devices with their start and end apart: 14, of which 12 were waited for; matrix products, arithmetic and copies ran while one was open for 0% of the time, Pallas kernels for 2%

profile of v3, /device:TPU:34, one launch (start us, length us, event | category | flops | bytes accessed | tf_op | source)
XLA Modules:
  0.0 203.4 jit_solution(11810701410827531408)
XLA Ops:
  0.6 0.0 copy-start
  0.7 1.3 constant_dynamic-slice_fusion
  2.0 1.9 collective-permute-start
  4.0 1.3 collective-permute-done
  5.3 3.8 %collective-permute-start.1 = (bf16[2,4,64,256]{3,2,1,0:T(8,128)(2,1)S(1)}, bf16[2,4,64,256]{3,2,1,0:T(8,128)(2,1)S(1)}, u32[]{:S(2)}, u32[]{:S(2)}) collective-permute-start(bf16[2,4,64,256]{3,2,1,0:T(8,128)(2,1)S(1)} %pad_maximum_fusion.refs_0_), channel_id=1, source_target_pairs={{0,32},{4,36},{8,40},{12,44},{16,243},{20,247},{24,251},{28,255},{... | collective-permute-start | bytes 786440 | tf_op jit(solution)/shard_map/ppermute | solution.py:42
  9.2 0.1 slice.19
  9.3 4.3 %collective-permute-done.1.refs_1_ = bf16[2,4,64,256]{3,2,1,0:T(8,128)(2,1)S(1)} collective-permute-done((bf16[2,4,64,256]{3,2,1,0:T(8,128)(2,1)S(1)}, bf16[2,4,64,256]{3,2,1,0:T(8,128)(2,1)S(1)}, u32[]{:S(2)}, u32[]{:S(2)}) %collective-permute-start.1) | collective-permute-done | bytes 262176 | tf_op jit(solution)/shard_map/ppermute | solution.py:42
  13.6 3.8 %collective-permute-start.2 = (bf16[2,4,64,256]{3,2,1,0:T(8,128)(2,1)S(1)}, bf16[2,4,64,256]{3,2,1,0:T(8,128)(2,1)S(1)}, u32[]{:S(2)}, u32[]{:S(2)}) collective-permute-start(bf16[2,4,64,256]{3,2,1,0:T(8,128)(2,1)S(1)} %collective-permute-done.1.refs_1_), channel_id=1, source_target_pairs={{0,32},{4,36},{8,40},{12,44},{16,243},{20,247},{24,251},{28,255},{... | collective-permute-start | bytes 786440 | tf_op jit(solution)/shard_map/ppermute | solution.py:42
  17.4 0.1 slice.20
  17.5 0.1 copy.18
  17.6 0.1 copy.17
  17.7 0.1 select_reduce_fusion
  17.8 0.7 all_to_all.22
  18.5 15.9 %all-to-all-start = ((s32[8,1,8]{2,1,0:T(1,128)}), s32[8,1,8]{2,1,0:T(1,128)S(1)}, u32[]{:S(2)}, u32[]{:S(2)}) async-start(s32[8,1,8]{2,1,0:T(1,128)} %bitcast.5), calls=%async_computation | async-start | bytes 8192 | tf_op jit(solution)/shard_map/all_to_all | solution.py:246
  34.4 3.7 %all-to-all-done = s32[8,1,8]{2,1,0:T(1,128)S(1)} async-done(((s32[8,1,8]{2,1,0:T(1,128)}), s32[8,1,8]{2,1,0:T(1,128)S(1)}, u32[]{:S(2)}, u32[]{:S(2)}) %all-to-all-start) | async-done | bytes 288 | tf_op jit(solution)/shard_map/all_to_all | solution.py:246
  38.1 1.7 pick_blocks.2
  39.8 4.9 %all-to-all-start.1 = ((bf16[8,4,64,256]{3,2,1,0:T(8,128)(2,1)}), bf16[8,4,64,256]{3,2,1,0:T(8,128)(2,1)S(1)}, u32[]{:S(2)}, u32[]{:S(2)}) async-start(bf16[8,4,64,256]{3,2,1,0:T(8,128)(2,1)} %pick_blocks.2), calls=%async_computation.1 | async-start | bytes 2097152 | tf_op jit(solution)/shard_map/all_to_all | solution.py:255
  44.7 1.9 collective-permute-start.3
  46.7 7.7 %collective-permute-done.3.refs_1_ = bf16[2,4,64,256]{3,2,1,0:T(8,128)(2,1)S(1)} collective-permute-done((bf16[2,4,64,256]{3,2,1,0:T(8,128)(2,1)S(1)}, bf16[2,4,64,256]{3,2,1,0:T(8,128)(2,1)S(1)}, u32[]{:S(2)}, u32[]{:S(2)}) %collective-permute-start.3) | collective-permute-done | bytes 262176 | tf_op jit(solution)/shard_map/ppermute | solution.py:42
  54.4 1.9 collective-permute-start.4
  56.3 7.5 %collective-permute-done.4.refs_2_ = bf16[2,4,64,256]{3,2,1,0:T(8,128)(2,1)S(1)} collective-permute-done((bf16[2,4,64,256]{3,2,1,0:T(8,128)(2,1)S(1)}, bf16[2,4,64,256]{3,2,1,0:T(8,128)(2,1)S(1)}, u32[]{:S(2)}, u32[]{:S(2)}) %collective-permute-start.4) | collective-permute-done | bytes 262176 | tf_op jit(solution)/shard_map/ppermute | solution.py:42
  63.8 1.6 pick_blocks.3
  65.5 4.9 %all-to-all-start.2 = ((bf16[8,4,64,256]{3,2,1,0:T(8,128)(2,1)}), bf16[8,4,64,256]{3,2,1,0:T(8,128)(2,1)S(1)}, u32[]{:S(2)}, u32[]{:S(2)}) async-start(bf16[8,4,64,256]{3,2,1,0:T(8,128)(2,1)} %pick_blocks.3), calls=%async_computation.2 | async-start | bytes 2097152 | tf_op jit(solution)/shard_map/all_to_all | solution.py:255
  70.5 14.5 %all-to-all-done.2 = bf16[8,4,64,256]{3,2,1,0:T(8,128)(2,1)S(1)} async-done(((bf16[8,4,64,256]{3,2,1,0:T(8,128)(2,1)}), bf16[8,4,64,256]{3,2,1,0:T(8,128)(2,1)S(1)}, u32[]{:S(2)}, u32[]{:S(2)}) %all-to-all-start.2) | async-done | bytes 1048608 | tf_op jit(solution)/shard_map/all_to_all | solution.py:255
  85.0 0.1 broadcast_in_dim.42.bias_ref
  85.0 9.6 %attend_grads.1 = (f32[1024,128]{1,0:T(8,128)}, f32[4,64,256]{2,1,0:T(8,128)S(1)}, bf16[32,64,256]{2,1,0:T(8,128)(2,1)}, bf16[32,64,256]{2,1,0:T(8,128)(2,1)S(1)}) custom-call(s32[4,16]{1,0:T(4,128)S(1)} %get-tuple-element.33.slot_ref, bf16[1024,128]{1,0:T(8,128)(2,1)S(1)} %bitcast.29, bf16[1024,128]{1,0:T(8,128)(2,1)S(1)} %bitcast.30, ...), custom_call_target="tpu_custom_call" | custom-call | tf_op jit(solution)/shard_map/attend_grads/pallas_call | solution.py:139
  94.7 18.5 %all_to_all.36.in_ref = bf16[8,4,64,256]{3,2,1,0:T(8,128)(2,1)S(1)} all-to-all(bf16[8,4,64,256]{3,2,1,0:T(8,128)(2,1)S(1)} %bitcast.28), channel_id=1, replica_groups=mesh['x'=4,'zl'=8,'c'=2,'y'=4,'zh'=4] {'x','c'}, dimensions={0} | all-to-all | bytes 2097152 | tf_op jit(solution)/shard_map/all_to_all | solution.py:269
  113.1 4.9 %all-to-all-start.4 = ((bf16[8,4,64,256]{3,2,1,0:T(8,128)(2,1)}), bf16[8,4,64,256]{3,2,1,0:T(8,128)(2,1)S(1)}, u32[]{:S(2)}, u32[]{:S(2)}) async-start(bf16[8,4,64,256]{3,2,1,0:T(8,128)(2,1)} %bitcast.14), calls=%async_computation.4 | async-start | bytes 2097152 | tf_op jit(solution)/shard_map/all_to_all | solution.py:269
  118.1 1.0 sum_parts.2
  119.0 5.1 %collective-permute-start.5 = (bf16[2,4,64,256]{3,2,1,0:T(8,128)(2,1)S(1)}, bf16[2,4,64,256]{3,2,1,0:T(8,128)(2,1)S(1)}, u32[]{:S(2)}, u32[]{:S(2)}) collective-permute-start(bf16[2,4,64,256]{3,2,1,0:T(8,128)(2,1)S(1)} %get-tuple-element.14), channel_id=1, source_target_pairs={{0,227},{4,231},{8,235},{12,239},{16,48},{20,52},{24,56},{28,60},{... | collective-permute-start | bytes 786440 | tf_op jit(solution)/shard_map/ppermute | solution.py:42
  124.2 3.9 %collective-permute-done.5 = bf16[2,4,64,256]{3,2,1,0:T(8,128)(2,1)S(1)} collective-permute-done((bf16[2,4,64,256]{3,2,1,0:T(8,128)(2,1)S(1)}, bf16[2,4,64,256]{3,2,1,0:T(8,128)(2,1)S(1)}, u32[]{:S(2)}, u32[]{:S(2)}) %collective-permute-start.5) | collective-permute-done | bytes 262176 | tf_op jit(solution)/shard_map/ppermute | solution.py:42
  128.0 0.1 add_convert_fusion.2
  128.1 4.4 %collective-permute-start.6 = (bf16[2,4,64,256]{3,2,1,0:T(8,128)(2,1)S(1)}, bf16[2,4,64,256]{3,2,1,0:T(8,128)(2,1)S(1)}, u32[]{:S(2)}, u32[]{:S(2)}) collective-permute-start(bf16[2,4,64,256]{3,2,1,0:T(8,128)(2,1)S(1)} %add_convert_fusion.2), channel_id=1, source_target_pairs={{0,227},{4,231},{8,235},{12,239},{16,48},{20,52},{24,56},{28,60},{... | collective-permute-start | bytes 786440 | tf_op jit(solution)/shard_map/ppermute | solution.py:42
  132.5 0.1 all-to-all-done.4.in_ref
  132.6 1.0 sum_parts.3
  133.6 2.8 %collective-permute-done.6 = bf16[2,4,64,256]{3,2,1,0:T(8,128)(2,1)S(1)} collective-permute-done((bf16[2,4,64,256]{3,2,1,0:T(8,128)(2,1)S(1)}, bf16[2,4,64,256]{3,2,1,0:T(8,128)(2,1)S(1)}, u32[]{:S(2)}, u32[]{:S(2)}) %collective-permute-start.6) | collective-permute-done | bytes 262176 | tf_op jit(solution)/shard_map/ppermute | solution.py:42
  136.4 0.1 add_convert_fusion.1
  136.4 4.4 %collective-permute-start.7 = (bf16[2,4,64,256]{3,2,1,0:T(8,128)(2,1)S(1)}, bf16[2,4,64,256]{3,2,1,0:T(8,128)(2,1)S(1)}, u32[]{:S(2)}, u32[]{:S(2)}) collective-permute-start(bf16[2,4,64,256]{3,2,1,0:T(8,128)(2,1)S(1)} %add_convert_fusion.1), channel_id=1, source_target_pairs={{0,227},{4,231},{8,235},{12,239},{16,48},{20,52},{24,56},{28,60},{... | collective-permute-start | bytes 786440 | tf_op jit(solution)/shard_map/ppermute | solution.py:42
  140.8 3.9 %collective-permute-done.7 = bf16[2,4,64,256]{3,2,1,0:T(8,128)(2,1)S(1)} collective-permute-done((bf16[2,4,64,256]{3,2,1,0:T(8,128)(2,1)S(1)}, bf16[2,4,64,256]{3,2,1,0:T(8,128)(2,1)S(1)}, u32[]{:S(2)}, u32[]{:S(2)}) %collective-permute-start.7) | collective-permute-done | bytes 262176 | tf_op jit(solution)/shard_map/ppermute | solution.py:42
  144.7 0.1 add_convert_fusion
  144.8 4.4 %collective-permute-start.8 = (bf16[4,64,256]{2,1,0:T(8,128)(2,1)S(1)}, bf16[4,64,256]{2,1,0:T(8,128)(2,1)S(1)}, u32[]{:S(2)}, u32[]{:S(2)}) collective-permute-start(bf16[4,64,256]{2,1,0:T(8,128)(2,1)S(1)} %get-tuple-element.28), channel_id=1, source_target_pairs={{0,227},{4,231},{8,235},{12,239},{32,0},{36,4},{40,8},{44,12},{64,... | collective-permute-start | bytes 393224 | tf_op jit(solution)/shard_map/ppermute | solution.py:42
  149.2 0.0 collective-permute-start.9
  149.2 2.5 %collective-permute-done.8 = bf16[4,64,256]{2,1,0:T(8,128)(2,1)S(1)} collective-permute-done((bf16[4,64,256]{2,1,0:T(8,128)(2,1)S(1)}, bf16[4,64,256]{2,1,0:T(8,128)(2,1)S(1)}, u32[]{:S(2)}, u32[]{:S(2)}) %collective-permute-start.8) | collective-permute-done | bytes 131104 | tf_op jit(solution)/shard_map/ppermute | solution.py:42
  151.7 1.4 collective-permute-done.9
  153.1 0.1 add_convert_fusion.3
  153.1 48.9 %all_to_all.37 = bf16[16,16,256]{2,1,0:T(8,128)(2,1)S(1)} all-to-all(bf16[16,16,256]{2,1,0:T(8,128)(2,1)S(1)} %bitcast.41), channel_id=1, replica_groups=mesh['x'=4,'zl'=8,'c'=2,'y'=4,'zh'=4] {'y','zh'}, dimensions={0} | all-to-all | bytes 262144 | tf_op jit(solution)/shard_map/all_to_all | solution.py:280
  202.1 0.6 copy.21
  202.7 0.6 copy.20
  (19 shorter events, 0.2 us)
Async XLA Ops:
  0.6 8.5 %copy-start = (s32[4,4,16]{2,1,0:T(4,128)S(1)}, s32[4,4,16]{2,1,0:T(4,128)}, u32[]{:S(2)}) copy-start(s32[4,4,16]{2,1,0:T(4,128)} %param.9) | copy-start | bytes 3076
  2.0 3.2 %collective-permute-start = (bf16[1,4,64,256]{3,2,1,0:T(8,128)(2,1)S(1)}, bf16[1,4,64,256]{3,2,1,0:T(8,128)(2,1)S(1)}, u32[]{:S(2)}, u32[]{:S(2)}) collective-permute-start(bf16[1,4,64,256]{3,2,1,0:T(8,128)(2,1)S(1)} %pad_maximum_fusion.2), channel_id=1, source_target_pairs={{0,16},{4,20},{8,24},{12,28},{16,0},{20,4},{24,8},{28,12},{32,48},... | collective-permute-start | bytes 393224 | tf_op jit(solution)/shard_map/ppermute | solution.py:42
  5.3 8.3 %collective-permute-start.1 = (bf16[2,4,64,256]{3,2,1,0:T(8,128)(2,1)S(1)}, bf16[2,4,64,256]{3,2,1,0:T(8,128)(2,1)S(1)}, u32[]{:S(2)}, u32[]{:S(2)}) collective-permute-start(bf16[2,4,64,256]{3,2,1,0:T(8,128)(2,1)S(1)} %pad_maximum_fusion.refs_0_), channel_id=1, source_target_pairs={{0,32},{4,36},{8,40},{12,44},{16,243},{20,247},{24,251},{28,255},{... | collective-permute-start | bytes 786440 | tf_op jit(solution)/shard_map/ppermute | solution.py:42
  13.6 24.6 %collective-permute-start.2 = (bf16[2,4,64,256]{3,2,1,0:T(8,128)(2,1)S(1)}, bf16[2,4,64,256]{3,2,1,0:T(8,128)(2,1)S(1)}, u32[]{:S(2)}, u32[]{:S(2)}) collective-permute-start(bf16[2,4,64,256]{3,2,1,0:T(8,128)(2,1)S(1)} %collective-permute-done.1.refs_1_), channel_id=1, source_target_pairs={{0,32},{4,36},{8,40},{12,44},{16,243},{20,247},{24,251},{28,255},{... | collective-permute-start | bytes 786440 | tf_op jit(solution)/shard_map/ppermute | solution.py:42
  18.5 19.7 %all-to-all-start = ((s32[8,1,8]{2,1,0:T(1,128)}), s32[8,1,8]{2,1,0:T(1,128)S(1)}, u32[]{:S(2)}, u32[]{:S(2)}) async-start(s32[8,1,8]{2,1,0:T(1,128)} %bitcast.5), calls=%async_computation | async-start | bytes 8192 | tf_op jit(solution)/shard_map/all_to_all | solution.py:246
  39.8 25.7 %all-to-all-start.1 = ((bf16[8,4,64,256]{3,2,1,0:T(8,128)(2,1)}), bf16[8,4,64,256]{3,2,1,0:T(8,128)(2,1)S(1)}, u32[]{:S(2)}, u32[]{:S(2)}) async-start(bf16[8,4,64,256]{3,2,1,0:T(8,128)(2,1)} %pick_blocks.2), calls=%async_computation.1 | async-start | bytes 2097152 | tf_op jit(solution)/shard_map/all_to_all | solution.py:255
  44.7 9.6 %collective-permute-start.3 = (bf16[2,4,64,256]{3,2,1,0:T(8,128)(2,1)S(1)}, bf16[2,4,64,256]{3,2,1,0:T(8,128)(2,1)S(1)}, u32[]{:S(2)}, u32[]{:S(2)}) collective-permute-start(bf16[2,4,64,256]{3,2,1,0:T(8,128)(2,1)S(1)} %collective-permute-done.2.refs_2_.refs_0_), channel_id=1, source_target_pairs={{0,32},{4,36},{8,40},{12,44},{16,243},{20,247},{24,251},{28,255},{... | collective-permute-start | bytes 786440 | tf_op jit(solution)/shard_map/ppermute | solution.py:42
  54.4 9.5 %collective-permute-start.4 = (bf16[2,4,64,256]{3,2,1,0:T(8,128)(2,1)S(1)}, bf16[2,4,64,256]{3,2,1,0:T(8,128)(2,1)S(1)}, u32[]{:S(2)}, u32[]{:S(2)}) collective-permute-start(bf16[2,4,64,256]{3,2,1,0:T(8,128)(2,1)S(1)} %collective-permute-done.3.refs_1_), channel_id=1, source_target_pairs={{0,32},{4,36},{8,40},{12,44},{32,64},{36,68},{40,72},{44,76},{64,9... | collective-permute-start | bytes 786440 | tf_op jit(solution)/shard_map/ppermute | solution.py:42
  65.5 19.5 %copy-start.2 = (bf16[256,4,128]{2,1,0:T(4,128)(2,1)S(1)}, bf16[256,4,128]{2,1,0:T(4,128)(2,1)}, u32[]{:S(2)}) copy-start(bf16[256,4,128]{2,1,0:T(4,128)(2,1)} %param.8) | copy-start | bytes 786436
  65.5 19.5 %all-to-all-start.2 = ((bf16[8,4,64,256]{3,2,1,0:T(8,128)(2,1)}), bf16[8,4,64,256]{3,2,1,0:T(8,128)(2,1)S(1)}, u32[]{:S(2)}, u32[]{:S(2)}) async-start(bf16[8,4,64,256]{3,2,1,0:T(8,128)(2,1)} %pick_blocks.3), calls=%async_computation.2 | async-start | bytes 2097152 | tf_op jit(solution)/shard_map/all_to_all | solution.py:255
  70.5 14.6 %copy-start.1 = (bf16[256,4,128]{2,1,0:T(4,128)(2,1)S(1)}, bf16[256,4,128]{2,1,0:T(4,128)(2,1)}, u32[]{:S(2)}) copy-start(bf16[256,4,128]{2,1,0:T(4,128)(2,1)} %param.5) | copy-start | bytes 786436
  113.1 19.5 %all-to-all-start.4 = ((bf16[8,4,64,256]{3,2,1,0:T(8,128)(2,1)}), bf16[8,4,64,256]{3,2,1,0:T(8,128)(2,1)S(1)}, u32[]{:S(2)}, u32[]{:S(2)}) async-start(bf16[8,4,64,256]{3,2,1,0:T(8,128)(2,1)} %bitcast.14), calls=%async_computation.4 | async-start | bytes 2097152 | tf_op jit(solution)/shard_map/all_to_all | solution.py:269
  119.0 9.0 %collective-permute-start.5 = (bf16[2,4,64,256]{3,2,1,0:T(8,128)(2,1)S(1)}, bf16[2,4,64,256]{3,2,1,0:T(8,128)(2,1)S(1)}, u32[]{:S(2)}, u32[]{:S(2)}) collective-permute-start(bf16[2,4,64,256]{3,2,1,0:T(8,128)(2,1)S(1)} %get-tuple-element.14), channel_id=1, source_target_pairs={{0,227},{4,231},{8,235},{12,239},{16,48},{20,52},{24,56},{28,60},{... | collective-permute-start | bytes 786440 | tf_op jit(solution)/shard_map/ppermute | solution.py:42
  128.1 8.3 %collective-permute-start.6 = (bf16[2,4,64,256]{3,2,1,0:T(8,128)(2,1)S(1)}, bf16[2,4,64,256]{3,2,1,0:T(8,128)(2,1)S(1)}, u32[]{:S(2)}, u32[]{:S(2)}) collective-permute-start(bf16[2,4,64,256]{3,2,1,0:T(8,128)(2,1)S(1)} %add_convert_fusion.2), channel_id=1, source_target_pairs={{0,227},{4,231},{8,235},{12,239},{16,48},{20,52},{24,56},{28,60},{... | collective-permute-start | bytes 786440 | tf_op jit(solution)/shard_map/ppermute | solution.py:42
  136.4 8.3 %collective-permute-start.7 = (bf16[2,4,64,256]{3,2,1,0:T(8,128)(2,1)S(1)}, bf16[2,4,64,256]{3,2,1,0:T(8,128)(2,1)S(1)}, u32[]{:S(2)}, u32[]{:S(2)}) collective-permute-start(bf16[2,4,64,256]{3,2,1,0:T(8,128)(2,1)S(1)} %add_convert_fusion.1), channel_id=1, source_target_pairs={{0,227},{4,231},{8,235},{12,239},{16,48},{20,52},{24,56},{28,60},{... | collective-permute-start | bytes 786440 | tf_op jit(solution)/shard_map/ppermute | solution.py:42
  144.8 6.9 %collective-permute-start.8 = (bf16[4,64,256]{2,1,0:T(8,128)(2,1)S(1)}, bf16[4,64,256]{2,1,0:T(8,128)(2,1)S(1)}, u32[]{:S(2)}, u32[]{:S(2)}) collective-permute-start(bf16[4,64,256]{2,1,0:T(8,128)(2,1)S(1)} %get-tuple-element.28), channel_id=1, source_target_pairs={{0,227},{4,231},{8,235},{12,239},{32,0},{36,4},{40,8},{44,12},{64,... | collective-permute-start | bytes 393224 | tf_op jit(solution)/shard_map/ppermute | solution.py:42
  149.2 3.9 %collective-permute-start.9 = (bf16[4,64,256]{2,1,0:T(8,128)(2,1)S(1)}, bf16[4,64,256]{2,1,0:T(8,128)(2,1)S(1)}, u32[]{:S(2)}, u32[]{:S(2)}) collective-permute-start(bf16[4,64,256]{2,1,0:T(8,128)(2,1)S(1)} %get-tuple-element.29), channel_id=1, source_target_pairs={{0,243},{4,247},{8,251},{12,255},{16,0},{20,4},{24,8},{28,12},{32,... | collective-permute-start | bytes 393224 | tf_op jit(solution)/shard_map/ppermute | solution.py:42

commit v4 on v3

--- a/solution.py
+++ b/solution.py
@@ -163,58 +163,62 @@
         @pl.when(core_ref[0] == core)
         def _():
             for step in range(PER):
-                near_ref = refs[step + 1 - core]
                 for which in range(NC):
+                    near_ref = refs[(step + 1 - core) * NC + which]
                     for peer in range(NX * NC):
                         slot = want_ref[peer, (part * PER + step) * NC + which]
-                        out_ref[peer, step * NC + which] = near_ref[which, jnp.maximum(slot, 0)]
+                        out_ref[peer, step * NC + which] = near_ref[jnp.maximum(slot, 0)]
 
 
 def pick_blocks(part, want, core, near):
-    cores, blocks, rows, width = near[0].shape
+    blocks, rows, width = near[0][0].shape
     shape = (NX * NC, PER * NC, rows, width)
-    spec = pl.BlockSpec(near[0].shape, lambda i, w, h: (0, 0, 0, 0))
+    spec = pl.BlockSpec((blocks, rows, width), lambda i, w, h: (0, 0, 0))
     return pl.pallas_call(
         functools.partial(pick_body, part),
         grid_spec=pltpu.PrefetchScalarGridSpec(
             num_scalar_prefetch=2,
             grid=(1,),
-            in_specs=[spec] * (PER + 1),
+            in_specs=[spec] * (NC * (PER + 1)),
             out_specs=pl.BlockSpec(shape, lambda i, w, h: (0, 0, 0, 0)),
         ),
-        out_shape=jax.ShapeDtypeStruct(shape, near[0].dtype),
+        out_shape=jax.ShapeDtypeStruct(shape, BF16),
         compiler_params=pltpu.CompilerParams(vmem_limit_bytes=32 * 2**20),
         name="pick_blocks",
-    )(want, core, *near[part * PER : (part + 1) * PER + 1])
+    )(want, core, *sum(near[part * PER : (part + 1) * PER + 1], []))
 
 
 def sum_body(part, want_ref, in_ref, *refs):
-    sum_ref = refs[-1]
+    carried_refs, out_refs, sum_ref = refs[: -1 - PER * NC], refs[-1 - PER * NC : -1], refs[-1]
     for step in range(PER):
         for which in range(NC):
             sum_ref[...] = jnp.zeros_like(sum_ref)
             for peer in range(NX * NC):
                 slot = jnp.maximum(want_ref[peer, (part * PER + step) * NC + which], 0)
                 sum_ref[slot] += in_ref[peer, step * NC + which].astype(F32)
-            refs[step][which] = sum_ref[...].astype(BF16)
-
-
-def sum_parts(part, want, parts, blocks):
+            total = sum_ref[...]
+            if carried_refs and step == PER - 1:
+                total += carried_refs[which][...].astype(F32)
+            out_refs[step * NC + which][...] = total.astype(BF16)
+
+
+def sum_parts(part, want, parts, blocks, carried):
     peers, runs, rows, width = parts.shape
-    shape = (NC, blocks, rows, width)
+    shape = (blocks, rows, width)
     return pl.pallas_call(
         functools.partial(sum_body, part),
         grid_spec=pltpu.PrefetchScalarGridSpec(
             num_scalar_prefetch=1,
             grid=(1,),
-            in_specs=[pl.BlockSpec(parts.shape, lambda k, w: (0, 0, 0, 0))],
-            out_specs=[pl.BlockSpec(shape, lambda k, w: (0, 0, 0, 0))] * PER,
+            in_specs=[pl.BlockSpec(parts.shape, lambda k, w: (0, 0, 0, 0))]
+            + [pl.BlockSpec(shape, lambda k, w: (0, 0, 0))] * len(carried),
+            out_specs=[pl.BlockSpec(shape, lambda k, w: (0, 0, 0))] * (PER * NC),
             scratch_shapes=[pltpu.VMEM((blocks, rows, width), F32)],
         ),
-        out_shape=[jax.ShapeDtypeStruct(shape, BF16)] * PER,
+        out_shape=[jax.ShapeDtypeStruct(shape, BF16)] * (PER * NC),
         compiler_params=pltpu.CompilerParams(vmem_limit_bytes=32 * 2**20),
         name="sum_parts",
-    )(want, parts)
+    )(want, parts, *carried)
 
 
 def plus(a, b):
@@ -229,7 +233,7 @@
     home = lax.axis_index("zl").astype(jnp.int32)
     own_keys = lax.dynamic_index_in_dim(key_states, group, 1, keepdims=False)
     own_values = lax.dynamic_index_in_dim(values, group, 1, keepdims=False)
-    own = jnp.concatenate([own_keys, own_values], axis=1).reshape(1, blocks, BLK, 2 * width)
+    own = jnp.concatenate([own_keys, own_values], axis=1).reshape(blocks, BLK, 2 * width)
     picks = lax.dynamic_index_in_dim(picked_blocks, group, 1, keepdims=False)
 
     live = picks >= 0
@@ -245,9 +249,9 @@
     wanted = wanted.reshape(NX * NC, ZL)
     asked = lax.all_to_all(wanted, XC, split_axis=0, concat_axis=0, tiled=True)
 
-    near = [jnp.concatenate([own, send(own, swap_cores)], axis=0)]
+    near = [[own, send(own, swap_cores)]]
     for turn in range(NEAR):
-        near.append(send(near[-1], spread if turn < NEAR - 1 else spread_last))
+        near.append([send(held, spread if turn < NEAR - 1 else spread_last) for held in near[-1]])
 
     got = []
     for part in range(PARTS):
@@ -259,18 +263,19 @@
     bias = jnp.where(live, 0.0, NEG).astype(F32)
     bias = jnp.broadcast_to(bias[:, :, None], (blocks, KSEL, BLK * heads))
     dq, own_grads, *back = attend_grads(
-        slots, queries.reshape(tokens * heads, width), grad_out.reshape(tokens * heads, width), own[0], bias, got
+        slots, queries.reshape(tokens * heads, width), grad_out.reshape(tokens * heads, width), own, bias, got
     )
     grad_queries = dq.reshape(tokens, heads, width)
 
-    sums = [None] * NEAR
+    chain = []
     for part in reversed(range(PARTS)):
         parts = back[part].reshape(NX * NC, PER * NC, BLK, 2 * width)
         parts = lax.all_to_all(parts, XC, split_axis=0, concat_axis=0, tiled=True)
-        sums[part * PER : (part + 1) * PER] = sum_parts(part, asked, parts, blocks)
-    chain = sums[NEAR - 1]
-    for turn in range(NEAR - 2, -1, -1):
-        chain = plus(send(chain, collect), sums[turn])
+        sums = sum_parts(part, asked, parts, blocks, [send(held, collect) for held in chain])
+        chain = sums[(PER - 1) * NC :]
+        for turn in range(PER - 2, -1, -1):
+            more = sums[turn * NC : (turn + 1) * NC]
+            chain = [plus(send(held, collect), new) for held, new in zip(chain, more)]
     same = send(chain[0], collect_same)
     cross = send(chain[1], collect_cross)
     same = jnp.where(core == 0, same, chain[0])

time: 204 us -> 207 us (1.015)
  the two profiles are of different devices: /device:TPU:34 before, /device:TPU:39 now
where the time goes in v4:
time: 207 us; the launch traced here: 206 us
  starting transfers between devices  79.6 us (38%)
  blocking collectives  67.8 us (33%)
  waiting for transfers between devices  38.6 us (19%)
  Pallas kernels  15 us (7%)
  local copies, waits for them, and re-layouts  3.71 us (2%)
    ppermute x17, starting transfers between devices, send(): return lax.ppermute(array, AXES, pairs)  52.9 us
    all_to_all x1, blocking collectives, on_device(): lax.all_to_all(pieces, HEAD, split_axis=0, concat_axis=0, tiled=True)  49.7 us
    ppermute x17, waiting for transfers between devices, send(): return lax.ppermute(array, AXES, pairs)  19.1 us
    all_to_all x1, blocking collectives, on_device(): parts = lax.all_to_all(parts, XC, split_axis=0, concat_axis=0, tiled=True)  18.2 us
    all_to_all x2, starting transfers between devices, on_device(): arrived = lax.all_to_all(sent, XC, split_axis=0, concat_axis=0, tiled=True)  15.9 us
    all_to_all x2, waiting for transfers between devices, on_device(): arrived = lax.all_to_all(sent, XC, split_axis=0, concat_axis=0, tiled=True)  15.7 us
    pallas_call x1, Pallas kernels, attend_grads(): pl.pallas_call(attend_body, grid_spec=pltpu.PrefetchScalarGridSpec(num_sc...  9.73 us
    all_to_all x1, starting transfers between devices, on_device(): parts = lax.all_to_all(parts, XC, split_axis=0, concat_axis=0, tiled=True)  6.25 us
  transfers between devices with their start and end apart: 21, of which 12 were waited for; matrix products, arithmetic and copies ran while one was open for 0% of the time, Pallas kernels for 1%

profile of v4, /device:TPU:39, one launch (start us, length us, event | category | flops | bytes accessed | tf_op | source)
XLA Modules:
  0.0 206.1 jit_solution(17381678664004001642)
XLA Ops:
  0.7 1.3 constant_dynamic-slice_fusion
  2.0 2.6 %collective-permute-start = (bf16[4,64,256]{2,1,0:T(8,128)(2,1)S(1)}, bf16[4,64,256]{2,1,0:T(8,128)(2,1)S(1)}, u32[]{:S(2)}, u32[]{:S(2)}) collective-permute-start(bf16[4,64,256]{2,1,0:T(8,128)(2,1)S(1)} %pad_maximum_fusion.refs_0_.own_ref), channel_id=1, source_target_pairs={{0,16},{4,20},{8,24},{12,28},{16,0},{20,4},{24,8},{28,12},{32,48},... | collective-permute-start | bytes 393224 | tf_op jit(solution)/shard_map/ppermute | solution.py:42
  4.6 1.9 collective-permute-start.1
  6.6 18.2 %collective-permute-start.2 = (bf16[4,64,256]{2,1,0:T(8,128)(2,1)S(1)}, bf16[4,64,256]{2,1,0:T(8,128)(2,1)S(1)}, u32[]{:S(2)}, u32[]{:S(2)}) collective-permute-start(bf16[4,64,256]{2,1,0:T(8,128)(2,1)S(1)} %collective-permute-done.refs_1_), channel_id=1, source_target_pairs={{0,32},{4,36},{8,40},{12,44},{16,243},{20,247},{24,251},{28,255},{... | collective-permute-start | bytes 393224 | tf_op jit(solution)/shard_map/ppermute | solution.py:42
  24.9 2.6 %collective-permute-start.3 = (bf16[4,64,256]{2,1,0:T(8,128)(2,1)S(1)}, bf16[4,64,256]{2,1,0:T(8,128)(2,1)S(1)}, u32[]{:S(2)}, u32[]{:S(2)}) collective-permute-start(bf16[4,64,256]{2,1,0:T(8,128)(2,1)S(1)} %collective-permute-done.1.refs_2_), channel_id=1, source_target_pairs={{0,32},{4,36},{8,40},{12,44},{16,243},{20,247},{24,251},{28,255},{... | collective-permute-start | bytes 393224 | tf_op jit(solution)/shard_map/ppermute | solution.py:42
  27.5 4.2 %collective-permute-start.4 = (bf16[4,64,256]{2,1,0:T(8,128)(2,1)S(1)}, bf16[4,64,256]{2,1,0:T(8,128)(2,1)S(1)}, u32[]{:S(2)}, u32[]{:S(2)}) collective-permute-start(bf16[4,64,256]{2,1,0:T(8,128)(2,1)S(1)} %collective-permute-done.2.refs_3_), channel_id=1, source_target_pairs={{0,32},{4,36},{8,40},{12,44},{16,243},{20,247},{24,251},{28,255},{... | collective-permute-start | bytes 393224 | tf_op jit(solution)/shard_map/ppermute | solution.py:42
  31.7 0.1 slice.12
  31.9 0.1 copy.18
  32.0 0.1 copy.17
  32.1 0.1 select_reduce_fusion
  32.2 0.7 all_to_all.22
  32.9 4.5 %all-to-all-start = ((s32[8,1,8]{2,1,0:T(1,128)}), s32[8,1,8]{2,1,0:T(1,128)S(1)}, u32[]{:S(2)}, u32[]{:S(2)}) async-start(s32[8,1,8]{2,1,0:T(1,128)} %bitcast.5), calls=%async_computation | async-start | bytes 8192 | tf_op jit(solution)/shard_map/all_to_all | solution.py:250
  37.4 2.8 %all-to-all-done = s32[8,1,8]{2,1,0:T(1,128)S(1)} async-done(((s32[8,1,8]{2,1,0:T(1,128)}), s32[8,1,8]{2,1,0:T(1,128)S(1)}, u32[]{:S(2)}, u32[]{:S(2)}) %all-to-all-start) | async-done | bytes 288 | tf_op jit(solution)/shard_map/all_to_all | solution.py:250
  40.2 1.7 pick_blocks.2
  41.9 5.9 %all-to-all-start.1 = ((bf16[8,4,64,256]{3,2,1,0:T(8,128)(2,1)}), bf16[8,4,64,256]{3,2,1,0:T(8,128)(2,1)S(1)}, u32[]{:S(2)}, u32[]{:S(2)}) async-start(bf16[8,4,64,256]{3,2,1,0:T(8,128)(2,1)} %pick_blocks.2), calls=%async_computation.1 | async-start | bytes 2097152 | tf_op jit(solution)/shard_map/all_to_all | solution.py:259
  47.8 2.7 %collective-permute-start.5 = (bf16[4,64,256]{2,1,0:T(8,128)(2,1)S(1)}, bf16[4,64,256]{2,1,0:T(8,128)(2,1)S(1)}, u32[]{:S(2)}, u32[]{:S(2)}) collective-permute-start(bf16[4,64,256]{2,1,0:T(8,128)(2,1)S(1)} %collective-permute-done.3.refs_4_.refs_0_), channel_id=1, source_target_pairs={{0,32},{4,36},{8,40},{12,44},{16,243},{20,247},{24,251},{28,255},{... | collective-permute-start | bytes 393224 | tf_op jit(solution)/shard_map/ppermute | solution.py:42
  50.4 2.3 %collective-permute-start.6 = (bf16[4,64,256]{2,1,0:T(8,128)(2,1)S(1)}, bf16[4,64,256]{2,1,0:T(8,128)(2,1)S(1)}, u32[]{:S(2)}, u32[]{:S(2)}) collective-permute-start(bf16[4,64,256]{2,1,0:T(8,128)(2,1)S(1)} %collective-permute-done.4.refs_5_.refs_1_), channel_id=1, source_target_pairs={{0,32},{4,36},{8,40},{12,44},{16,243},{20,247},{24,251},{28,255},{... | collective-permute-start | bytes 393224 | tf_op jit(solution)/shard_map/ppermute | solution.py:42
  52.7 1.0 collective-permute-done.5.refs_2_
  53.7 0.7 collective-permute-start.7
  54.4 2.0 collective-permute-done.6.refs_3_
  56.4 0.7 collective-permute-start.8
  57.1 1.6 pick_blocks.3
  58.8 2.4 %all-to-all-done.1 = bf16[8,4,64,256]{3,2,1,0:T(8,128)(2,1)S(1)} async-done(((bf16[8,4,64,256]{3,2,1,0:T(8,128)(2,1)}), bf16[8,4,64,256]{3,2,1,0:T(8,128)(2,1)S(1)}, u32[]{:S(2)}, u32[]{:S(2)}) %all-to-all-start.1) | async-done | bytes 1048608 | tf_op jit(solution)/shard_map/all_to_all | solution.py:259
  61.1 10.0 %all-to-all-start.2 = ((bf16[8,4,64,256]{3,2,1,0:T(8,128)(2,1)}), bf16[8,4,64,256]{3,2,1,0:T(8,128)(2,1)S(1)}, u32[]{:S(2)}, u32[]{:S(2)}) async-start(bf16[8,4,64,256]{3,2,1,0:T(8,128)(2,1)} %pick_blocks.3), calls=%async_computation.2 | async-start | bytes 2097152 | tf_op jit(solution)/shard_map/all_to_all | solution.py:259
  71.2 13.4 %all-to-all-done.2 = bf16[8,4,64,256]{3,2,1,0:T(8,128)(2,1)S(1)} async-done(((bf16[8,4,64,256]{3,2,1,0:T(8,128)(2,1)}), bf16[8,4,64,256]{3,2,1,0:T(8,128)(2,1)S(1)}, u32[]{:S(2)}, u32[]{:S(2)}) %all-to-all-start.2) | async-done | bytes 1048608 | tf_op jit(solution)/shard_map/all_to_all | solution.py:259
  84.6 9.7 %attend_grads.1 = (f32[1024,128]{1,0:T(8,128)}, f32[4,64,256]{2,1,0:T(8,128)S(1)}, bf16[32,64,256]{2,1,0:T(8,128)(2,1)}, bf16[32,64,256]{2,1,0:T(8,128)(2,1)S(1)}) custom-call(s32[4,16]{1,0:T(4,128)S(1)} %get-tuple-element.39.slot_ref, bf16[1024,128]{1,0:T(8,128)(2,1)S(1)} %bitcast.21, bf16[1024,128]{1,0:T(8,128)(2,1)S(1)} %bitcast.22, ...), custom_call_target="tpu_custom_call" | custom-call | tf_op jit(solution)/shard_map/attend_grads/pallas_call | solution.py:139
  94.4 18.2 %all_to_all.36.in_ref = bf16[8,4,64,256]{3,2,1,0:T(8,128)(2,1)S(1)} all-to-all(bf16[8,4,64,256]{3,2,1,0:T(8,128)(2,1)S(1)} %bitcast.20), channel_id=1, replica_groups=mesh['x'=4,'zl'=8,'c'=2,'y'=4,'zh'=4] {'x','c'}, dimensions={0} | all-to-all | bytes 2097152 | tf_op jit(solution)/shard_map/all_to_all | solution.py:273
  112.5 6.2 %all-to-all-start.3 = ((bf16[8,4,64,256]{3,2,1,0:T(8,128)(2,1)}), bf16[8,4,64,256]{3,2,1,0:T(8,128)(2,1)S(1)}, u32[]{:S(2)}, u32[]{:S(2)}) async-start(bf16[8,4,64,256]{3,2,1,0:T(8,128)(2,1)} %bitcast.11), calls=%async_computation.3 | async-start | bytes 2097152 | tf_op jit(solution)/shard_map/all_to_all | solution.py:273
  118.8 1.0 sum_parts.2
  119.8 1.9 collective-permute-start.9
  121.7 1.9 collective-permute-start.11
  123.6 3.6 %collective-permute-done.9 = bf16[4,64,256]{2,1,0:T(8,128)(2,1)S(1)} collective-permute-done((bf16[4,64,256]{2,1,0:T(8,128)(2,1)S(1)}, bf16[4,64,256]{2,1,0:T(8,128)(2,1)S(1)}, u32[]{:S(2)}, u32[]{:S(2)}) %collective-permute-start.9) | collective-permute-done | bytes 131104 | tf_op jit(solution)/shard_map/ppermute | solution.py:42
  127.3 1.9 collective-permute-start.10
  129.3 1.9 collective-permute-start.12
  131.2 0.9 all-to-all-done.3.in_ref
  132.2 2.4 %collective-permute-done.10.refs_0_ = bf16[4,64,256]{2,1,0:T(8,128)(2,1)S(1)} collective-permute-done((bf16[4,64,256]{2,1,0:T(8,128)(2,1)S(1)}, bf16[4,64,256]{2,1,0:T(8,128)(2,1)S(1)}, u32[]{:S(2)}, u32[]{:S(2)}) %collective-permute-start.10) | collective-permute-done | bytes 131104 | tf_op jit(solution)/shard_map/ppermute | solution.py:42
  134.5 1.7 collective-permute-done.12.refs_1_
  136.2 1.0 sum_parts.3
  137.2 1.9 collective-permute-start.13
  139.2 1.9 collective-permute-start.15
  141.1 3.1 %collective-permute-done.13 = bf16[4,64,256]{2,1,0:T(8,128)(2,1)S(1)} collective-permute-done((bf16[4,64,256]{2,1,0:T(8,128)(2,1)S(1)}, bf16[4,64,256]{2,1,0:T(8,128)(2,1)S(1)}, u32[]{:S(2)}, u32[]{:S(2)}) %collective-permute-start.13) | collective-permute-done | bytes 131104 | tf_op jit(solution)/shard_map/ppermute | solution.py:42
  144.2 0.7 collective-permute-start.14
  144.9 1.5 collective-permute-done.15
  146.4 4.9 %collective-permute-start.16 = (bf16[4,64,256]{2,1,0:T(8,128)(2,1)S(1)}, bf16[4,64,256]{2,1,0:T(8,128)(2,1)S(1)}, u32[]{:S(2)}, u32[]{:S(2)}) collective-permute-start(bf16[4,64,256]{2,1,0:T(8,128)(2,1)S(1)} %add_convert_fusion.1), channel_id=1, source_target_pairs={{0,243},{4,247},{8,251},{12,255},{16,0},{20,4},{24,8},{28,12},{32,... | collective-permute-start | bytes 393224 | tf_op jit(solution)/shard_map/ppermute | solution.py:42
  151.3 3.8 %collective-permute-done.16 = bf16[4,64,256]{2,1,0:T(8,128)(2,1)S(1)} collective-permute-done((bf16[4,64,256]{2,1,0:T(8,128)(2,1)S(1)}, bf16[4,64,256]{2,1,0:T(8,128)(2,1)S(1)}, u32[]{:S(2)}, u32[]{:S(2)}) %collective-permute-start.16) | collective-permute-done | bytes 131104 | tf_op jit(solution)/shard_map/ppermute | solution.py:42
  155.1 49.7 %all_to_all.37 = bf16[16,16,256]{2,1,0:T(8,128)(2,1)S(1)} all-to-all(bf16[16,16,256]{2,1,0:T(8,128)(2,1)S(1)} %bitcast.27), channel_id=1, replica_groups=mesh['x'=4,'zl'=8,'c'=2,'y'=4,'zh'=4] {'y','zh'}, dimensions={0} | all-to-all | bytes 262144 | tf_op jit(solution)/shard_map/all_to_all | solution.py:285
  204.8 0.6 copy.21
  205.4 0.6 copy.20
  (31 shorter events, 0.5 us)
Async XLA Ops:
  0.6 5.9 %copy-start = (s32[4,4,16]{2,1,0:T(4,128)S(1)}, s32[4,4,16]{2,1,0:T(4,128)}, u32[]{:S(2)}) copy-start(s32[4,4,16]{2,1,0:T(4,128)} %param.9) | copy-start | bytes 3076
  2.0 4.6 %collective-permute-start = (bf16[4,64,256]{2,1,0:T(8,128)(2,1)S(1)}, bf16[4,64,256]{2,1,0:T(8,128)(2,1)S(1)}, u32[]{:S(2)}, u32[]{:S(2)}) collective-permute-start(bf16[4,64,256]{2,1,0:T(8,128)(2,1)S(1)} %pad_maximum_fusion.refs_0_.own_ref), channel_id=1, source_target_pairs={{0,16},{4,20},{8,24},{12,28},{16,0},{20,4},{24,8},{28,12},{32,48},... | collective-permute-start | bytes 393224 | tf_op jit(solution)/shard_map/ppermute | solution.py:42
  4.6 20.2 %collective-permute-start.1 = (bf16[4,64,256]{2,1,0:T(8,128)(2,1)S(1)}, bf16[4,64,256]{2,1,0:T(8,128)(2,1)S(1)}, u32[]{:S(2)}, u32[]{:S(2)}) collective-permute-start(bf16[4,64,256]{2,1,0:T(8,128)(2,1)S(1)} %pad_maximum_fusion.refs_0_.own_ref), channel_id=1, source_target_pairs={{0,32},{4,36},{8,40},{12,44},{16,243},{20,247},{24,251},{28,255},{... | collective-permute-start | bytes 393224 | tf_op jit(solution)/shard_map/ppermute | solution.py:42
  6.6 20.9 %collective-permute-start.2 = (bf16[4,64,256]{2,1,0:T(8,128)(2,1)S(1)}, bf16[4,64,256]{2,1,0:T(8,128)(2,1)S(1)}, u32[]{:S(2)}, u32[]{:S(2)}) collective-permute-start(bf16[4,64,256]{2,1,0:T(8,128)(2,1)S(1)} %collective-permute-done.refs_1_), channel_id=1, source_target_pairs={{0,32},{4,36},{8,40},{12,44},{16,243},{20,247},{24,251},{28,255},{... | collective-permute-start | bytes 393224 | tf_op jit(solution)/shard_map/ppermute | solution.py:42
  24.9 15.3 %collective-permute-start.3 = (bf16[4,64,256]{2,1,0:T(8,128)(2,1)S(1)}, bf16[4,64,256]{2,1,0:T(8,128)(2,1)S(1)}, u32[]{:S(2)}, u32[]{:S(2)}) collective-permute-start(bf16[4,64,256]{2,1,0:T(8,128)(2,1)S(1)} %collective-permute-done.1.refs_2_), channel_id=1, source_target_pairs={{0,32},{4,36},{8,40},{12,44},{16,243},{20,247},{24,251},{28,255},{... | collective-permute-start | bytes 393224 | tf_op jit(solution)/shard_map/ppermute | solution.py:42
  27.5 12.7 %collective-permute-start.4 = (bf16[4,64,256]{2,1,0:T(8,128)(2,1)S(1)}, bf16[4,64,256]{2,1,0:T(8,128)(2,1)S(1)}, u32[]{:S(2)}, u32[]{:S(2)}) collective-permute-start(bf16[4,64,256]{2,1,0:T(8,128)(2,1)S(1)} %collective-permute-done.2.refs_3_), channel_id=1, source_target_pairs={{0,32},{4,36},{8,40},{12,44},{16,243},{20,247},{24,251},{28,255},{... | collective-permute-start | bytes 393224 | tf_op jit(solution)/shard_map/ppermute | solution.py:42
  32.9 7.3 %all-to-all-start = ((s32[8,1,8]{2,1,0:T(1,128)}), s32[8,1,8]{2,1,0:T(1,128)S(1)}, u32[]{:S(2)}, u32[]{:S(2)}) async-start(s32[8,1,8]{2,1,0:T(1,128)} %bitcast.5), calls=%async_computation | async-start | bytes 8192 | tf_op jit(solution)/shard_map/all_to_all | solution.py:250
  41.9 19.3 %all-to-all-start.1 = ((bf16[8,4,64,256]{3,2,1,0:T(8,128)(2,1)}), bf16[8,4,64,256]{3,2,1,0:T(8,128)(2,1)S(1)}, u32[]{:S(2)}, u32[]{:S(2)}) async-start(bf16[8,4,64,256]{3,2,1,0:T(8,128)(2,1)} %pick_blocks.2), calls=%async_computation.1 | async-start | bytes 2097152 | tf_op jit(solution)/shard_map/all_to_all | solution.py:259
  47.8 6.0 %collective-permute-start.5 = (bf16[4,64,256]{2,1,0:T(8,128)(2,1)S(1)}, bf16[4,64,256]{2,1,0:T(8,128)(2,1)S(1)}, u32[]{:S(2)}, u32[]{:S(2)}) collective-permute-start(bf16[4,64,256]{2,1,0:T(8,128)(2,1)S(1)} %collective-permute-done.3.refs_4_.refs_0_), channel_id=1, source_target_pairs={{0,32},{4,36},{8,40},{12,44},{16,243},{20,247},{24,251},{28,255},{... | collective-permute-start | bytes 393224 | tf_op jit(solution)/shard_map/ppermute | solution.py:42
  50.4 6.0 %collective-permute-start.6 = (bf16[4,64,256]{2,1,0:T(8,128)(2,1)S(1)}, bf16[4,64,256]{2,1,0:T(8,128)(2,1)S(1)}, u32[]{:S(2)}, u32[]{:S(2)}) collective-permute-start(bf16[4,64,256]{2,1,0:T(8,128)(2,1)S(1)} %collective-permute-done.4.refs_5_.refs_1_), channel_id=1, source_target_pairs={{0,32},{4,36},{8,40},{12,44},{16,243},{20,247},{24,251},{28,255},{... | collective-permute-start | bytes 393224 | tf_op jit(solution)/shard_map/ppermute | solution.py:42
  53.7 3.3 %collective-permute-start.7 = (bf16[4,64,256]{2,1,0:T(8,128)(2,1)S(1)}, bf16[4,64,256]{2,1,0:T(8,128)(2,1)S(1)}, u32[]{:S(2)}, u32[]{:S(2)}) collective-permute-start(bf16[4,64,256]{2,1,0:T(8,128)(2,1)S(1)} %collective-permute-done.5.refs_2_), channel_id=1, source_target_pairs={{0,32},{4,36},{8,40},{12,44},{32,64},{36,68},{40,72},{44,76},{64,9... | collective-permute-start | bytes 393224 | tf_op jit(solution)/shard_map/ppermute | solution.py:42
  56.4 0.7 collective-permute-start.8
  58.8 25.9 %copy-start.1 = (bf16[256,4,128]{2,1,0:T(4,128)(2,1)S(1)}, bf16[256,4,128]{2,1,0:T(4,128)(2,1)}, u32[]{:S(2)}) copy-start(bf16[256,4,128]{2,1,0:T(4,128)(2,1)} %param.5) | copy-start | bytes 786436
  58.8 25.9 %copy-start.2 = (bf16[256,4,128]{2,1,0:T(4,128)(2,1)S(1)}, bf16[256,4,128]{2,1,0:T(4,128)(2,1)}, u32[]{:S(2)}) copy-start(bf16[256,4,128]{2,1,0:T(4,128)(2,1)} %param.8) | copy-start | bytes 786436
  61.1 23.4 %all-to-all-start.2 = ((bf16[8,4,64,256]{3,2,1,0:T(8,128)(2,1)}), bf16[8,4,64,256]{3,2,1,0:T(8,128)(2,1)S(1)}, u32[]{:S(2)}, u32[]{:S(2)}) async-start(bf16[8,4,64,256]{3,2,1,0:T(8,128)(2,1)} %pick_blocks.3), calls=%async_computation.2 | async-start | bytes 2097152 | tf_op jit(solution)/shard_map/all_to_all | solution.py:259
  112.5 19.6 %all-to-all-start.3 = ((bf16[8,4,64,256]{3,2,1,0:T(8,128)(2,1)}), bf16[8,4,64,256]{3,2,1,0:T(8,128)(2,1)S(1)}, u32[]{:S(2)}, u32[]{:S(2)}) async-start(bf16[8,4,64,256]{3,2,1,0:T(8,128)(2,1)} %bitcast.11), calls=%async_computation.3 | async-start | bytes 2097152 | tf_op jit(solution)/shard_map/all_to_all | solution.py:273
  119.8 7.5 %collective-permute-start.9 = (bf16[4,64,256]{2,1,0:T(8,128)(2,1)S(1)}, bf16[4,64,256]{2,1,0:T(8,128)(2,1)S(1)}, u32[]{:S(2)}, u32[]{:S(2)}) collective-permute-start(bf16[4,64,256]{2,1,0:T(8,128)(2,1)S(1)} %get-tuple-element.19), channel_id=1, source_target_pairs={{0,227},{4,231},{8,235},{12,239},{16,48},{20,52},{24,56},{28,60},{... | collective-permute-start | bytes 393224 | tf_op jit(solution)/shard_map/ppermute | solution.py:42
  121.7 7.5 %collective-permute-start.11 = (bf16[4,64,256]{2,1,0:T(8,128)(2,1)S(1)}, bf16[4,64,256]{2,1,0:T(8,128)(2,1)S(1)}, u32[]{:S(2)}, u32[]{:S(2)}) collective-permute-start(bf16[4,64,256]{2,1,0:T(8,128)(2,1)S(1)} %get-tuple-element.21), channel_id=1, source_target_pairs={{0,227},{4,231},{8,235},{12,239},{16,48},{20,52},{24,56},{28,60},{... | collective-permute-start | bytes 393224 | tf_op jit(solution)/shard_map/ppermute | solution.py:42
  127.3 7.2 %collective-permute-start.10 = (bf16[4,64,256]{2,1,0:T(8,128)(2,1)S(1)}, bf16[4,64,256]{2,1,0:T(8,128)(2,1)S(1)}, u32[]{:S(2)}, u32[]{:S(2)}) collective-permute-start(bf16[4,64,256]{2,1,0:T(8,128)(2,1)S(1)} %add_convert_fusion.4), channel_id=1, source_target_pairs={{0,227},{4,231},{8,235},{12,239},{16,48},{20,52},{24,56},{28,60},{... | collective-permute-start | bytes 393224 | tf_op jit(solution)/shard_map/ppermute | solution.py:42
  129.3 6.9 %collective-permute-start.12 = (bf16[4,64,256]{2,1,0:T(8,128)(2,1)S(1)}, bf16[4,64,256]{2,1,0:T(8,128)(2,1)S(1)}, u32[]{:S(2)}, u32[]{:S(2)}) collective-permute-start(bf16[4,64,256]{2,1,0:T(8,128)(2,1)S(1)} %add_convert_fusion.3), channel_id=1, source_target_pairs={{0,227},{4,231},{8,235},{12,239},{16,48},{20,52},{24,56},{28,60},{... | collective-permute-start | bytes 393224 | tf_op jit(solution)/shard_map/ppermute | solution.py:42
  137.2 6.9 %collective-permute-start.13 = (bf16[4,64,256]{2,1,0:T(8,128)(2,1)S(1)}, bf16[4,64,256]{2,1,0:T(8,128)(2,1)S(1)}, u32[]{:S(2)}, u32[]{:S(2)}) collective-permute-start(bf16[4,64,256]{2,1,0:T(8,128)(2,1)S(1)} %get-tuple-element.23), channel_id=1, source_target_pairs={{0,227},{4,231},{8,235},{12,239},{16,48},{20,52},{24,56},{28,60},{... | collective-permute-start | bytes 393224 | tf_op jit(solution)/shard_map/ppermute | solution.py:42
  139.2 7.2 %collective-permute-start.15 = (bf16[4,64,256]{2,1,0:T(8,128)(2,1)S(1)}, bf16[4,64,256]{2,1,0:T(8,128)(2,1)S(1)}, u32[]{:S(2)}, u32[]{:S(2)}) collective-permute-start(bf16[4,64,256]{2,1,0:T(8,128)(2,1)S(1)} %get-tuple-element.25), channel_id=1, source_target_pairs={{0,227},{4,231},{8,235},{12,239},{16,48},{20,52},{24,56},{28,60},{... | collective-permute-start | bytes 393224 | tf_op jit(solution)/shard_map/ppermute | solution.py:42
  144.2 7.1 %collective-permute-start.14 = (bf16[4,64,256]{2,1,0:T(8,128)(2,1)S(1)}, bf16[4,64,256]{2,1,0:T(8,128)(2,1)S(1)}, u32[]{:S(2)}, u32[]{:S(2)}) collective-permute-start(bf16[4,64,256]{2,1,0:T(8,128)(2,1)S(1)} %add_convert_fusion.2), channel_id=1, source_target_pairs={{0,227},{4,231},{8,235},{12,239},{32,0},{36,4},{40,8},{44,12},{64,... | collective-permute-start | bytes 393224 | tf_op jit(solution)/shard_map/ppermute | solution.py:42
  146.4 8.7 %collective-permute-start.16 = (bf16[4,64,256]{2,1,0:T(8,128)(2,1)S(1)}, bf16[4,64,256]{2,1,0:T(8,128)(2,1)S(1)}, u32[]{:S(2)}, u32[]{:S(2)}) collective-permute-start(bf16[4,64,256]{2,1,0:T(8,128)(2,1)S(1)} %add_convert_fusion.1), channel_id=1, source_target_pairs={{0,243},{4,247},{8,251},{12,255},{16,0},{20,4},{24,8},{28,12},{32,... | collective-permute-start | bytes 393224 | tf_op jit(solution)/shard_map/ppermute | solution.py:42

commit v5 on v4

--- a/solution.py
+++ b/solution.py
@@ -18,9 +18,9 @@
 HEAD = ("y", "zh")
 XC = ("x", "c")
 AXES = SEQ + HEAD
-NEAR = ZL // 2
+AWAY = [(p + 1) // 2 if p % 2 else -(p // 2) for p in range(ZL)]
 PARTS = 2
-PER = NEAR // PARTS
+PER = ZL // PARTS
 
 F32 = jnp.float32
 BF16 = jnp.bfloat16
@@ -30,40 +30,15 @@
     return (((x * ZL + z % ZL) * NC + c) * NY + y) * ZH + z % NZ // ZL
 
 
-def send(array, move):
-    pairs = []
-    for x in range(NX):
-        for z in range(NZ):
-            for c in range(NC):
-                for y in range(NY):
-                    to = move(c)
-                    if to is not None:
-                        pairs.append((number(x, z, c, y), number(x, z + to[0], to[1], y)))
+def send(array, step):
+    pairs = [
+        (number(x, z, c, y), number(x, z + step, c, y))
+        for x in range(NX)
+        for z in range(NZ)
+        for c in range(NC)
+        for y in range(NY)
+    ]
     return lax.ppermute(array, AXES, pairs)
-
-
-def swap_cores(c):
-    return (0, 1 - c)
-
-
-def spread(c):
-    return (1 if c == 0 else -1, c)
-
-
-def spread_last(c):
-    return (1, 0) if c == 0 else None
-
-
-def collect(c):
-    return (-1 if c == 0 else 1, c)
-
-
-def collect_same(c):
-    return (-1, 0) if c == 0 else None
-
-
-def collect_cross(c):
-    return (-1, 1) if c == 0 else (0, 0)
 
 
 def attend_body(slot_ref, q_ref, g_ref, own_ref, bias_ref, *refs):
@@ -156,53 +131,46 @@
     )(slots, q_rows, g_rows, own, bias, *got)
 
 
-def pick_body(part, want_ref, core_ref, *refs):
+def pick_body(part, want_ref, *refs):
     out_ref = refs[-1]
-    for core in range(NC):
-
-        @pl.when(core_ref[0] == core)
-        def _():
-            for step in range(PER):
-                for which in range(NC):
-                    near_ref = refs[(step + 1 - core) * NC + which]
-                    for peer in range(NX * NC):
-                        slot = want_ref[peer, (part * PER + step) * NC + which]
-                        out_ref[peer, step * NC + which] = near_ref[jnp.maximum(slot, 0)]
-
-
-def pick_blocks(part, want, core, near):
-    blocks, rows, width = near[0][0].shape
-    shape = (NX * NC, PER * NC, rows, width)
-    spec = pl.BlockSpec((blocks, rows, width), lambda i, w, h: (0, 0, 0))
+    for place, near_ref in enumerate(refs[:-1]):
+        for peer in range(NX * NC):
+            slot = want_ref[peer, part * PER + place]
+            out_ref[peer, place] = near_ref[jnp.maximum(slot, 0)]
+
+
+def pick_blocks(part, want, near):
+    blocks, rows, width = near[0].shape
+    shape = (NX * NC, PER, rows, width)
     return pl.pallas_call(
         functools.partial(pick_body, part),
         grid_spec=pltpu.PrefetchScalarGridSpec(
-            num_scalar_prefetch=2,
+            num_scalar_prefetch=1,
             grid=(1,),
-            in_specs=[spec] * (NC * (PER + 1)),
-            out_specs=pl.BlockSpec(shape, lambda i, w, h: (0, 0, 0, 0)),
+            in_specs=[pl.BlockSpec((blocks, rows, width), lambda i, w: (0, 0, 0))] * PER,
+            out_specs=pl.BlockSpec(shape, lambda i, w: (0, 0, 0, 0)),
         ),
         out_shape=jax.ShapeDtypeStruct(shape, BF16),
         compiler_params=pltpu.CompilerParams(vmem_limit_bytes=32 * 2**20),
         name="pick_blocks",
-    )(want, core, *sum(near[part * PER : (part + 1) * PER + 1], []))
+    )(want, *near[part * PER : (part + 1) * PER])
 
 
 def sum_body(part, want_ref, in_ref, *refs):
-    carried_refs, out_refs, sum_ref = refs[: -1 - PER * NC], refs[-1 - PER * NC : -1], refs[-1]
-    for step in range(PER):
-        for which in range(NC):
-            sum_ref[...] = jnp.zeros_like(sum_ref)
-            for peer in range(NX * NC):
-                slot = jnp.maximum(want_ref[peer, (part * PER + step) * NC + which], 0)
-                sum_ref[slot] += in_ref[peer, step * NC + which].astype(F32)
-            total = sum_ref[...]
-            if carried_refs and step == PER - 1:
-                total += carried_refs[which][...].astype(F32)
-            out_refs[step * NC + which][...] = total.astype(BF16)
-
-
-def sum_parts(part, want, parts, blocks, carried):
+    home_refs, out_refs, sum_ref = refs[: -1 - PER], refs[-1 - PER : -1], refs[-1]
+    for place, out_ref in enumerate(out_refs):
+        sum_ref[...] = jnp.zeros_like(sum_ref)
+        for peer in range(NX * NC):
+            slot = jnp.maximum(want_ref[peer, part * PER + place], 0)
+            sum_ref[slot] += in_ref[peer, place].astype(F32)
+        total = sum_ref[...]
+        if place == 0:
+            for home_ref in home_refs:
+                total += home_ref[...].astype(F32)
+        out_ref[...] = total.astype(out_ref.dtype)
+
+
+def sum_parts(part, want, parts, blocks, home):
     peers, runs, rows, width = parts.shape
     shape = (blocks, rows, width)
     return pl.pallas_call(
@@ -211,25 +179,20 @@
             num_scalar_prefetch=1,
             grid=(1,),
             in_specs=[pl.BlockSpec(parts.shape, lambda k, w: (0, 0, 0, 0))]
-            + [pl.BlockSpec(shape, lambda k, w: (0, 0, 0))] * len(carried),
-            out_specs=[pl.BlockSpec(shape, lambda k, w: (0, 0, 0))] * (PER * NC),
-            scratch_shapes=[pltpu.VMEM((blocks, rows, width), F32)],
+            + [pl.BlockSpec(shape, lambda k, w: (0, 0, 0))] * len(home),
+            out_specs=[pl.BlockSpec(shape, lambda k, w: (0, 0, 0))] * PER,
+            scratch_shapes=[pltpu.VMEM(shape, F32)],
         ),
-        out_shape=[jax.ShapeDtypeStruct(shape, BF16)] * (PER * NC),
+        out_shape=[jax.ShapeDtypeStruct(shape, BF16 if place or not home else F32) for place in range(PER)],
         compiler_params=pltpu.CompilerParams(vmem_limit_bytes=32 * 2**20),
         name="sum_parts",
-    )(want, parts, *carried)
-
-
-def plus(a, b):
-    return (a.astype(F32) + b.astype(F32)).astype(BF16)
+    )(want, parts, *home)
 
 
 def on_device(queries, key_states, values, grad_out, picked_blocks):
     tokens, heads, width = queries.shape
     blocks = tokens // BLK
     group = lax.axis_index("y")
-    core = lax.axis_index("c").astype(jnp.int32)
     home = lax.axis_index("zl").astype(jnp.int32)
     own_keys = lax.dynamic_index_in_dim(key_states, group, 1, keepdims=False)
     own_values = lax.dynamic_index_in_dim(values, group, 1, keepdims=False)
@@ -239,26 +202,21 @@
     live = picks >= 0
     run = picks // blocks
     ahead = lax.rem(run // NC % ZL - home + ZL, ZL)
-    holder = (ahead < NEAR).astype(jnp.int32)
-    step = jnp.where(holder == 1, ahead, ZL - 1 - ahead)
-    which = jnp.where(run % NC == holder, 0, 1)
-    peer = run // (ZL * NC) * NC + holder
-    place = jnp.where(live, peer * ZL + step * NC + which, -1)
-    match = place[:, 1:, None] == jnp.arange(NX * ZL * NC, dtype=jnp.int32)
+    place = jnp.where(ahead <= ZL // 2, jnp.maximum(2 * ahead - 1, 0), 2 * (ZL - ahead))
+    peer = run // (ZL * NC) * NC + run % NC
+    key = jnp.where(live, peer * ZL + place, -1)
+    match = key[:, 1:, None] == jnp.arange(NX * ZL * NC, dtype=jnp.int32)
     wanted = jnp.max(jnp.where(match, (picks % blocks)[:, 1:, None], -1), axis=(0, 1))
     wanted = wanted.reshape(NX * NC, ZL)
     asked = lax.all_to_all(wanted, XC, split_axis=0, concat_axis=0, tiled=True)
 
-    near = [[own, send(own, swap_cores)]]
-    for turn in range(NEAR):
-        near.append([send(held, spread if turn < NEAR - 1 else spread_last) for held in near[-1]])
-
-    got = []
-    for part in range(PARTS):
-        sent = pick_blocks(part, asked, core[None], near)
+    near = [own] + [send(own, -away) for away in AWAY[1:]]
+    got = [None] * PARTS
+    for part in reversed(range(PARTS)):
+        sent = pick_blocks(part, asked, near)
         arrived = lax.all_to_all(sent, XC, split_axis=0, concat_axis=0, tiled=True)
-        got.append(arrived.reshape(NX * NC * PER * NC, BLK, 2 * width))
-    slots = (step // PER * (NX * NC) + peer) * (PER * NC) + step % PER * NC + which
+        got[part] = arrived.reshape(NX * NC * PER, BLK, 2 * width)
+    slots = (place // PER * (NX * NC) + peer) * PER + place % PER
     slots = jnp.where(live, slots, -1)
     bias = jnp.where(live, 0.0, NEG).astype(F32)
     bias = jnp.broadcast_to(bias[:, :, None], (blocks, KSEL, BLK * heads))
@@ -267,19 +225,17 @@
     )
     grad_queries = dq.reshape(tokens, heads, width)
 
-    chain = []
+    arrived = [own_grads]
     for part in reversed(range(PARTS)):
-        parts = back[part].reshape(NX * NC, PER * NC, BLK, 2 * width)
+        parts = back[part].reshape(NX * NC, PER, BLK, 2 * width)
         parts = lax.all_to_all(parts, XC, split_axis=0, concat_axis=0, tiled=True)
-        sums = sum_parts(part, asked, parts, blocks, [send(held, collect) for held in chain])
-        chain = sums[(PER - 1) * NC :]
-        for turn in range(PER - 2, -1, -1):
-            more = sums[turn * NC : (turn + 1) * NC]
-            chain = [plus(send(held, collect), new) for held, new in zip(chain, more)]
-    same = send(chain[0], collect_same)
-    cross = send(chain[1], collect_cross)
-    same = jnp.where(core == 0, same, chain[0])
-    total = own_grads + same.astype(F32) + cross.astype(F32)
+        sums = sum_parts(part, asked, parts, blocks, [] if part else arrived)
+        if part == 0:
+            arrived = [sums[0]]
+        for away, held in zip(reversed(AWAY[part * PER : (part + 1) * PER]), reversed(sums)):
+            if away:
+                arrived.append(send(held, away))
+    total = sum(held.astype(F32) for held in arrived)
 
     pieces = total.astype(BF16).reshape(NY * ZH, tokens // (NY * ZH), 2 * width)
     pieces = lax.all_to_all(pieces, HEAD, split_axis=0, concat_axis=0, tiled=True)

time: 207 us -> 212 us (1.024)
  the two profiles are of different devices: /device:TPU:39 before, /device:TPU:34 now
where the time goes in v5:
time: 212 us
  starting transfers between devices  83.3 us (39%)
  blocking collectives  78.2 us (37%)
  waiting for transfers between devices  30.9 us (15%)
  Pallas kernels  15 us (7%)
  local copies, waits for them, and re-layouts  3.11 us (1%)
    ppermute x14, starting transfers between devices, send(): return lax.ppermute(array, AXES, pairs)  68.6 us
    all_to_all x1, blocking collectives, on_device(): lax.all_to_all(pieces, HEAD, split_axis=0, concat_axis=0, tiled=True)  51.3 us
    all_to_all x1, blocking collectives, on_device(): parts = lax.all_to_all(parts, XC, split_axis=0, concat_axis=0, tiled=True)  18.5 us
    ppermute x14, waiting for transfers between devices, send(): return lax.ppermute(array, AXES, pairs)  16.4 us
    all_to_all x2, waiting for transfers between devices, on_device(): arrived = lax.all_to_all(sent, XC, split_axis=0, concat_axis=0, tiled=True)  14.5 us
    all_to_all x2, starting transfers between devices, on_device(): arrived = lax.all_to_all(sent, XC, split_axis=0, concat_axis=0, tiled=True)  9.78 us
    pallas_call x1, Pallas kernels, attend_grads(): pl.pallas_call(attend_body, grid_spec=pltpu.PrefetchScalarGridSpec(num_sc...  9.62 us
    all_to_all x1, blocking collectives, on_device(): asked = lax.all_to_all(wanted, XC, split_axis=0, concat_axis=0, tiled=True)  8.43 us
  transfers between devices with their start and end apart: 17, of which 9 were waited for; matrix products, arithmetic and copies ran while one was open for 0% of the time, Pallas kernels for 1%

profile of v5, /device:TPU:34, one launch (start us, length us, event | category | flops | bytes accessed | tf_op | source)
XLA Modules:
  0.0 211.7 jit_solution(6563894177180336042)
XLA Ops:
  0.6 0.0 copy-start
  0.7 1.3 constant_dynamic-slice_fusion
  2.0 19.1 %collective-permute-start.6 = (bf16[4,64,256]{2,1,0:T(8,128)(2,1)S(1)}, bf16[4,64,256]{2,1,0:T(8,128)(2,1)S(1)}, u32[]{:S(2)}, u32[]{:S(2)}) collective-permute-start(bf16[4,64,256]{2,1,0:T(8,128)(2,1)S(1)} %pad_maximum_fusion.refs_0_.own_ref), channel_id=1, source_target_pairs={{0,131},{4,135},{8,139},{12,143},{16,147},{20,151},{24,155},{28,15... | collective-permute-start | bytes 393224 | tf_op jit(solution)/shard_map/ppermute | solution.py:41
  21.1 1.9 collective-permute-start.5
  23.1 6.9 %collective-permute-start.4 = (bf16[4,64,256]{2,1,0:T(8,128)(2,1)S(1)}, bf16[4,64,256]{2,1,0:T(8,128)(2,1)S(1)}, u32[]{:S(2)}, u32[]{:S(2)}) collective-permute-start(bf16[4,64,256]{2,1,0:T(8,128)(2,1)S(1)} %pad_maximum_fusion.refs_0_.own_ref), channel_id=1, source_target_pairs={{0,163},{4,167},{8,171},{12,175},{16,179},{20,183},{24,187},{28,19... | collective-permute-start | bytes 393224 | tf_op jit(solution)/shard_map/ppermute | solution.py:41
  30.0 2.2 %collective-permute-start.3 = (bf16[4,64,256]{2,1,0:T(8,128)(2,1)S(1)}, bf16[4,64,256]{2,1,0:T(8,128)(2,1)S(1)}, u32[]{:S(2)}, u32[]{:S(2)}) collective-permute-start(bf16[4,64,256]{2,1,0:T(8,128)(2,1)S(1)} %pad_maximum_fusion.refs_0_.own_ref), channel_id=1, source_target_pairs={{0,64},{4,68},{8,72},{12,76},{16,80},{20,84},{24,88},{28,92},{32,9... | collective-permute-start | bytes 393224 | tf_op jit(solution)/shard_map/ppermute | solution.py:41
  32.3 0.1 slice.12
  32.3 0.1 slice.13
  32.4 0.1 copy.18
  32.5 0.1 copy.17
  32.6 0.1 select_reduce_fusion
  32.7 0.1 all_to_all.22
  32.8 8.4 %all_to_all.36 = s32[8,1,8]{2,1,0:T(1,128)S(1)} all-to-all(s32[8,1,8]{2,1,0:T(1,128)S(1)} %bitcast.30), channel_id=1, replica_groups=mesh['x'=4,'zl'=8,'c'=2,'y'=4,'zh'=4] {'x','c'}, dimensions={0} | all-to-all | bytes 512 | tf_op jit(solution)/shard_map/all_to_all | solution.py:211
  41.2 0.0 collective-permute-done.6.refs_3_
  41.2 0.0 collective-permute-done.5.refs_2_
  41.2 0.6 collective-permute-done.3.refs_0_
  41.9 1.6 pick_blocks.3
  43.5 4.8 %all-to-all-start.2 = ((bf16[8,4,64,256]{3,2,1,0:T(8,128)(2,1)}), bf16[8,4,64,256]{3,2,1,0:T(8,128)(2,1)S(1)}, u32[]{:S(2)}, u32[]{:S(2)}) async-start(bf16[8,4,64,256]{3,2,1,0:T(8,128)(2,1)} %pick_blocks.3), calls=%async_computation.2 | async-start | bytes 2097152 | tf_op jit(solution)/shard_map/all_to_all | solution.py:217
  48.3 5.2 %collective-permute-start.2 = (bf16[4,64,256]{2,1,0:T(8,128)(2,1)S(1)}, bf16[4,64,256]{2,1,0:T(8,128)(2,1)S(1)}, u32[]{:S(2)}, u32[]{:S(2)}) collective-permute-start(bf16[4,64,256]{2,1,0:T(8,128)(2,1)S(1)} %pad_maximum_fusion.refs_0_.own_ref), channel_id=1, source_target_pairs={{0,195},{4,199},{8,203},{12,207},{16,211},{20,215},{24,219},{28,22... | collective-permute-start | bytes 393224 | tf_op jit(solution)/shard_map/ppermute | solution.py:41
  53.6 1.9 collective-permute-start.1
  55.5 3.9 %collective-permute-start = (bf16[4,64,256]{2,1,0:T(8,128)(2,1)S(1)}, bf16[4,64,256]{2,1,0:T(8,128)(2,1)S(1)}, u32[]{:S(2)}, u32[]{:S(2)}) collective-permute-start(bf16[4,64,256]{2,1,0:T(8,128)(2,1)S(1)} %pad_maximum_fusion.refs_0_.own_ref), channel_id=1, source_target_pairs={{0,227},{4,231},{8,235},{12,239},{16,243},{20,247},{24,251},{28,25... | collective-permute-start | bytes 393224 | tf_op jit(solution)/shard_map/ppermute | solution.py:41
  59.5 0.3 collective-permute-done.2.refs_3_
  59.7 1.0 collective-permute-done.1.refs_2_
  60.8 1.9 collective-permute-done.refs_1_
  62.7 1.7 pick_blocks.2
  64.4 4.9 %all-to-all-start.1 = ((bf16[8,4,64,256]{3,2,1,0:T(8,128)(2,1)}), bf16[8,4,64,256]{3,2,1,0:T(8,128)(2,1)S(1)}, u32[]{:S(2)}, u32[]{:S(2)}) async-start(bf16[8,4,64,256]{3,2,1,0:T(8,128)(2,1)} %pick_blocks.2), calls=%async_computation.1 | async-start | bytes 2097152 | tf_op jit(solution)/shard_map/all_to_all | solution.py:217
  69.3 14.5 %all-to-all-done.1 = bf16[8,4,64,256]{3,2,1,0:T(8,128)(2,1)S(1)} async-done(((bf16[8,4,64,256]{3,2,1,0:T(8,128)(2,1)}), bf16[8,4,64,256]{3,2,1,0:T(8,128)(2,1)S(1)}, u32[]{:S(2)}, u32[]{:S(2)}) %all-to-all-start.1) | async-done | bytes 1048608 | tf_op jit(solution)/shard_map/all_to_all | solution.py:217
  83.8 0.1 broadcast_in_dim.34.bias_ref
  83.9 9.6 %attend_grads.1 = (f32[1024,128]{1,0:T(8,128)}, f32[4,64,256]{2,1,0:T(8,128)S(1)}, bf16[32,64,256]{2,1,0:T(8,128)(2,1)}, bf16[32,64,256]{2,1,0:T(8,128)(2,1)S(1)}) custom-call(s32[4,16]{1,0:T(4,128)S(1)} %fusion.8.slot_ref, bf16[1024,128]{1,0:T(8,128)(2,1)S(1)} %bitcast.20, bf16[1024,128]{1,0:T(8,128)(2,1)S(1)} %bitcast.21, ...), custom_call_target="tpu_custom_call" | custom-call | tf_op jit(solution)/shard_map/attend_grads/pallas_call | solution.py:114
  93.5 18.5 %all_to_all.37.in_ref = bf16[8,4,64,256]{3,2,1,0:T(8,128)(2,1)S(1)} all-to-all(bf16[8,4,64,256]{3,2,1,0:T(8,128)(2,1)S(1)} %bitcast.19), channel_id=1, replica_groups=mesh['x'=4,'zl'=8,'c'=2,'y'=4,'zh'=4] {'x','c'}, dimensions={0} | all-to-all | bytes 2097152 | tf_op jit(solution)/shard_map/all_to_all | solution.py:231
  112.0 4.9 %all-to-all-start.3 = ((bf16[8,4,64,256]{3,2,1,0:T(8,128)(2,1)}), bf16[8,4,64,256]{3,2,1,0:T(8,128)(2,1)S(1)}, u32[]{:S(2)}, u32[]{:S(2)}) async-start(bf16[8,4,64,256]{3,2,1,0:T(8,128)(2,1)} %bitcast.10), calls=%async_computation.3 | async-start | bytes 2097152 | tf_op jit(solution)/shard_map/all_to_all | solution.py:231
  116.9 1.0 sum_parts.2
  117.9 2.4 %collective-permute-start.7 = (bf16[4,64,256]{2,1,0:T(8,128)(2,1)S(1)}, bf16[4,64,256]{2,1,0:T(8,128)(2,1)S(1)}, u32[]{:S(2)}, u32[]{:S(2)}) collective-permute-start(bf16[4,64,256]{2,1,0:T(8,128)(2,1)S(1)} %get-tuple-element.19), channel_id=1, source_target_pairs={{0,128},{4,132},{8,136},{12,140},{16,144},{20,148},{24,152},{28,15... | collective-permute-start | bytes 393224 | tf_op jit(solution)/shard_map/ppermute | solution.py:41
  120.3 6.1 %collective-permute-start.8 = (bf16[4,64,256]{2,1,0:T(8,128)(2,1)S(1)}, bf16[4,64,256]{2,1,0:T(8,128)(2,1)S(1)}, u32[]{:S(2)}, u32[]{:S(2)}) collective-permute-start(bf16[4,64,256]{2,1,0:T(8,128)(2,1)S(1)} %get-tuple-element.20), channel_id=1, source_target_pairs={{0,163},{4,167},{8,171},{12,175},{16,179},{20,183},{24,187},{28,19... | collective-permute-start | bytes 393224 | tf_op jit(solution)/shard_map/ppermute | solution.py:41
  126.4 2.8 %collective-permute-start.9 = (bf16[4,64,256]{2,1,0:T(8,128)(2,1)S(1)}, bf16[4,64,256]{2,1,0:T(8,128)(2,1)S(1)}, u32[]{:S(2)}, u32[]{:S(2)}) collective-permute-start(bf16[4,64,256]{2,1,0:T(8,128)(2,1)S(1)} %get-tuple-element.21), channel_id=1, source_target_pairs={{0,96},{4,100},{8,104},{12,108},{16,112},{20,116},{24,120},{28,124... | collective-permute-start | bytes 393224 | tf_op jit(solution)/shard_map/ppermute | solution.py:41
  129.2 7.0 %collective-permute-start.10 = (bf16[4,64,256]{2,1,0:T(8,128)(2,1)S(1)}, bf16[4,64,256]{2,1,0:T(8,128)(2,1)S(1)}, u32[]{:S(2)}, u32[]{:S(2)}) collective-permute-start(bf16[4,64,256]{2,1,0:T(8,128)(2,1)S(1)} %get-tuple-element.22), channel_id=1, source_target_pairs={{0,195},{4,199},{8,203},{12,207},{16,211},{20,215},{24,219},{28,22... | collective-permute-start | bytes 393224 | tf_op jit(solution)/shard_map/ppermute | solution.py:41
  136.2 7.6 %collective-permute-done.9.refs_3_ = bf16[4,64,256]{2,1,0:T(8,128)(2,1)S(1)} collective-permute-done((bf16[4,64,256]{2,1,0:T(8,128)(2,1)S(1)}, bf16[4,64,256]{2,1,0:T(8,128)(2,1)S(1)}, u32[]{:S(2)}, u32[]{:S(2)}) %collective-permute-start.9) | collective-permute-done | bytes 131104 | tf_op jit(solution)/shard_map/ppermute | solution.py:41
  143.8 1.1 sum_parts.3
  144.9 2.1 collective-permute-start.11
  146.9 5.2 %collective-permute-start.12 = (bf16[4,64,256]{2,1,0:T(8,128)(2,1)S(1)}, bf16[4,64,256]{2,1,0:T(8,128)(2,1)S(1)}, u32[]{:S(2)}, u32[]{:S(2)}) collective-permute-start(bf16[4,64,256]{2,1,0:T(8,128)(2,1)S(1)} %get-tuple-element.25), channel_id=1, source_target_pairs={{0,227},{4,231},{8,235},{12,239},{16,243},{20,247},{24,251},{28,25... | collective-permute-start | bytes 393224 | tf_op jit(solution)/shard_map/ppermute | solution.py:41
  152.1 1.9 collective-permute-start.13
  154.0 0.1 collective-permute-done.11
  154.1 0.7 collective-permute-done.12
  154.7 4.2 %collective-permute-done.13 = bf16[4,64,256]{2,1,0:T(8,128)(2,1)S(1)} collective-permute-done((bf16[4,64,256]{2,1,0:T(8,128)(2,1)S(1)}, bf16[4,64,256]{2,1,0:T(8,128)(2,1)S(1)}, u32[]{:S(2)}, u32[]{:S(2)}) %collective-permute-start.13) | collective-permute-done | bytes 131104 | tf_op jit(solution)/shard_map/ppermute | solution.py:41
  159.0 0.1 add_convert_fusion
  159.0 51.3 %all_to_all.38 = bf16[16,16,256]{2,1,0:T(8,128)(2,1)S(1)} all-to-all(bf16[16,16,256]{2,1,0:T(8,128)(2,1)S(1)} %bitcast.26), channel_id=1, replica_groups=mesh['x'=4,'zl'=8,'c'=2,'y'=4,'zh'=4] {'y','zh'}, dimensions={0} | all-to-all | bytes 262144 | tf_op jit(solution)/shard_map/all_to_all | solution.py:241
  210.4 0.6 copy.21
  211.0 0.6 copy.20
  (20 shorter events, 0.2 us)
Async XLA Ops:
  0.6 31.6 %copy-start = (s32[4,4,16]{2,1,0:T(4,128)S(1)}, s32[4,4,16]{2,1,0:T(4,128)}, u32[]{:S(2)}) copy-start(s32[4,4,16]{2,1,0:T(4,128)} %param.9) | copy-start | bytes 3076
  2.0 39.2 %collective-permute-start.6 = (bf16[4,64,256]{2,1,0:T(8,128)(2,1)S(1)}, bf16[4,64,256]{2,1,0:T(8,128)(2,1)S(1)}, u32[]{:S(2)}, u32[]{:S(2)}) collective-permute-start(bf16[4,64,256]{2,1,0:T(8,128)(2,1)S(1)} %pad_maximum_fusion.refs_0_.own_ref), channel_id=1, source_target_pairs={{0,131},{4,135},{8,139},{12,143},{16,147},{20,151},{24,155},{28,15... | collective-permute-start | bytes 393224 | tf_op jit(solution)/shard_map/ppermute | solution.py:41
  21.1 20.1 %collective-permute-start.5 = (bf16[4,64,256]{2,1,0:T(8,128)(2,1)S(1)}, bf16[4,64,256]{2,1,0:T(8,128)(2,1)S(1)}, u32[]{:S(2)}, u32[]{:S(2)}) collective-permute-start(bf16[4,64,256]{2,1,0:T(8,128)(2,1)S(1)} %pad_maximum_fusion.refs_0_.own_ref), channel_id=1, source_target_pairs={{0,96},{4,100},{8,104},{12,108},{16,112},{20,116},{24,120},{28,124... | collective-permute-start | bytes 393224 | tf_op jit(solution)/shard_map/ppermute | solution.py:41
  23.1 18.2 %collective-permute-start.4 = (bf16[4,64,256]{2,1,0:T(8,128)(2,1)S(1)}, bf16[4,64,256]{2,1,0:T(8,128)(2,1)S(1)}, u32[]{:S(2)}, u32[]{:S(2)}) collective-permute-start(bf16[4,64,256]{2,1,0:T(8,128)(2,1)S(1)} %pad_maximum_fusion.refs_0_.own_ref), channel_id=1, source_target_pairs={{0,163},{4,167},{8,171},{12,175},{16,179},{20,183},{24,187},{28,19... | collective-permute-start | bytes 393224 | tf_op jit(solution)/shard_map/ppermute | solution.py:41
  30.0 11.9 %collective-permute-start.3 = (bf16[4,64,256]{2,1,0:T(8,128)(2,1)S(1)}, bf16[4,64,256]{2,1,0:T(8,128)(2,1)S(1)}, u32[]{:S(2)}, u32[]{:S(2)}) collective-permute-start(bf16[4,64,256]{2,1,0:T(8,128)(2,1)S(1)} %pad_maximum_fusion.refs_0_.own_ref), channel_id=1, source_target_pairs={{0,64},{4,68},{8,72},{12,76},{16,80},{20,84},{24,88},{28,92},{32,9... | collective-permute-start | bytes 393224 | tf_op jit(solution)/shard_map/ppermute | solution.py:41
  43.5 20.8 %all-to-all-start.2 = ((bf16[8,4,64,256]{3,2,1,0:T(8,128)(2,1)}), bf16[8,4,64,256]{3,2,1,0:T(8,128)(2,1)S(1)}, u32[]{:S(2)}, u32[]{:S(2)}) async-start(bf16[8,4,64,256]{3,2,1,0:T(8,128)(2,1)} %pick_blocks.3), calls=%async_computation.2 | async-start | bytes 2097152 | tf_op jit(solution)/shard_map/all_to_all | solution.py:217
  48.3 11.4 %collective-permute-start.2 = (bf16[4,64,256]{2,1,0:T(8,128)(2,1)S(1)}, bf16[4,64,256]{2,1,0:T(8,128)(2,1)S(1)}, u32[]{:S(2)}, u32[]{:S(2)}) collective-permute-start(bf16[4,64,256]{2,1,0:T(8,128)(2,1)S(1)} %pad_maximum_fusion.refs_0_.own_ref), channel_id=1, source_target_pairs={{0,195},{4,199},{8,203},{12,207},{16,211},{20,215},{24,219},{28,22... | collective-permute-start | bytes 393224 | tf_op jit(solution)/shard_map/ppermute | solution.py:41
  53.6 7.2 %collective-permute-start.1 = (bf16[4,64,256]{2,1,0:T(8,128)(2,1)S(1)}, bf16[4,64,256]{2,1,0:T(8,128)(2,1)S(1)}, u32[]{:S(2)}, u32[]{:S(2)}) collective-permute-start(bf16[4,64,256]{2,1,0:T(8,128)(2,1)S(1)} %pad_maximum_fusion.refs_0_.own_ref), channel_id=1, source_target_pairs={{0,32},{4,36},{8,40},{12,44},{16,48},{20,52},{24,56},{28,60},{32,6... | collective-permute-start | bytes 393224 | tf_op jit(solution)/shard_map/ppermute | solution.py:41
  55.5 7.2 %collective-permute-start = (bf16[4,64,256]{2,1,0:T(8,128)(2,1)S(1)}, bf16[4,64,256]{2,1,0:T(8,128)(2,1)S(1)}, u32[]{:S(2)}, u32[]{:S(2)}) collective-permute-start(bf16[4,64,256]{2,1,0:T(8,128)(2,1)S(1)} %pad_maximum_fusion.refs_0_.own_ref), channel_id=1, source_target_pairs={{0,227},{4,231},{8,235},{12,239},{16,243},{20,247},{24,251},{28,25... | collective-permute-start | bytes 393224 | tf_op jit(solution)/shard_map/ppermute | solution.py:41
  64.4 19.5 %copy-start.1 = (bf16[256,4,128]{2,1,0:T(4,128)(2,1)S(1)}, bf16[256,4,128]{2,1,0:T(4,128)(2,1)}, u32[]{:S(2)}) copy-start(bf16[256,4,128]{2,1,0:T(4,128)(2,1)} %param.5) | copy-start | bytes 786436
  64.4 19.5 %copy-start.2 = (bf16[256,4,128]{2,1,0:T(4,128)(2,1)S(1)}, bf16[256,4,128]{2,1,0:T(4,128)(2,1)}, u32[]{:S(2)}) copy-start(bf16[256,4,128]{2,1,0:T(4,128)(2,1)} %param.8) | copy-start | bytes 786436
  64.4 19.5 %all-to-all-start.1 = ((bf16[8,4,64,256]{3,2,1,0:T(8,128)(2,1)}), bf16[8,4,64,256]{3,2,1,0:T(8,128)(2,1)S(1)}, u32[]{:S(2)}, u32[]{:S(2)}) async-start(bf16[8,4,64,256]{3,2,1,0:T(8,128)(2,1)} %pick_blocks.2), calls=%async_computation.1 | async-start | bytes 2097152 | tf_op jit(solution)/shard_map/all_to_all | solution.py:217
  112.0 24.1 %all-to-all-start.3 = ((bf16[8,4,64,256]{3,2,1,0:T(8,128)(2,1)}), bf16[8,4,64,256]{3,2,1,0:T(8,128)(2,1)S(1)}, u32[]{:S(2)}, u32[]{:S(2)}) async-start(bf16[8,4,64,256]{3,2,1,0:T(8,128)(2,1)} %bitcast.10), calls=%async_computation.3 | async-start | bytes 2097152 | tf_op jit(solution)/shard_map/all_to_all | solution.py:231
  117.9 18.2 %collective-permute-start.7 = (bf16[4,64,256]{2,1,0:T(8,128)(2,1)S(1)}, bf16[4,64,256]{2,1,0:T(8,128)(2,1)S(1)}, u32[]{:S(2)}, u32[]{:S(2)}) collective-permute-start(bf16[4,64,256]{2,1,0:T(8,128)(2,1)S(1)} %get-tuple-element.19), channel_id=1, source_target_pairs={{0,128},{4,132},{8,136},{12,140},{16,144},{20,148},{24,152},{28,15... | collective-permute-start | bytes 393224 | tf_op jit(solution)/shard_map/ppermute | solution.py:41
  120.3 15.9 %collective-permute-start.8 = (bf16[4,64,256]{2,1,0:T(8,128)(2,1)S(1)}, bf16[4,64,256]{2,1,0:T(8,128)(2,1)S(1)}, u32[]{:S(2)}, u32[]{:S(2)}) collective-permute-start(bf16[4,64,256]{2,1,0:T(8,128)(2,1)S(1)} %get-tuple-element.20), channel_id=1, source_target_pairs={{0,163},{4,167},{8,171},{12,175},{16,179},{20,183},{24,187},{28,19... | collective-permute-start | bytes 393224 | tf_op jit(solution)/shard_map/ppermute | solution.py:41
  126.4 17.4 %collective-permute-start.9 = (bf16[4,64,256]{2,1,0:T(8,128)(2,1)S(1)}, bf16[4,64,256]{2,1,0:T(8,128)(2,1)S(1)}, u32[]{:S(2)}, u32[]{:S(2)}) collective-permute-start(bf16[4,64,256]{2,1,0:T(8,128)(2,1)S(1)} %get-tuple-element.21), channel_id=1, source_target_pairs={{0,96},{4,100},{8,104},{12,108},{16,112},{20,116},{24,120},{28,124... | collective-permute-start | bytes 393224 | tf_op jit(solution)/shard_map/ppermute | solution.py:41
  129.2 14.6 %collective-permute-start.10 = (bf16[4,64,256]{2,1,0:T(8,128)(2,1)S(1)}, bf16[4,64,256]{2,1,0:T(8,128)(2,1)S(1)}, u32[]{:S(2)}, u32[]{:S(2)}) collective-permute-start(bf16[4,64,256]{2,1,0:T(8,128)(2,1)S(1)} %get-tuple-element.22), channel_id=1, source_target_pairs={{0,195},{4,199},{8,203},{12,207},{16,211},{20,215},{24,219},{28,22... | collective-permute-start | bytes 393224 | tf_op jit(solution)/shard_map/ppermute | solution.py:41
  144.9 9.2 %collective-permute-start.11 = (bf16[4,64,256]{2,1,0:T(8,128)(2,1)S(1)}, bf16[4,64,256]{2,1,0:T(8,128)(2,1)S(1)}, u32[]{:S(2)}, u32[]{:S(2)}) collective-permute-start(bf16[4,64,256]{2,1,0:T(8,128)(2,1)S(1)} %get-tuple-element.24), channel_id=1, source_target_pairs={{0,64},{4,68},{8,72},{12,76},{16,80},{20,84},{24,88},{28,92},{32,9... | collective-permute-start | bytes 393224 | tf_op jit(solution)/shard_map/ppermute | solution.py:41
  146.9 7.8 %collective-permute-start.12 = (bf16[4,64,256]{2,1,0:T(8,128)(2,1)S(1)}, bf16[4,64,256]{2,1,0:T(8,128)(2,1)S(1)}, u32[]{:S(2)}, u32[]{:S(2)}) collective-permute-start(bf16[4,64,256]{2,1,0:T(8,128)(2,1)S(1)} %get-tuple-element.25), channel_id=1, source_target_pairs={{0,227},{4,231},{8,235},{12,239},{16,243},{20,247},{24,251},{28,25... | collective-permute-start | bytes 393224 | tf_op jit(solution)/shard_map/ppermute | solution.py:41
  152.1 6.9 %collective-permute-start.13 = (bf16[4,64,256]{2,1,0:T(8,128)(2,1)S(1)}, bf16[4,64,256]{2,1,0:T(8,128)(2,1)S(1)}, u32[]{:S(2)}, u32[]{:S(2)}) collective-permute-start(bf16[4,64,256]{2,1,0:T(8,128)(2,1)S(1)} %get-tuple-element.26), channel_id=1, source_target_pairs={{0,32},{4,36},{8,40},{12,44},{16,48},{20,52},{24,56},{28,60},{32,6... | collective-permute-start | bytes 393224 | tf_op jit(solution)/shard_map/ppermute | solution.py:41

commit v6 on v5

--- a/solution.py
+++ b/solution.py
@@ -18,7 +18,7 @@
 HEAD = ("y", "zh")
 XC = ("x", "c")
 AXES = SEQ + HEAD
-AWAY = [(p + 1) // 2 if p % 2 else -(p // 2) for p in range(ZL)]
+AWAY = [-(p + 1) // 2 if p % 2 else p // 2 for p in range(ZL)]
 PARTS = 2
 PER = ZL // PARTS
 
@@ -157,20 +157,20 @@
 
 
 def sum_body(part, want_ref, in_ref, *refs):
-    home_refs, out_refs, sum_ref = refs[: -1 - PER], refs[-1 - PER : -1], refs[-1]
+    carried_refs, out_refs, sum_ref = list(refs[: -1 - PER]), refs[-1 - PER : -1], refs[-1]
+    carried_at = [0, PER - 2, PER - 1] if carried_refs else []
     for place, out_ref in enumerate(out_refs):
         sum_ref[...] = jnp.zeros_like(sum_ref)
         for peer in range(NX * NC):
             slot = jnp.maximum(want_ref[peer, part * PER + place], 0)
             sum_ref[slot] += in_ref[peer, place].astype(F32)
         total = sum_ref[...]
-        if place == 0:
-            for home_ref in home_refs:
-                total += home_ref[...].astype(F32)
+        if place in carried_at:
+            total += carried_refs[carried_at.index(place)][...].astype(F32)
         out_ref[...] = total.astype(out_ref.dtype)
 
 
-def sum_parts(part, want, parts, blocks, home):
+def sum_parts(part, want, parts, blocks, carried):
     peers, runs, rows, width = parts.shape
     shape = (blocks, rows, width)
     return pl.pallas_call(
@@ -179,14 +179,18 @@
             num_scalar_prefetch=1,
             grid=(1,),
             in_specs=[pl.BlockSpec(parts.shape, lambda k, w: (0, 0, 0, 0))]
-            + [pl.BlockSpec(shape, lambda k, w: (0, 0, 0))] * len(home),
+            + [pl.BlockSpec(shape, lambda k, w: (0, 0, 0))] * len(carried),
             out_specs=[pl.BlockSpec(shape, lambda k, w: (0, 0, 0))] * PER,
             scratch_shapes=[pltpu.VMEM(shape, F32)],
         ),
-        out_shape=[jax.ShapeDtypeStruct(shape, BF16 if place or not home else F32) for place in range(PER)],
+        out_shape=[jax.ShapeDtypeStruct(shape, BF16 if place or not carried else F32) for place in range(PER)],
         compiler_params=pltpu.CompilerParams(vmem_limit_bytes=32 * 2**20),
         name="sum_parts",
-    )(want, parts, *home)
+    )(want, parts, *carried)
+
+
+def plus(a, b):
+    return (a.astype(F32) + b.astype(F32)).astype(BF16)
 
 
 def on_device(queries, key_states, values, grad_out, picked_blocks):
@@ -202,7 +206,7 @@
     live = picks >= 0
     run = picks // blocks
     ahead = lax.rem(run // NC % ZL - home + ZL, ZL)
-    place = jnp.where(ahead <= ZL // 2, jnp.maximum(2 * ahead - 1, 0), 2 * (ZL - ahead))
+    place = jnp.where(ahead < ZL // 2, 2 * ahead, 2 * (ZL - ahead) - 1)
     peer = run // (ZL * NC) * NC + run % NC
     key = jnp.where(live, peer * ZL + place, -1)
     match = key[:, 1:, None] == jnp.arange(NX * ZL * NC, dtype=jnp.int32)
@@ -210,9 +214,11 @@
     wanted = wanted.reshape(NX * NC, ZL)
     asked = lax.all_to_all(wanted, XC, split_axis=0, concat_axis=0, tiled=True)
 
-    near = [own] + [send(own, -away) for away in AWAY[1:]]
+    near = [own]
+    for away in AWAY[1:]:
+        near.append(send(near[max(len(near) - 2, 0)], 1 if away < 0 else -1))
     got = [None] * PARTS
-    for part in reversed(range(PARTS)):
+    for part in range(PARTS):
         sent = pick_blocks(part, asked, near)
         arrived = lax.all_to_all(sent, XC, split_axis=0, concat_axis=0, tiled=True)
         got[part] = arrived.reshape(NX * NC * PER, BLK, 2 * width)
@@ -225,17 +231,17 @@
     )
     grad_queries = dq.reshape(tokens, heads, width)
 
-    arrived = [own_grads]
-    for part in reversed(range(PARTS)):
+    def returned(part, carried):
         parts = back[part].reshape(NX * NC, PER, BLK, 2 * width)
         parts = lax.all_to_all(parts, XC, split_axis=0, concat_axis=0, tiled=True)
-        sums = sum_parts(part, asked, parts, blocks, [] if part else arrived)
-        if part == 0:
-            arrived = [sums[0]]
-        for away, held in zip(reversed(AWAY[part * PER : (part + 1) * PER]), reversed(sums)):
-            if away:
-                arrived.append(send(held, away))
-    total = sum(held.astype(F32) for held in arrived)
+        return sum_parts(part, asked, parts, blocks, carried)
+
+    up2, down3, up3, down4 = returned(1, [])
+    down = send(plus(send(down4, -1), down3), -1)
+    up = send(plus(send(up3, 1), up2), 1)
+    total, down1, up1, down2 = returned(0, [own_grads, up, down])
+    down = send(plus(send(down2, -1), down1), -1)
+    total = total + down.astype(F32) + send(up1, 1).astype(F32)
 
     pieces = total.astype(BF16).reshape(NY * ZH, tokens // (NY * ZH), 2 * width)
     pieces = lax.all_to_all(pieces, HEAD, split_axis=0, concat_axis=0, tiled=True)

time: 212 us -> 199 us (0.939)
  the two profiles are of different devices: /device:TPU:34 before, /device:TPU:32 now
where the time goes in v6:
time: 199 us; the launch traced here: 198 us
  starting transfers between devices  73.9 us (37%)
  blocking collectives  72.4 us (36%)
  waiting for transfers between devices  32.6 us (16%)
  Pallas kernels  14.8 us (7%)
  local copies, waits for them, and re-layouts  3.11 us (2%)
    ppermute x14, starting transfers between devices, send(): return lax.ppermute(array, AXES, pairs)  62.1 us
    all_to_all x1, blocking collectives, on_device(): lax.all_to_all(pieces, HEAD, split_axis=0, concat_axis=0, tiled=True)  46.3 us
    all_to_all x1, blocking collectives, returned(): parts = lax.all_to_all(parts, XC, split_axis=0, concat_axis=0, tiled=True)  18.5 us
    ppermute x14, waiting for transfers between devices, send(): return lax.ppermute(array, AXES, pairs)  16.7 us
    all_to_all x2, waiting for transfers between devices, on_device(): arrived = lax.all_to_all(sent, XC, split_axis=0, concat_axis=0, tiled=True)  15.9 us
    pallas_call x1, Pallas kernels, attend_grads(): pl.pallas_call(attend_body, grid_spec=pltpu.PrefetchScalarGridSpec(num_sc...  9.58 us
    all_to_all x2, starting transfers between devices, on_device(): arrived = lax.all_to_all(sent, XC, split_axis=0, concat_axis=0, tiled=True)  8.29 us
    all_to_all x1, blocking collectives, on_device(): asked = lax.all_to_all(wanted, XC, split_axis=0, concat_axis=0, tiled=True)  7.62 us
  transfers between devices with their start and end apart: 17, of which 12 were waited for; matrix products, arithmetic and copies ran while one was open for 0% of the time, Pallas kernels for 1%

profile of v6, /device:TPU:32, one launch (start us, length us, event | category | flops | bytes accessed | tf_op | source)
XLA Modules:
  0.0 198.2 jit_solution(18233489894622272352)
XLA Ops:
  0.7 1.3 constant_dynamic-slice_fusion
  2.0 3.8 %collective-permute-start = (bf16[4,64,256]{2,1,0:T(8,128)(2,1)S(1)}, bf16[4,64,256]{2,1,0:T(8,128)(2,1)S(1)}, u32[]{:S(2)}, u32[]{:S(2)}) collective-permute-start(bf16[4,64,256]{2,1,0:T(8,128)(2,1)S(1)} %pad_maximum_fusion.refs_0_.own_ref), channel_id=1, source_target_pairs={{0,32},{4,36},{8,40},{12,44},{16,48},{20,52},{24,56},{28,60},{32,6... | collective-permute-start | bytes 393224 | tf_op jit(solution)/shard_map/ppermute | solution.py:41
  5.9 12.8 %collective-permute-start.1 = (bf16[4,64,256]{2,1,0:T(8,128)(2,1)S(1)}, bf16[4,64,256]{2,1,0:T(8,128)(2,1)S(1)}, u32[]{:S(2)}, u32[]{:S(2)}) collective-permute-start(bf16[4,64,256]{2,1,0:T(8,128)(2,1)S(1)} %pad_maximum_fusion.refs_0_.own_ref), channel_id=1, source_target_pairs={{0,227},{4,231},{8,235},{12,239},{16,243},{20,247},{24,251},{28,25... | collective-permute-start | bytes 393224 | tf_op jit(solution)/shard_map/ppermute | solution.py:41
  18.7 1.0 collective-permute-done.refs_1_
  19.6 1.9 collective-permute-start.2
  21.6 0.1 slice.12
  21.7 0.1 slice.13
  21.7 0.1 copy.18
  21.8 0.1 copy.17
  21.9 0.1 select_reduce_fusion
  22.0 0.1 all_to_all.22
  22.1 7.6 %all_to_all.36 = s32[8,1,8]{2,1,0:T(1,128)S(1)} all-to-all(s32[8,1,8]{2,1,0:T(1,128)S(1)} %bitcast.30), channel_id=1, replica_groups=mesh['x'=4,'zl'=8,'c'=2,'y'=4,'zh'=4] {'x','c'}, dimensions={0} | all-to-all | bytes 512 | tf_op jit(solution)/shard_map/all_to_all | solution.py:215
  29.7 1.7 pick_blocks.2
  31.4 3.7 %all-to-all-start.1 = ((bf16[8,4,64,256]{3,2,1,0:T(8,128)(2,1)}), bf16[8,4,64,256]{3,2,1,0:T(8,128)(2,1)S(1)}, u32[]{:S(2)}, u32[]{:S(2)}) async-start(bf16[8,4,64,256]{3,2,1,0:T(8,128)(2,1)} %pick_blocks.2), calls=%async_computation.1 | async-start | bytes 2097152 | tf_op jit(solution)/shard_map/all_to_all | solution.py:223
  35.1 8.2 %collective-permute-start.3 = (bf16[4,64,256]{2,1,0:T(8,128)(2,1)S(1)}, bf16[4,64,256]{2,1,0:T(8,128)(2,1)S(1)}, u32[]{:S(2)}, u32[]{:S(2)}) collective-permute-start(bf16[4,64,256]{2,1,0:T(8,128)(2,1)S(1)} %collective-permute-done.1.refs_2_), channel_id=1, source_target_pairs={{0,227},{4,231},{8,235},{12,239},{16,243},{20,247},{24,251},{28,25... | collective-permute-start | bytes 393224 | tf_op jit(solution)/shard_map/ppermute | solution.py:41
  43.3 1.9 collective-permute-start.4
  45.3 1.3 collective-permute-done.3.refs_0_
  46.6 5.1 %collective-permute-start.5 = (bf16[4,64,256]{2,1,0:T(8,128)(2,1)S(1)}, bf16[4,64,256]{2,1,0:T(8,128)(2,1)S(1)}, u32[]{:S(2)}, u32[]{:S(2)}) collective-permute-start(bf16[4,64,256]{2,1,0:T(8,128)(2,1)S(1)} %collective-permute-done.3.refs_0_), channel_id=1, source_target_pairs={{0,227},{4,231},{8,235},{12,239},{16,243},{20,247},{24,251},{28,25... | collective-permute-start | bytes 393224 | tf_op jit(solution)/shard_map/ppermute | solution.py:41
  51.7 0.5 collective-permute-done.4.refs_1_
  52.2 1.9 collective-permute-start.6
  54.1 0.1 collective-permute-done.5.refs_2_
  54.2 6.1 %collective-permute-done.6.refs_3_ = bf16[4,64,256]{2,1,0:T(8,128)(2,1)S(1)} collective-permute-done((bf16[4,64,256]{2,1,0:T(8,128)(2,1)S(1)}, bf16[4,64,256]{2,1,0:T(8,128)(2,1)S(1)}, u32[]{:S(2)}, u32[]{:S(2)}) %collective-permute-start.6) | collective-permute-done | bytes 131104 | tf_op jit(solution)/shard_map/ppermute | solution.py:41
  60.3 1.6 pick_blocks.3
  61.9 4.6 %all-to-all-start.2 = ((bf16[8,4,64,256]{3,2,1,0:T(8,128)(2,1)}), bf16[8,4,64,256]{3,2,1,0:T(8,128)(2,1)S(1)}, u32[]{:S(2)}, u32[]{:S(2)}) async-start(bf16[8,4,64,256]{3,2,1,0:T(8,128)(2,1)} %pick_blocks.3), calls=%async_computation.2 | async-start | bytes 2097152 | tf_op jit(solution)/shard_map/all_to_all | solution.py:223
  66.5 15.9 %all-to-all-done.2 = bf16[8,4,64,256]{3,2,1,0:T(8,128)(2,1)S(1)} async-done(((bf16[8,4,64,256]{3,2,1,0:T(8,128)(2,1)}), bf16[8,4,64,256]{3,2,1,0:T(8,128)(2,1)S(1)}, u32[]{:S(2)}, u32[]{:S(2)}) %all-to-all-start.2) | async-done | bytes 1048608 | tf_op jit(solution)/shard_map/all_to_all | solution.py:223
  82.5 0.1 broadcast_in_dim.34.bias_ref
  82.6 9.6 %attend_grads.1 = (f32[1024,128]{1,0:T(8,128)}, f32[4,64,256]{2,1,0:T(8,128)S(1)}, bf16[32,64,256]{2,1,0:T(8,128)(2,1)}, bf16[32,64,256]{2,1,0:T(8,128)(2,1)S(1)}) custom-call(s32[4,16]{1,0:T(4,128)S(1)} %fusion.8.slot_ref, bf16[1024,128]{1,0:T(8,128)(2,1)S(1)} %bitcast.20, bf16[1024,128]{1,0:T(8,128)(2,1)S(1)} %bitcast.21, ...), custom_call_target="tpu_custom_call" | custom-call | tf_op jit(solution)/shard_map/attend_grads/pallas_call | solution.py:114
  92.2 18.5 %all_to_all.37.in_ref = bf16[8,4,64,256]{3,2,1,0:T(8,128)(2,1)S(1)} all-to-all(bf16[8,4,64,256]{3,2,1,0:T(8,128)(2,1)S(1)} %bitcast.19), channel_id=1, replica_groups=mesh['x'=4,'zl'=8,'c'=2,'y'=4,'zh'=4] {'x','c'}, dimensions={0} | all-to-all | bytes 2097152 | tf_op jit(solution)/shard_map/all_to_all | solution.py:236
  110.7 3.6 %all-to-all-start.3 = ((bf16[8,4,64,256]{3,2,1,0:T(8,128)(2,1)}), bf16[8,4,64,256]{3,2,1,0:T(8,128)(2,1)S(1)}, u32[]{:S(2)}, u32[]{:S(2)}) async-start(bf16[8,4,64,256]{3,2,1,0:T(8,128)(2,1)} %bitcast.10), calls=%async_computation.3 | async-start | bytes 2097152 | tf_op jit(solution)/shard_map/all_to_all | solution.py:236
  114.2 1.0 sum_parts.2
  115.2 1.9 collective-permute-start.7
  117.1 5.1 %collective-permute-start.9 = (bf16[4,64,256]{2,1,0:T(8,128)(2,1)S(1)}, bf16[4,64,256]{2,1,0:T(8,128)(2,1)S(1)}, u32[]{:S(2)}, u32[]{:S(2)}) collective-permute-start(bf16[4,64,256]{2,1,0:T(8,128)(2,1)S(1)} %get-tuple-element.21), channel_id=1, source_target_pairs={{0,227},{4,231},{8,235},{12,239},{16,243},{20,247},{24,251},{28,25... | collective-permute-start | bytes 393224 | tf_op jit(solution)/shard_map/ppermute | solution.py:41
  122.2 2.1 %collective-permute-done.7 = bf16[4,64,256]{2,1,0:T(8,128)(2,1)S(1)} collective-permute-done((bf16[4,64,256]{2,1,0:T(8,128)(2,1)S(1)}, bf16[4,64,256]{2,1,0:T(8,128)(2,1)S(1)}, u32[]{:S(2)}, u32[]{:S(2)}) %collective-permute-start.7) | collective-permute-done | bytes 131104 | tf_op jit(solution)/shard_map/ppermute | solution.py:41
  124.4 1.9 collective-permute-start.8
  126.4 4.9 %collective-permute-start.10 = (bf16[4,64,256]{2,1,0:T(8,128)(2,1)S(1)}, bf16[4,64,256]{2,1,0:T(8,128)(2,1)S(1)}, u32[]{:S(2)}, u32[]{:S(2)}) collective-permute-start(bf16[4,64,256]{2,1,0:T(8,128)(2,1)S(1)} %add_convert_fusion.2), channel_id=1, source_target_pairs={{0,227},{4,231},{8,235},{12,239},{16,243},{20,247},{24,251},{28,25... | collective-permute-start | bytes 393224 | tf_op jit(solution)/shard_map/ppermute | solution.py:41
  131.3 1.3 collective-permute-done.8.refs_1_
  132.6 1.2 collective-permute-done.10.refs_2_
  133.8 1.0 sum_parts.3
  134.8 5.1 %collective-permute-start.11 = (bf16[4,64,256]{2,1,0:T(8,128)(2,1)S(1)}, bf16[4,64,256]{2,1,0:T(8,128)(2,1)S(1)}, u32[]{:S(2)}, u32[]{:S(2)}) collective-permute-start(bf16[4,64,256]{2,1,0:T(8,128)(2,1)S(1)} %get-tuple-element.24), channel_id=1, source_target_pairs={{0,227},{4,231},{8,235},{12,239},{16,243},{20,247},{24,251},{28,25... | collective-permute-start | bytes 393224 | tf_op jit(solution)/shard_map/ppermute | solution.py:41
  139.9 1.9 collective-permute-start.13
  141.8 0.6 collective-permute-done.11
  142.4 5.6 %collective-permute-start.12 = (bf16[4,64,256]{2,1,0:T(8,128)(2,1)S(1)}, bf16[4,64,256]{2,1,0:T(8,128)(2,1)S(1)}, u32[]{:S(2)}, u32[]{:S(2)}) collective-permute-start(bf16[4,64,256]{2,1,0:T(8,128)(2,1)S(1)} %add_convert_fusion.1), channel_id=1, source_target_pairs={{0,227},{4,231},{8,235},{12,239},{16,243},{20,247},{24,251},{28,25... | collective-permute-start | bytes 393224 | tf_op jit(solution)/shard_map/ppermute | solution.py:41
  148.0 0.4 collective-permute-done.13
  148.4 2.1 %collective-permute-done.12 = bf16[4,64,256]{2,1,0:T(8,128)(2,1)S(1)} collective-permute-done((bf16[4,64,256]{2,1,0:T(8,128)(2,1)S(1)}, bf16[4,64,256]{2,1,0:T(8,128)(2,1)S(1)}, u32[]{:S(2)}, u32[]{:S(2)}) %collective-permute-start.12) | collective-permute-done | bytes 131104 | tf_op jit(solution)/shard_map/ppermute | solution.py:41
  150.5 0.1 add_convert_fusion
  150.6 46.3 %all_to_all.38 = bf16[16,16,256]{2,1,0:T(8,128)(2,1)S(1)} all-to-all(bf16[16,16,256]{2,1,0:T(8,128)(2,1)S(1)} %bitcast.26), channel_id=1, replica_groups=mesh['x'=4,'zl'=8,'c'=2,'y'=4,'zh'=4] {'y','zh'}, dimensions={0} | all-to-all | bytes 262144 | tf_op jit(solution)/shard_map/all_to_all | solution.py:247
  196.9 0.6 copy.21
  197.5 0.6 copy.20
  (23 shorter events, 0.3 us)
Async XLA Ops:
  0.6 18.0 %copy-start = (s32[4,4,16]{2,1,0:T(4,128)S(1)}, s32[4,4,16]{2,1,0:T(4,128)}, u32[]{:S(2)}) copy-start(s32[4,4,16]{2,1,0:T(4,128)} %param.9) | copy-start | bytes 3076
  2.0 17.6 %collective-permute-start = (bf16[4,64,256]{2,1,0:T(8,128)(2,1)S(1)}, bf16[4,64,256]{2,1,0:T(8,128)(2,1)S(1)}, u32[]{:S(2)}, u32[]{:S(2)}) collective-permute-start(bf16[4,64,256]{2,1,0:T(8,128)(2,1)S(1)} %pad_maximum_fusion.refs_0_.own_ref), channel_id=1, source_target_pairs={{0,32},{4,36},{8,40},{12,44},{16,48},{20,52},{24,56},{28,60},{32,6... | collective-permute-start | bytes 393224 | tf_op jit(solution)/shard_map/ppermute | solution.py:41
  5.9 23.9 %collective-permute-start.1 = (bf16[4,64,256]{2,1,0:T(8,128)(2,1)S(1)}, bf16[4,64,256]{2,1,0:T(8,128)(2,1)S(1)}, u32[]{:S(2)}, u32[]{:S(2)}) collective-permute-start(bf16[4,64,256]{2,1,0:T(8,128)(2,1)S(1)} %pad_maximum_fusion.refs_0_.own_ref), channel_id=1, source_target_pairs={{0,227},{4,231},{8,235},{12,239},{16,243},{20,247},{24,251},{28,25... | collective-permute-start | bytes 393224 | tf_op jit(solution)/shard_map/ppermute | solution.py:41
  19.6 10.1 %collective-permute-start.2 = (bf16[4,64,256]{2,1,0:T(8,128)(2,1)S(1)}, bf16[4,64,256]{2,1,0:T(8,128)(2,1)S(1)}, u32[]{:S(2)}, u32[]{:S(2)}) collective-permute-start(bf16[4,64,256]{2,1,0:T(8,128)(2,1)S(1)} %collective-permute-done.refs_1_), channel_id=1, source_target_pairs={{0,32},{4,36},{8,40},{12,44},{16,48},{20,52},{24,56},{28,60},{32,6... | collective-permute-start | bytes 393224 | tf_op jit(solution)/shard_map/ppermute | solution.py:41
  31.4 30.5 %all-to-all-start.1 = ((bf16[8,4,64,256]{3,2,1,0:T(8,128)(2,1)}), bf16[8,4,64,256]{3,2,1,0:T(8,128)(2,1)S(1)}, u32[]{:S(2)}, u32[]{:S(2)}) async-start(bf16[8,4,64,256]{3,2,1,0:T(8,128)(2,1)} %pick_blocks.2), calls=%async_computation.1 | async-start | bytes 2097152 | tf_op jit(solution)/shard_map/all_to_all | solution.py:223
  35.1 11.5 %collective-permute-start.3 = (bf16[4,64,256]{2,1,0:T(8,128)(2,1)S(1)}, bf16[4,64,256]{2,1,0:T(8,128)(2,1)S(1)}, u32[]{:S(2)}, u32[]{:S(2)}) collective-permute-start(bf16[4,64,256]{2,1,0:T(8,128)(2,1)S(1)} %collective-permute-done.1.refs_2_), channel_id=1, source_target_pairs={{0,227},{4,231},{8,235},{12,239},{16,243},{20,247},{24,251},{28,25... | collective-permute-start | bytes 393224 | tf_op jit(solution)/shard_map/ppermute | solution.py:41
  43.3 8.9 %collective-permute-start.4 = (bf16[4,64,256]{2,1,0:T(8,128)(2,1)S(1)}, bf16[4,64,256]{2,1,0:T(8,128)(2,1)S(1)}, u32[]{:S(2)}, u32[]{:S(2)}) collective-permute-start(bf16[4,64,256]{2,1,0:T(8,128)(2,1)S(1)} %collective-permute-done.2.refs_3_), channel_id=1, source_target_pairs={{0,32},{4,36},{8,40},{12,44},{16,48},{20,52},{24,56},{28,60},{32,6... | collective-permute-start | bytes 393224 | tf_op jit(solution)/shard_map/ppermute | solution.py:41
  46.6 7.6 %collective-permute-start.5 = (bf16[4,64,256]{2,1,0:T(8,128)(2,1)S(1)}, bf16[4,64,256]{2,1,0:T(8,128)(2,1)S(1)}, u32[]{:S(2)}, u32[]{:S(2)}) collective-permute-start(bf16[4,64,256]{2,1,0:T(8,128)(2,1)S(1)} %collective-permute-done.3.refs_0_), channel_id=1, source_target_pairs={{0,227},{4,231},{8,235},{12,239},{16,243},{20,247},{24,251},{28,25... | collective-permute-start | bytes 393224 | tf_op jit(solution)/shard_map/ppermute | solution.py:41
  52.2 8.1 %collective-permute-start.6 = (bf16[4,64,256]{2,1,0:T(8,128)(2,1)S(1)}, bf16[4,64,256]{2,1,0:T(8,128)(2,1)S(1)}, u32[]{:S(2)}, u32[]{:S(2)}) collective-permute-start(bf16[4,64,256]{2,1,0:T(8,128)(2,1)S(1)} %collective-permute-done.4.refs_1_), channel_id=1, source_target_pairs={{0,32},{4,36},{8,40},{12,44},{16,48},{20,52},{24,56},{28,60},{32,6... | collective-permute-start | bytes 393224 | tf_op jit(solution)/shard_map/ppermute | solution.py:41
  61.9 20.6 %copy-start.1 = (bf16[256,4,128]{2,1,0:T(4,128)(2,1)S(1)}, bf16[256,4,128]{2,1,0:T(4,128)(2,1)}, u32[]{:S(2)}) copy-start(bf16[256,4,128]{2,1,0:T(4,128)(2,1)} %param.5) | copy-start | bytes 786436
  61.9 20.6 %copy-start.2 = (bf16[256,4,128]{2,1,0:T(4,128)(2,1)S(1)}, bf16[256,4,128]{2,1,0:T(4,128)(2,1)}, u32[]{:S(2)}) copy-start(bf16[256,4,128]{2,1,0:T(4,128)(2,1)} %param.8) | copy-start | bytes 786436
  61.9 20.6 %all-to-all-start.2 = ((bf16[8,4,64,256]{3,2,1,0:T(8,128)(2,1)}), bf16[8,4,64,256]{3,2,1,0:T(8,128)(2,1)S(1)}, u32[]{:S(2)}, u32[]{:S(2)}) async-start(bf16[8,4,64,256]{3,2,1,0:T(8,128)(2,1)} %pick_blocks.3), calls=%async_computation.2 | async-start | bytes 2097152 | tf_op jit(solution)/shard_map/all_to_all | solution.py:223
  110.7 20.6 %all-to-all-start.3 = ((bf16[8,4,64,256]{3,2,1,0:T(8,128)(2,1)}), bf16[8,4,64,256]{3,2,1,0:T(8,128)(2,1)S(1)}, u32[]{:S(2)}, u32[]{:S(2)}) async-start(bf16[8,4,64,256]{3,2,1,0:T(8,128)(2,1)} %bitcast.10), calls=%async_computation.3 | async-start | bytes 2097152 | tf_op jit(solution)/shard_map/all_to_all | solution.py:236
  115.2 9.2 %collective-permute-start.7 = (bf16[4,64,256]{2,1,0:T(8,128)(2,1)S(1)}, bf16[4,64,256]{2,1,0:T(8,128)(2,1)S(1)}, u32[]{:S(2)}, u32[]{:S(2)}) collective-permute-start(bf16[4,64,256]{2,1,0:T(8,128)(2,1)S(1)} %get-tuple-element.19), channel_id=1, source_target_pairs={{0,32},{4,36},{8,40},{12,44},{16,48},{20,52},{24,56},{28,60},{32,6... | collective-permute-start | bytes 393224 | tf_op jit(solution)/shard_map/ppermute | solution.py:41
  117.1 9.2 %collective-permute-start.9 = (bf16[4,64,256]{2,1,0:T(8,128)(2,1)S(1)}, bf16[4,64,256]{2,1,0:T(8,128)(2,1)S(1)}, u32[]{:S(2)}, u32[]{:S(2)}) collective-permute-start(bf16[4,64,256]{2,1,0:T(8,128)(2,1)S(1)} %get-tuple-element.21), channel_id=1, source_target_pairs={{0,227},{4,231},{8,235},{12,239},{16,243},{20,247},{24,251},{28,25... | collective-permute-start | bytes 393224 | tf_op jit(solution)/shard_map/ppermute | solution.py:41
  124.4 8.2 %collective-permute-start.8 = (bf16[4,64,256]{2,1,0:T(8,128)(2,1)S(1)}, bf16[4,64,256]{2,1,0:T(8,128)(2,1)S(1)}, u32[]{:S(2)}, u32[]{:S(2)}) collective-permute-start(bf16[4,64,256]{2,1,0:T(8,128)(2,1)S(1)} %add_convert_fusion.3), channel_id=1, source_target_pairs={{0,32},{4,36},{8,40},{12,44},{16,48},{20,52},{24,56},{28,60},{32,6... | collective-permute-start | bytes 393224 | tf_op jit(solution)/shard_map/ppermute | solution.py:41
  126.4 7.4 %collective-permute-start.10 = (bf16[4,64,256]{2,1,0:T(8,128)(2,1)S(1)}, bf16[4,64,256]{2,1,0:T(8,128)(2,1)S(1)}, u32[]{:S(2)}, u32[]{:S(2)}) collective-permute-start(bf16[4,64,256]{2,1,0:T(8,128)(2,1)S(1)} %add_convert_fusion.2), channel_id=1, source_target_pairs={{0,227},{4,231},{8,235},{12,239},{16,243},{20,247},{24,251},{28,25... | collective-permute-start | bytes 393224 | tf_op jit(solution)/shard_map/ppermute | solution.py:41
  134.8 7.6 %collective-permute-start.11 = (bf16[4,64,256]{2,1,0:T(8,128)(2,1)S(1)}, bf16[4,64,256]{2,1,0:T(8,128)(2,1)S(1)}, u32[]{:S(2)}, u32[]{:S(2)}) collective-permute-start(bf16[4,64,256]{2,1,0:T(8,128)(2,1)S(1)} %get-tuple-element.24), channel_id=1, source_target_pairs={{0,227},{4,231},{8,235},{12,239},{16,243},{20,247},{24,251},{28,25... | collective-permute-start | bytes 393224 | tf_op jit(solution)/shard_map/ppermute | solution.py:41
  139.9 8.5 %collective-permute-start.13 = (bf16[4,64,256]{2,1,0:T(8,128)(2,1)S(1)}, bf16[4,64,256]{2,1,0:T(8,128)(2,1)S(1)}, u32[]{:S(2)}, u32[]{:S(2)}) collective-permute-start(bf16[4,64,256]{2,1,0:T(8,128)(2,1)S(1)} %get-tuple-element.26), channel_id=1, source_target_pairs={{0,32},{4,36},{8,40},{12,44},{16,48},{20,52},{24,56},{28,60},{32,6... | collective-permute-start | bytes 393224 | tf_op jit(solution)/shard_map/ppermute | solution.py:41
  142.4 8.1 %collective-permute-start.12 = (bf16[4,64,256]{2,1,0:T(8,128)(2,1)S(1)}, bf16[4,64,256]{2,1,0:T(8,128)(2,1)S(1)}, u32[]{:S(2)}, u32[]{:S(2)}) collective-permute-start(bf16[4,64,256]{2,1,0:T(8,128)(2,1)S(1)} %add_convert_fusion.1), channel_id=1, source_target_pairs={{0,227},{4,231},{8,235},{12,239},{16,243},{20,247},{24,251},{28,25... | collective-permute-start | bytes 393224 | tf_op jit(solution)/shard_map/ppermute | solution.py:41

commit v7 on v6

v7 whole, which is shorter than its diff:
```python
import jax
import jax.numpy as jnp
from jax import lax
from jax.experimental import pallas as pl
from jax.experimental.pallas import tpu as pltpu
from jax.sharding import Mesh
from jax.sharding import PartitionSpec as P

BLK = 64
KSEL = 16
NEG = -1e30

NX, ZS, ZB, NC, NY, ZH = 4, 4, 2, 2, 4, 4
NZ = ZH * ZS * ZB
SEQ = ("x", "zs", "zb", "c")
HEAD = ("y", "zh")
AXES = SEQ + HEAD
SIDE = ("x", "zb", "c")
PEERS = NX * ZB * NC
AWAY = [-(p + 1) // 2 if p % 2 else p // 2 for p in range(ZS)]

F32 = jnp.float32
BF16 = jnp.bfloat16


def number(x, z, c, y):
    run = ZS * ZB
    return (((x * run + z % run) * NC + c) * NY + y) * ZH + z % NZ // run


def send(array, step):
    pairs = [
        (number(x, z, c, y), number(x, z + step * ZB, c, y))
        for x in range(NX)
        for z in range(NZ)
        for c in range(NC)
        for y in range(NY)
    ]
    return lax.ppermute(array, AXES, pairs)


def attend_body(slot_ref, q_ref, g_ref, own_ref, bias_ref, got_ref, dq_ref, down_ref, back_ref, k_ref, v_ref):
    b = pl.program_id(0)
    rows = q_ref.shape[0]
    width = q_ref.shape[1]
    heads = rows // BLK
    factor = width ** (-0.5)

    @pl.when(b == 0)
    def _():
        back_ref[...] = jnp.zeros_like(back_ref)

    k_ref[0:BLK, :] = own_ref[0, :, :width]
    v_ref[0:BLK, :] = own_ref[0, :, width:]
    for j in range(1, KSEL):
        slot = jnp.maximum(slot_ref[b, j], 0)
        k_ref[j * BLK : (j + 1) * BLK, :] = got_ref[slot, :, :width]
        v_ref[j * BLK : (j + 1) * BLK, :] = got_ref[slot, :, width:]
    q = q_ref[...]
    g = g_ref[...]
    k = k_ref[...]
    v = v_ref[...]
    nt = (((1,), (1,)), ((), ()))
    scores = lax.dot_general(k, q, nt, preferred_element_type=F32) * factor
    key_row = lax.broadcasted_iota(jnp.int32, (BLK, rows), 0)
    token = lax.broadcasted_iota(jnp.int32, (BLK, rows), 1) // heads
    own = jnp.where(key_row <= token, scores[:BLK], NEG)
    far = scores[BLK:].reshape(KSEL - 1, BLK, rows) + bias_ref[0, 1:][:, None, :]
    scores = jnp.concatenate([own, far.reshape((KSEL - 1) * BLK, rows)], axis=0)
    weights = jnp.exp(scores - jnp.max(scores, axis=0, keepdims=True))
    attend = weights * (1.0 / jnp.sum(weights, axis=0, keepdims=True))
    grad_prob = lax.dot_general(v, g, nt, preferred_element_type=F32)
    row_dot = jnp.sum(attend * grad_prob, axis=0, keepdims=True)
    dscore = (attend * (grad_prob - row_dot)).astype(BF16)
    tn = (((0,), (0,)), ((), ()))
    nn = (((1,), (0,)), ((), ()))
    dq = lax.dot_general(k, dscore, tn, preferred_element_type=F32) * factor
    dq_ref[...] = dq.T
    dk = lax.dot_general(dscore, q, nn, preferred_element_type=F32) * factor
    dv = lax.dot_general(attend.astype(BF16), g, nn, preferred_element_type=F32)
    down_ref[0, :, :width] = dk[:BLK]
    down_ref[0, :, width:] = dv[:BLK]
    for j in range(1, KSEL):
        slot = slot_ref[b, j]

        @pl.when(slot >= 0)
        def _():
            back_ref[slot, :, :width] = dk[j * BLK : (j + 1) * BLK].astype(BF16)
            back_ref[slot, :, width:] = dv[j * BLK : (j + 1) * BLK].astype(BF16)


def attend_grads(slots, q_rows, g_rows, own, bias, got):
    blocks = slots.shape[0]
    total, width = q_rows.shape
    rows = total // blocks
    row_spec = pl.BlockSpec((rows, width), lambda b, s: (b, 0))
    own_spec = pl.BlockSpec((1, BLK, 2 * width), lambda b, s: (b, 0, 0))
    whole = pl.BlockSpec(got.shape, lambda b, s: (0, 0, 0))
    return pl.pallas_call(
        attend_body,
        grid_spec=pltpu.PrefetchScalarGridSpec(
            num_scalar_prefetch=1,
            grid=(blocks,),
            in_specs=[row_spec, row_spec, own_spec, pl.BlockSpec((1, KSEL, rows), lambda b, s: (b, 0, 0)), whole],
            out_specs=[row_spec, own_spec, whole],
            scratch_shapes=[pltpu.VMEM((KSEL * BLK, width), BF16), pltpu.VMEM((KSEL * BLK, width), BF16)],
        ),
        out_shape=[
            jax.ShapeDtypeStruct((total, width), F32),
            jax.ShapeDtypeStruct((blocks, BLK, 2 * width), F32),
            jax.ShapeDtypeStruct(got.shape, BF16),
        ],
        compiler_params=pltpu.CompilerParams(dimension_semantics=("arbitrary",), vmem_limit_bytes=48 * 2**20),
        name="attend_grads",
    )(slots, q_rows, g_rows, own, bias, got)


def pick_body(want_ref, *refs):
    out_ref = refs[-1]
    for place, near_ref in enumerate(refs[:-1]):
        for peer in range(PEERS):
            slot = want_ref[peer, place]
            out_ref[peer, place] = near_ref[jnp.maximum(slot, 0)]


def pick_blocks(want, near):
    blocks, rows, width = near[0].shape
    shape = (PEERS, ZS, rows, width)
    return pl.pallas_call(
        pick_body,
        grid_spec=pltpu.PrefetchScalarGridSpec(
            num_scalar_prefetch=1,
            grid=(1,),
            in_specs=[pl.BlockSpec((blocks, rows, width), lambda i, w: (0, 0, 0))] * ZS,
            out_specs=pl.BlockSpec(shape, lambda i, w: (0, 0, 0, 0)),
        ),
        out_shape=jax.ShapeDtypeStruct(shape, BF16),
        compiler_params=pltpu.CompilerParams(vmem_limit_bytes=32 * 2**20),
        name="pick_blocks",
    )(want, *near)


def sum_body(want_ref, in_ref, own_ref, *refs):
    out_refs, sum_ref = refs[:-1], refs[-1]
    for place, out_ref in enumerate(out_refs):
        sum_ref[...] = jnp.zeros_like(sum_ref) if place else own_ref[...]
        for peer in range(PEERS):
            slot = jnp.maximum(want_ref[peer, place], 0)
            sum_ref[slot] += in_ref[peer, place].astype(F32)
        out_ref[...] = sum_ref[...].astype(out_ref.dtype)


def sum_parts(want, parts, own_grads):
    shape = own_grads.shape
    spec = pl.BlockSpec(shape, lambda k, w: (0, 0, 0))
    return pl.pallas_call(
        sum_body,
        grid_spec=pltpu.PrefetchScalarGridSpec(
            num_scalar_prefetch=1,
            grid=(1,),
            in_specs=[pl.BlockSpec(parts.shape, lambda k, w: (0, 0, 0, 0)), spec],
            out_specs=[spec] * ZS,
            scratch_shapes=[pltpu.VMEM(shape, F32)],
        ),
        out_shape=[jax.ShapeDtypeStruct(shape, BF16 if place else F32) for place in range(ZS)],
        compiler_params=pltpu.CompilerParams(vmem_limit_bytes=32 * 2**20),
        name="sum_parts",
    )(want, parts, own_grads)


def plus(a, b):
    return (a.astype(F32) + b.astype(F32)).astype(BF16)


def on_device(queries, key_states, values, grad_out, picked_blocks):
    tokens, heads, width = queries.shape
    blocks = tokens // BLK
    group = lax.axis_index("y")
    home = lax.axis_index("zs").astype(jnp.int32)
    own_keys = lax.dynamic_index_in_dim(key_states, group, 1, keepdims=False)
    own_values = lax.dynamic_index_in_dim(values, group, 1, keepdims=False)
    own = jnp.concatenate([own_keys, own_values], axis=1).reshape(blocks, BLK, 2 * width)
    picks = lax.dynamic_index_in_dim(picked_blocks, group, 1, keepdims=False)

    live = picks >= 0
    run = picks // blocks
    ahead = lax.rem(run // (ZB * NC) % ZS - home + ZS, ZS)
    place = jnp.where(ahead < ZS // 2, 2 * ahead, 2 * (ZS - ahead) - 1)
    peer = run // (ZS * ZB * NC) * (ZB * NC) + run % (ZB * NC)
    slots = jnp.where(live, peer * ZS + place, -1)
    match = slots[:, 1:, None] == jnp.arange(PEERS * ZS, dtype=jnp.int32)
    wanted = jnp.max(jnp.where(match, (picks % blocks)[:, 1:, None], -1), axis=(0, 1))
    asked = lax.all_to_all(wanted.reshape(PEERS, ZS), SIDE, split_axis=0, concat_axis=0, tiled=True)

    near = [own]
    for away in AWAY[1:]:
        near.append(send(near[max(len(near) - 2, 0)], 1 if away < 0 else -1))
    got = lax.all_to_all(pick_blocks(asked, near), SIDE, split_axis=0, concat_axis=0, tiled=True)
    got = got.reshape(PEERS * ZS, BLK, 2 * width)
    bias = jnp.where(live, 0.0, NEG).astype(F32)
    bias = jnp.broadcast_to(bias[:, :, None], (blocks, KSEL, BLK * heads))
    dq, own_grads, back = attend_grads(
        slots, queries.reshape(tokens * heads, width), grad_out.reshape(tokens * heads, width), own, bias, got
    )
    grad_queries = dq.reshape(tokens, heads, width)

    parts = lax.all_to_all(back.reshape(PEERS, ZS, BLK, 2 * width), SIDE, split_axis=0, concat_axis=0, tiled=True)
    total, down1, up1, down2 = sum_parts(asked, parts, own_grads)
    down = send(plus(send(down2, -1), down1), -1)
    total = total + down.astype(F32) + send(up1, 1).astype(F32)

    pieces = total.astype(BF16).reshape(NY * ZH, tokens // (NY * ZH), 2 * width)
    pieces = lax.all_to_all(pieces, HEAD, split_axis=0, concat_axis=0, tiled=True)
    summed = pieces.astype(F32).reshape(NY, ZH, tokens // (NY * ZH), 2 * width).sum(axis=1)
    summed = summed.transpose(1, 0, 2)
    return (grad_queries, summed[:, :, :width], summed[:, :, width:])


def solution(mesh):
    torus = Mesh(mesh.devices.reshape(NX, ZS, ZB, NC, NY, ZH), AXES)
    by_head = P(SEQ, HEAD, None)
    by_run = P(SEQ, None, None)
    by_all = P(AXES, None, None)
    return jax.shard_map(
        on_device,
        mesh=torus,
        in_specs=(by_head, by_run, by_run, by_head, by_run),
        out_specs=(by_head, by_all, by_all),
        check_vma=False,
    )
```

time: 199 us -> 185 us (0.930)
  the two profiles are of different devices: /device:TPU:32 before, /device:TPU:34 now
where the time goes in v7:
time: 185 us; the launch traced here: 184 us
  blocking collectives  89.9 us (49%)
  starting transfers between devices  42.5 us (23%)
  waiting for transfers between devices  36.5 us (20%)
  Pallas kernels  11.2 us (6%)
  local copies, waits for them, and re-layouts  3.11 us (2%)
    all_to_all x1, blocking collectives, on_device(): lax.all_to_all(pieces, HEAD, split_axis=0, concat_axis=0, tiled=True)  50.2 us
    ppermute x6, starting transfers between devices, send(): return lax.ppermute(array, AXES, pairs)  36.5 us
    all_to_all x1, blocking collectives, on_device(): lax.all_to_all(back.reshape(PEERS, ZS, BLK, 2 * width), SIDE, split_axis=...  30.4 us
    all_to_all x1, waiting for transfers between devices, on_device(): lax.all_to_all(pick_blocks(asked, near), SIDE, split_axis=0, concat_axis=...  24.7 us
    ppermute x6, waiting for transfers between devices, send(): return lax.ppermute(array, AXES, pairs)  11.9 us
    all_to_all x1, blocking collectives, on_device(): lax.all_to_all(wanted.reshape(PEERS, ZS), SIDE, split_axis=0, concat_axis...  9.34 us
    pallas_call x1, Pallas kernels, attend_grads(): pl.pallas_call(attend_body, grid_spec=pltpu.PrefetchScalarGridSpec(num_sc...  7.8 us
    all_to_all x1, starting transfers between devices, on_device(): lax.all_to_all(pick_blocks(asked, near), SIDE, split_axis=0, concat_axis=...  6.02 us
  transfers between devices with their start and end apart: 7, of which 5 were waited for; matrix products, arithmetic and copies ran while one was open for 0% of the time, Pallas kernels for 0%

profile of v7, /device:TPU:34, one launch (start us, length us, event | category | flops | bytes accessed | tf_op | source)
XLA Modules:
  0.0 184.4 jit_solution(3150578140686376173)
XLA Ops:
  0.6 0.0 copy-start
  0.7 1.3 constant_dynamic-slice_fusion
  2.0 5.2 %collective-permute-start = (bf16[4,64,256]{2,1,0:T(8,128)(2,1)S(1)}, bf16[4,64,256]{2,1,0:T(8,128)(2,1)S(1)}, u32[]{:S(2)}, u32[]{:S(2)}) collective-permute-start(bf16[4,64,256]{2,1,0:T(8,128)(2,1)S(1)} %pad_maximum_fusion.refs_0_.own_ref), channel_id=1, source_target_pairs={{0,64},{4,68},{8,72},{12,76},{16,80},{20,84},{24,88},{28,92},{32,9... | collective-permute-start | bytes 393224 | tf_op jit(solution)/shard_map/ppermute | solution.py:39
  7.2 15.0 %collective-permute-start.1 = (bf16[4,64,256]{2,1,0:T(8,128)(2,1)S(1)}, bf16[4,64,256]{2,1,0:T(8,128)(2,1)S(1)}, u32[]{:S(2)}, u32[]{:S(2)}) collective-permute-start(bf16[4,64,256]{2,1,0:T(8,128)(2,1)S(1)} %pad_maximum_fusion.refs_0_.own_ref), channel_id=1, source_target_pairs={{0,195},{4,199},{8,203},{12,207},{16,211},{20,215},{24,219},{28,22... | collective-permute-start | bytes 393224 | tf_op jit(solution)/shard_map/ppermute | solution.py:39
  22.2 0.0 copy-done
  22.2 4.3 %collective-permute-done.refs_1_ = bf16[4,64,256]{2,1,0:T(8,128)(2,1)S(1)} collective-permute-done((bf16[4,64,256]{2,1,0:T(8,128)(2,1)S(1)}, bf16[4,64,256]{2,1,0:T(8,128)(2,1)S(1)}, u32[]{:S(2)}, u32[]{:S(2)}) %collective-permute-start) | collective-permute-done | bytes 131104 | tf_op jit(solution)/shard_map/ppermute | solution.py:39
  26.5 1.9 %collective-permute-start.2 = (bf16[4,64,256]{2,1,0:T(8,128)(2,1)S(1)}, bf16[4,64,256]{2,1,0:T(8,128)(2,1)S(1)}, u32[]{:S(2)}, u32[]{:S(2)}) collective-permute-start(bf16[4,64,256]{2,1,0:T(8,128)(2,1)S(1)} %collective-permute-done.refs_1_), channel_id=1, source_target_pairs={{0,64},{4,68},{8,72},{12,76},{16,80},{20,84},{24,88},{28,92},{32,9... | collective-permute-start | bytes 393224 | tf_op jit(solution)/shard_map/ppermute | solution.py:39
  28.5 0.1 slice.13
  28.6 0.1 slice.12
  28.6 0.1 copy.26
  28.7 0.1 copy.27
  28.8 0.1 select_reduce_fusion
  29.0 0.1 all_to_all.16
  29.0 9.3 %all_to_all.26 = s32[16,1,4]{2,1,0:T(1,128)S(1)} all-to-all(s32[16,1,4]{2,1,0:T(1,128)S(1)} %bitcast.25), channel_id=1, replica_groups=mesh['x'=4,'zs'=4,'zb'=2,'c'=2,'y'=4,'zh'=4] {'x','zb','c'}, dimensions={0} | all-to-all | bytes 512 | tf_op jit(solution)/shard_map/all_to_all | solution.py:193
  38.4 0.0 collective-permute-done.1.refs_2_
  38.4 0.0 collective-permute-done.2.refs_3_
  38.4 2.1 %pick_blocks.1 = bf16[16,4,64,256]{3,2,1,0:T(8,128)(2,1)} custom-call(s32[16,4]{1,0:T(8,128)S(1)} %bitcast.19, bf16[4,64,256]{2,1,0:T(8,128)(2,1)S(1)} %pad_maximum_fusion.refs_0_.own_ref, bf16[4,64,256]{2,1,0:T(8,128)(2,1)S(1)} %collective-permute-done.refs_1_, bf16[4,64,256]{2,1,0:T(8,128)(2,1)S(1)} %collective-permute-done.1.refs_2_, ...), custom_call_target="tpu_custom_call" | custom-call | tf_op jit(solution)/shard_map/pick_blocks/pallas_call | solution.py:129
  40.5 0.0 copy-start.1
  40.5 0.0 copy-start.2
  40.5 6.0 %all-to-all-start.1 = ((bf16[16,4,64,256]{3,2,1,0:T(8,128)(2,1)}), bf16[16,4,64,256]{3,2,1,0:T(8,128)(2,1)S(1)}, u32[]{:S(2)}, u32[]{:S(2)}) async-start(bf16[16,4,64,256]{3,2,1,0:T(8,128)(2,1)} %pick_blocks.1), calls=%async_computation.1 | async-start | bytes 4194304 | tf_op jit(solution)/shard_map/all_to_all | solution.py:198
  46.6 24.7 %all-to-all-done.1 = bf16[16,4,64,256]{3,2,1,0:T(8,128)(2,1)S(1)} async-done(((bf16[16,4,64,256]{3,2,1,0:T(8,128)(2,1)}), bf16[16,4,64,256]{3,2,1,0:T(8,128)(2,1)S(1)}, u32[]{:S(2)}, u32[]{:S(2)}) %all-to-all-start.1) | async-done | bytes 2097184 | tf_op jit(solution)/shard_map/all_to_all | solution.py:198
  71.2 0.1 broadcast_in_dim.33.bias_ref
  71.3 0.0 copy-done.1
  71.3 0.0 copy-done.2
  71.3 7.8 %attend_grads.1 = (f32[1024,128]{1,0:T(8,128)}, f32[4,64,256]{2,1,0:T(8,128)S(1)}, bf16[64,64,256]{2,1,0:T(8,128)(2,1)S(1)}) custom-call(s32[4,16]{1,0:T(4,128)S(1)} %get-tuple-element.26.slot_ref, bf16[1024,128]{1,0:T(8,128)(2,1)S(1)} %bitcast.17, bf16[1024,128]{1,0:T(8,128)(2,1)S(1)} %bitcast.18, bf16[4,64,256]{2,1,0:T(8,128)(2,1)S(1)} %pad_maximum_fusion.refs_0_.own_ref, ...), custom_call_target="tpu_custom_call" | custom-call | tf_op jit(solution)/shard_map/attend_grads/pallas_call | solution.py:99
  79.1 30.4 %all_to_all.27.in_ref = bf16[16,4,64,256]{3,2,1,0:T(8,128)(2,1)S(1)} all-to-all(bf16[16,4,64,256]{3,2,1,0:T(8,128)(2,1)S(1)} %bitcast.16), channel_id=1, replica_groups=mesh['x'=4,'zs'=4,'zb'=2,'c'=2,'y'=4,'zh'=4] {'x','zb','c'}, dimensions={0} | all-to-all | bytes 4194304 | tf_op jit(solution)/shard_map/all_to_all | solution.py:207
  109.5 1.3 sum_parts.1
  110.8 6.1 %collective-permute-start.3 = (bf16[4,64,256]{2,1,0:T(8,128)(2,1)S(1)}, bf16[4,64,256]{2,1,0:T(8,128)(2,1)S(1)}, u32[]{:S(2)}, u32[]{:S(2)}) collective-permute-start(bf16[4,64,256]{2,1,0:T(8,128)(2,1)S(1)} %get-tuple-element.14), channel_id=1, source_target_pairs={{0,195},{4,199},{8,203},{12,207},{16,211},{20,215},{24,219},{28,22... | collective-permute-start | bytes 393224 | tf_op jit(solution)/shard_map/ppermute | solution.py:39
  116.9 1.9 %collective-permute-start.5 = (bf16[4,64,256]{2,1,0:T(8,128)(2,1)S(1)}, bf16[4,64,256]{2,1,0:T(8,128)(2,1)S(1)}, u32[]{:S(2)}, u32[]{:S(2)}) collective-permute-start(bf16[4,64,256]{2,1,0:T(8,128)(2,1)S(1)} %get-tuple-element.16), channel_id=1, source_target_pairs={{0,64},{4,68},{8,72},{12,76},{16,80},{20,84},{24,88},{28,92},{32,9... | collective-permute-start | bytes 393224 | tf_op jit(solution)/shard_map/ppermute | solution.py:39
  118.8 3.2 %collective-permute-done.3 = bf16[4,64,256]{2,1,0:T(8,128)(2,1)S(1)} collective-permute-done((bf16[4,64,256]{2,1,0:T(8,128)(2,1)S(1)}, bf16[4,64,256]{2,1,0:T(8,128)(2,1)S(1)}, u32[]{:S(2)}, u32[]{:S(2)}) %collective-permute-start.3) | collective-permute-done | bytes 131104 | tf_op jit(solution)/shard_map/ppermute | solution.py:39
  122.0 6.5 %collective-permute-start.4 = (bf16[4,64,256]{2,1,0:T(8,128)(2,1)S(1)}, bf16[4,64,256]{2,1,0:T(8,128)(2,1)S(1)}, u32[]{:S(2)}, u32[]{:S(2)}) collective-permute-start(bf16[4,64,256]{2,1,0:T(8,128)(2,1)S(1)} %add_convert_fusion.1), channel_id=1, source_target_pairs={{0,195},{4,199},{8,203},{12,207},{16,211},{20,215},{24,219},{28,22... | collective-permute-start | bytes 393224 | tf_op jit(solution)/shard_map/ppermute | solution.py:39
  128.5 1.1 collective-permute-done.5
  129.7 3.2 %collective-permute-done.4 = bf16[4,64,256]{2,1,0:T(8,128)(2,1)S(1)} collective-permute-done((bf16[4,64,256]{2,1,0:T(8,128)(2,1)S(1)}, bf16[4,64,256]{2,1,0:T(8,128)(2,1)S(1)}, u32[]{:S(2)}, u32[]{:S(2)}) %collective-permute-start.4) | collective-permute-done | bytes 131104 | tf_op jit(solution)/shard_map/ppermute | solution.py:39
  132.9 50.2 %all_to_all.28 = bf16[16,16,256]{2,1,0:T(8,128)(2,1)S(1)} all-to-all(bf16[16,16,256]{2,1,0:T(8,128)(2,1)S(1)} %bitcast.21), channel_id=1, replica_groups=mesh['x'=4,'zs'=4,'zb'=2,'c'=2,'y'=4,'zh'=4] {'y','zh'}, dimensions={0} | all-to-all | bytes 262144 | tf_op jit(solution)/shard_map/all_to_all | solution.py:213
  183.1 0.6 copy.33
  183.8 0.6 copy.32
  (10 shorter events, 0.2 us)
Async XLA Ops:
  0.6 21.6 %copy-start = (s32[4,4,16]{2,1,0:T(4,128)S(1)}, s32[4,4,16]{2,1,0:T(4,128)}, u32[]{:S(2)}) copy-start(s32[4,4,16]{2,1,0:T(4,128)} %param.9) | copy-start | bytes 3076
  2.0 24.5 %collective-permute-start = (bf16[4,64,256]{2,1,0:T(8,128)(2,1)S(1)}, bf16[4,64,256]{2,1,0:T(8,128)(2,1)S(1)}, u32[]{:S(2)}, u32[]{:S(2)}) collective-permute-start(bf16[4,64,256]{2,1,0:T(8,128)(2,1)S(1)} %pad_maximum_fusion.refs_0_.own_ref), channel_id=1, source_target_pairs={{0,64},{4,68},{8,72},{12,76},{16,80},{20,84},{24,88},{28,92},{32,9... | collective-permute-start | bytes 393224 | tf_op jit(solution)/shard_map/ppermute | solution.py:39
  7.2 31.2 %collective-permute-start.1 = (bf16[4,64,256]{2,1,0:T(8,128)(2,1)S(1)}, bf16[4,64,256]{2,1,0:T(8,128)(2,1)S(1)}, u32[]{:S(2)}, u32[]{:S(2)}) collective-permute-start(bf16[4,64,256]{2,1,0:T(8,128)(2,1)S(1)} %pad_maximum_fusion.refs_0_.own_ref), channel_id=1, source_target_pairs={{0,195},{4,199},{8,203},{12,207},{16,211},{20,215},{24,219},{28,22... | collective-permute-start | bytes 393224 | tf_op jit(solution)/shard_map/ppermute | solution.py:39
  26.5 11.8 %collective-permute-start.2 = (bf16[4,64,256]{2,1,0:T(8,128)(2,1)S(1)}, bf16[4,64,256]{2,1,0:T(8,128)(2,1)S(1)}, u32[]{:S(2)}, u32[]{:S(2)}) collective-permute-start(bf16[4,64,256]{2,1,0:T(8,128)(2,1)S(1)} %collective-permute-done.refs_1_), channel_id=1, source_target_pairs={{0,64},{4,68},{8,72},{12,76},{16,80},{20,84},{24,88},{28,92},{32,9... | collective-permute-start | bytes 393224 | tf_op jit(solution)/shard_map/ppermute | solution.py:39
  40.5 30.8 %copy-start.1 = (bf16[256,4,128]{2,1,0:T(4,128)(2,1)S(1)}, bf16[256,4,128]{2,1,0:T(4,128)(2,1)}, u32[]{:S(2)}) copy-start(bf16[256,4,128]{2,1,0:T(4,128)(2,1)} %param.5) | copy-start | bytes 786436
  40.5 30.8 %copy-start.2 = (bf16[256,4,128]{2,1,0:T(4,128)(2,1)S(1)}, bf16[256,4,128]{2,1,0:T(4,128)(2,1)}, u32[]{:S(2)}) copy-start(bf16[256,4,128]{2,1,0:T(4,128)(2,1)} %param.8) | copy-start | bytes 786436
  40.5 30.7 %all-to-all-start.1 = ((bf16[16,4,64,256]{3,2,1,0:T(8,128)(2,1)}), bf16[16,4,64,256]{3,2,1,0:T(8,128)(2,1)S(1)}, u32[]{:S(2)}, u32[]{:S(2)}) async-start(bf16[16,4,64,256]{3,2,1,0:T(8,128)(2,1)} %pick_blocks.1), calls=%async_computation.1 | async-start | bytes 4194304 | tf_op jit(solution)/shard_map/all_to_all | solution.py:198
  110.8 11.2 %collective-permute-start.3 = (bf16[4,64,256]{2,1,0:T(8,128)(2,1)S(1)}, bf16[4,64,256]{2,1,0:T(8,128)(2,1)S(1)}, u32[]{:S(2)}, u32[]{:S(2)}) collective-permute-start(bf16[4,64,256]{2,1,0:T(8,128)(2,1)S(1)} %get-tuple-element.14), channel_id=1, source_target_pairs={{0,195},{4,199},{8,203},{12,207},{16,211},{20,215},{24,219},{28,22... | collective-permute-start | bytes 393224 | tf_op jit(solution)/shard_map/ppermute | solution.py:39
  116.9 12.8 %collective-permute-start.5 = (bf16[4,64,256]{2,1,0:T(8,128)(2,1)S(1)}, bf16[4,64,256]{2,1,0:T(8,128)(2,1)S(1)}, u32[]{:S(2)}, u32[]{:S(2)}) collective-permute-start(bf16[4,64,256]{2,1,0:T(8,128)(2,1)S(1)} %get-tuple-element.16), channel_id=1, source_target_pairs={{0,64},{4,68},{8,72},{12,76},{16,80},{20,84},{24,88},{28,92},{32,9... | collective-permute-start | bytes 393224 | tf_op jit(solution)/shard_map/ppermute | solution.py:39
  122.0 10.8 %collective-permute-start.4 = (bf16[4,64,256]{2,1,0:T(8,128)(2,1)S(1)}, bf16[4,64,256]{2,1,0:T(8,128)(2,1)S(1)}, u32[]{:S(2)}, u32[]{:S(2)}) collective-permute-start(bf16[4,64,256]{2,1,0:T(8,128)(2,1)S(1)} %add_convert_fusion.1), channel_id=1, source_target_pairs={{0,195},{4,199},{8,203},{12,207},{16,211},{20,215},{24,219},{28,22... | collective-permute-start | bytes 393224 | tf_op jit(solution)/shard_map/ppermute | solution.py:39

commit v8 on v7

--- a/solution.py
+++ b/solution.py
@@ -1,3 +1,6 @@
+import functools
+import math
+
 import jax
 import jax.numpy as jnp
 from jax import lax
@@ -17,6 +20,7 @@
 AXES = SEQ + HEAD
 SIDE = ("x", "zb", "c")
 PEERS = NX * ZB * NC
+PER = ZS // 2
 AWAY = [-(p + 1) // 2 if p % 2 else p // 2 for p in range(ZS)]
 
 F32 = jnp.float32
@@ -39,7 +43,8 @@
     return lax.ppermute(array, AXES, pairs)
 
 
-def attend_body(slot_ref, q_ref, g_ref, own_ref, bias_ref, got_ref, dq_ref, down_ref, back_ref, k_ref, v_ref):
+def attend_body(slot_ref, q_ref, g_ref, own_ref, bias_ref, got_ref, dq_ref, down_ref, *refs):
+    *out_refs, k_ref, v_ref, back_ref = refs
     b = pl.program_id(0)
     rows = q_ref.shape[0]
     width = q_ref.shape[1]
@@ -61,13 +66,13 @@
     k = k_ref[...]
     v = v_ref[...]
     nt = (((1,), (1,)), ((), ()))
-    scores = lax.dot_general(k, q, nt, preferred_element_type=F32) * factor
+    scores = lax.dot_general(k, q, nt, preferred_element_type=F32)
     key_row = lax.broadcasted_iota(jnp.int32, (BLK, rows), 0)
     token = lax.broadcasted_iota(jnp.int32, (BLK, rows), 1) // heads
     own = jnp.where(key_row <= token, scores[:BLK], NEG)
     far = scores[BLK:].reshape(KSEL - 1, BLK, rows) + bias_ref[0, 1:][:, None, :]
     scores = jnp.concatenate([own, far.reshape((KSEL - 1) * BLK, rows)], axis=0)
-    weights = jnp.exp(scores - jnp.max(scores, axis=0, keepdims=True))
+    weights = jnp.exp2((scores - jnp.max(scores, axis=0, keepdims=True)) * (factor * math.log2(math.e)))
     attend = weights * (1.0 / jnp.sum(weights, axis=0, keepdims=True))
     grad_prob = lax.dot_general(v, g, nt, preferred_element_type=F32)
     row_dot = jnp.sum(attend * grad_prob, axis=0, keepdims=True)
@@ -82,11 +87,16 @@
     down_ref[0, :, width:] = dv[:BLK]
     for j in range(1, KSEL):
         slot = slot_ref[b, j]
-
-        @pl.when(slot >= 0)
-        def _():
-            back_ref[slot, :, :width] = dk[j * BLK : (j + 1) * BLK].astype(BF16)
-            back_ref[slot, :, width:] = dv[j * BLK : (j + 1) * BLK].astype(BF16)
+        peer, place = slot // ZS, slot % ZS
+        spare = len(out_refs) * PEERS * PER
+        slot = jnp.where(slot < 0, spare, (place // PER * PEERS + peer) * PER + place % PER)
+        back_ref[slot, :, :width] = dk[j * BLK : (j + 1) * BLK].astype(BF16)
+        back_ref[slot, :, width:] = dv[j * BLK : (j + 1) * BLK].astype(BF16)
+
+    @pl.when(b == pl.num_programs(0) - 1)
+    def _():
+        for part, out_ref in enumerate(out_refs):
+            out_ref[...] = back_ref[part * PEERS * PER : (part + 1) * PEERS * PER]
 
 
 def attend_grads(slots, q_rows, g_rows, own, bias, got):
@@ -96,20 +106,26 @@
     row_spec = pl.BlockSpec((rows, width), lambda b, s: (b, 0))
     own_spec = pl.BlockSpec((1, BLK, 2 * width), lambda b, s: (b, 0, 0))
     whole = pl.BlockSpec(got.shape, lambda b, s: (0, 0, 0))
+    parts = got.shape[0] // (PEERS * PER)
+    back = (PEERS * PER, BLK, 2 * width)
     return pl.pallas_call(
         attend_body,
         grid_spec=pltpu.PrefetchScalarGridSpec(
             num_scalar_prefetch=1,
             grid=(blocks,),
             in_specs=[row_spec, row_spec, own_spec, pl.BlockSpec((1, KSEL, rows), lambda b, s: (b, 0, 0)), whole],
-            out_specs=[row_spec, own_spec, whole],
-            scratch_shapes=[pltpu.VMEM((KSEL * BLK, width), BF16), pltpu.VMEM((KSEL * BLK, width), BF16)],
+            out_specs=[row_spec, own_spec] + [pl.BlockSpec(back, lambda b, s: (0, 0, 0))] * parts,
+            scratch_shapes=[
+                pltpu.VMEM((KSEL * BLK, width), BF16),
+                pltpu.VMEM((KSEL * BLK, width), BF16),
+                pltpu.VMEM((parts * PEERS * PER + 1, BLK, 2 * width), BF16),
+            ],
         ),
         out_shape=[
             jax.ShapeDtypeStruct((total, width), F32),
             jax.ShapeDtypeStruct((blocks, BLK, 2 * width), F32),
-            jax.ShapeDtypeStruct(got.shape, BF16),
-        ],
+        ]
+        + [jax.ShapeDtypeStruct(back, BF16)] * parts,
         compiler_params=pltpu.CompilerParams(dimension_semantics=("arbitrary",), vmem_limit_bytes=48 * 2**20),
         name="attend_grads",
     )(slots, q_rows, g_rows, own, bias, got)
@@ -140,36 +156,32 @@
     )(want, *near)
 
 
-def sum_body(want_ref, in_ref, own_ref, *refs):
-    out_refs, sum_ref = refs[:-1], refs[-1]
+def sum_body(part, want_ref, in_ref, *refs):
+    home_refs, out_refs, sum_ref = refs[: -1 - PER], refs[-1 - PER : -1], refs[-1]
     for place, out_ref in enumerate(out_refs):
-        sum_ref[...] = jnp.zeros_like(sum_ref) if place else own_ref[...]
+        joined = (home_refs[-1:] if place else home_refs[:-1]) if home_refs else ()
+        sum_ref[...] = sum((ref[...].astype(F32) for ref in joined), jnp.zeros_like(sum_ref))
         for peer in range(PEERS):
-            slot = jnp.maximum(want_ref[peer, place], 0)
+            slot = jnp.maximum(want_ref[peer, part * PER + place], 0)
             sum_ref[slot] += in_ref[peer, place].astype(F32)
         out_ref[...] = sum_ref[...].astype(out_ref.dtype)
 
 
-def sum_parts(want, parts, own_grads):
-    shape = own_grads.shape
+def sum_parts(part, want, parts, shape, home):
     spec = pl.BlockSpec(shape, lambda k, w: (0, 0, 0))
     return pl.pallas_call(
-        sum_body,
+        functools.partial(sum_body, part),
         grid_spec=pltpu.PrefetchScalarGridSpec(
             num_scalar_prefetch=1,
             grid=(1,),
-            in_specs=[pl.BlockSpec(parts.shape, lambda k, w: (0, 0, 0, 0)), spec],
-            out_specs=[spec] * ZS,
+            in_specs=[pl.BlockSpec(parts.shape, lambda k, w: (0, 0, 0, 0))] + [spec] * len(home),
+            out_specs=[spec] * PER,
             scratch_shapes=[pltpu.VMEM(shape, F32)],
         ),
-        out_shape=[jax.ShapeDtypeStruct(shape, BF16 if place else F32) for place in range(ZS)],
+        out_shape=[jax.ShapeDtypeStruct(shape, F32 if home and place == 0 else BF16) for place in range(PER)],
         compiler_params=pltpu.CompilerParams(vmem_limit_bytes=32 * 2**20),
         name="sum_parts",
-    )(want, parts, own_grads)
-
-
-def plus(a, b):
-    return (a.astype(F32) + b.astype(F32)).astype(BF16)
+    )(want, parts, *home)
 
 
 def on_device(queries, key_states, values, grad_out, picked_blocks):
@@ -192,22 +204,24 @@
     wanted = jnp.max(jnp.where(match, (picks % blocks)[:, 1:, None], -1), axis=(0, 1))
     asked = lax.all_to_all(wanted.reshape(PEERS, ZS), SIDE, split_axis=0, concat_axis=0, tiled=True)
 
-    near = [own]
-    for away in AWAY[1:]:
-        near.append(send(near[max(len(near) - 2, 0)], 1 if away < 0 else -1))
+    near = [own] + [send(own, -away) for away in AWAY[1:]]
     got = lax.all_to_all(pick_blocks(asked, near), SIDE, split_axis=0, concat_axis=0, tiled=True)
     got = got.reshape(PEERS * ZS, BLK, 2 * width)
     bias = jnp.where(live, 0.0, NEG).astype(F32)
     bias = jnp.broadcast_to(bias[:, :, None], (blocks, KSEL, BLK * heads))
-    dq, own_grads, back = attend_grads(
+    dq, own_grads, *back = attend_grads(
         slots, queries.reshape(tokens * heads, width), grad_out.reshape(tokens * heads, width), own, bias, got
     )
     grad_queries = dq.reshape(tokens, heads, width)
 
-    parts = lax.all_to_all(back.reshape(PEERS, ZS, BLK, 2 * width), SIDE, split_axis=0, concat_axis=0, tiled=True)
-    total, down1, up1, down2 = sum_parts(asked, parts, own_grads)
-    down = send(plus(send(down2, -1), down1), -1)
-    total = total + down.astype(F32) + send(up1, 1).astype(F32)
+    def returned(part, home):
+        parts = back[part].reshape(PEERS, PER, BLK, 2 * width)
+        parts = lax.all_to_all(parts, SIDE, split_axis=0, concat_axis=0, tiled=True)
+        return sum_parts(part, asked, parts, own.shape, home)
+
+    up1, down2 = returned(1, [])
+    total, down1 = returned(0, [own_grads, send(up1, 1), send(down2, -1)])
+    total = total + send(down1, -1).astype(F32)
 
     pieces = total.astype(BF16).reshape(NY * ZH, tokens // (NY * ZH), 2 * width)
     pieces = lax.all_to_all(pieces, HEAD, split_axis=0, concat_axis=0, tiled=True)

time: 185 us -> 185 us (level)
  the two profiles are of different devices: /device:TPU:34 before, /device:TPU:46 now
where the time goes in v8:
time: 185 us
  blocking collectives  80.9 us (44%)
  starting transfers between devices  48 us (26%)
  waiting for transfers between devices  39.9 us (22%)
  Pallas kernels  11.9 us (6%)
  local copies, waits for them, and re-layouts  3.11 us (2%)
    all_to_all x1, blocking collectives, on_device(): lax.all_to_all(pieces, HEAD, split_axis=0, concat_axis=0, tiled=True)  47.7 us
    ppermute x6, starting transfers between devices, send(): return lax.ppermute(array, AXES, pairs)  35.2 us
    all_to_all x1, waiting for transfers between devices, on_device(): lax.all_to_all(pick_blocks(asked, near), SIDE, split_axis=0, concat_axis=...  24.6 us
    all_to_all x1, blocking collectives, returned(): parts = lax.all_to_all(parts, SIDE, split_axis=0, concat_axis=0, tiled=True)  19.2 us
    all_to_all x1, blocking collectives, on_device(): lax.all_to_all(wanted.reshape(PEERS, ZS), SIDE, split_axis=0, concat_axis...  14 us
    ppermute x6, waiting for transfers between devices, send(): return lax.ppermute(array, AXES, pairs)  8.02 us
    pallas_call x1, Pallas kernels, attend_grads(): pl.pallas_call(attend_body, grid_spec=pltpu.PrefetchScalarGridSpec(num_sc...  7.72 us
    all_to_all x1, waiting for transfers between devices, returned(): parts = lax.all_to_all(parts, SIDE, split_axis=0, concat_axis=0, tiled=True)  7.28 us
  transfers between devices with their start and end apart: 8, of which 4 were waited for; matrix products, arithmetic and copies ran while one was open for 0% of the time, Pallas kernels for 1%

profile of v8, /device:TPU:46, one launch (start us, length us, event | category | flops | bytes accessed | tf_op | source)
XLA Modules:
  0.0 184.8 jit_solution(7089015006660544129)
XLA Ops:
  0.6 0.0 copy-start
  0.7 1.3 constant_dynamic-slice_fusion
  2.0 9.1 %collective-permute-start.2 = (bf16[4,64,256]{2,1,0:T(8,128)(2,1)S(1)}, bf16[4,64,256]{2,1,0:T(8,128)(2,1)S(1)}, u32[]{:S(2)}, u32[]{:S(2)}) collective-permute-start(bf16[4,64,256]{2,1,0:T(8,128)(2,1)S(1)} %pad_maximum_fusion.refs_0_.own_ref), channel_id=1, source_target_pairs={{0,128},{4,132},{8,136},{12,140},{16,144},{20,148},{24,152},{28,15... | collective-permute-start | bytes 393224 | tf_op jit(solution)/shard_map/ppermute | solution.py:43
  11.1 11.0 %collective-permute-start.1 = (bf16[4,64,256]{2,1,0:T(8,128)(2,1)S(1)}, bf16[4,64,256]{2,1,0:T(8,128)(2,1)S(1)}, u32[]{:S(2)}, u32[]{:S(2)}) collective-permute-start(bf16[4,64,256]{2,1,0:T(8,128)(2,1)S(1)} %pad_maximum_fusion.refs_0_.own_ref), channel_id=1, source_target_pairs={{0,195},{4,199},{8,203},{12,207},{16,211},{20,215},{24,219},{28,22... | collective-permute-start | bytes 393224 | tf_op jit(solution)/shard_map/ppermute | solution.py:43
  22.2 1.9 %collective-permute-start = (bf16[4,64,256]{2,1,0:T(8,128)(2,1)S(1)}, bf16[4,64,256]{2,1,0:T(8,128)(2,1)S(1)}, u32[]{:S(2)}, u32[]{:S(2)}) collective-permute-start(bf16[4,64,256]{2,1,0:T(8,128)(2,1)S(1)} %pad_maximum_fusion.refs_0_.own_ref), channel_id=1, source_target_pairs={{0,64},{4,68},{8,72},{12,76},{16,80},{20,84},{24,88},{28,92},{32,9... | collective-permute-start | bytes 393224 | tf_op jit(solution)/shard_map/ppermute | solution.py:43
  24.1 0.0 copy-done
  24.2 0.1 slice.13
  24.3 0.1 slice.12
  24.3 0.1 copy.29
  24.4 0.1 copy.30
  24.5 0.1 select_reduce_fusion
  24.6 0.1 all_to_all.19
  24.7 14.0 %all_to_all.31 = s32[16,1,4]{2,1,0:T(1,128)S(1)} all-to-all(s32[16,1,4]{2,1,0:T(1,128)S(1)} %bitcast.27), channel_id=1, replica_groups=mesh['x'=4,'zs'=4,'zb'=2,'c'=2,'y'=4,'zh'=4] {'x','zb','c'}, dimensions={0} | all-to-all | bytes 512 | tf_op jit(solution)/shard_map/all_to_all | solution.py:205
  38.7 0.0 collective-permute-done.2.refs_3_
  38.7 0.0 collective-permute-done.1.refs_2_
  38.7 0.0 collective-permute-done.refs_1_
  38.8 2.1 %pick_blocks.1 = bf16[16,4,64,256]{3,2,1,0:T(8,128)(2,1)} custom-call(s32[16,4]{1,0:T(8,128)S(1)} %bitcast.20, bf16[4,64,256]{2,1,0:T(8,128)(2,1)S(1)} %pad_maximum_fusion.refs_0_.own_ref, bf16[4,64,256]{2,1,0:T(8,128)(2,1)S(1)} %collective-permute-done.refs_1_, bf16[4,64,256]{2,1,0:T(8,128)(2,1)S(1)} %collective-permute-done.1.refs_2_, ...), custom_call_target="tpu_custom_call" | custom-call | tf_op jit(solution)/shard_map/pick_blocks/pallas_call | solution.py:145
  40.9 0.0 copy-start.1
  40.9 0.0 copy-start.2
  40.9 5.6 %all-to-all-start.1 = ((bf16[16,4,64,256]{3,2,1,0:T(8,128)(2,1)}), bf16[16,4,64,256]{3,2,1,0:T(8,128)(2,1)S(1)}, u32[]{:S(2)}, u32[]{:S(2)}) async-start(bf16[16,4,64,256]{3,2,1,0:T(8,128)(2,1)} %pick_blocks.1), calls=%async_computation.1 | async-start | bytes 4194304 | tf_op jit(solution)/shard_map/all_to_all | solution.py:208
  46.5 24.6 %all-to-all-done.1 = bf16[16,4,64,256]{3,2,1,0:T(8,128)(2,1)S(1)} async-done(((bf16[16,4,64,256]{3,2,1,0:T(8,128)(2,1)}), bf16[16,4,64,256]{3,2,1,0:T(8,128)(2,1)S(1)}, u32[]{:S(2)}, u32[]{:S(2)}) %all-to-all-start.1) | async-done | bytes 2097184 | tf_op jit(solution)/shard_map/all_to_all | solution.py:208
  71.1 0.1 broadcast_in_dim.33.bias_ref
  71.2 0.0 copy-done.1
  71.2 0.0 copy-done.2
  71.2 7.7 %attend_grads.1 = (f32[1024,128]{1,0:T(8,128)}, f32[4,64,256]{2,1,0:T(8,128)S(1)}, bf16[32,64,256]{2,1,0:T(8,128)(2,1)}, bf16[32,64,256]{2,1,0:T(8,128)(2,1)S(1)}) custom-call(s32[4,16]{1,0:T(4,128)S(1)} %get-tuple-element.28.slot_ref, bf16[1024,128]{1,0:T(8,128)(2,1)S(1)} %bitcast.18, bf16[1024,128]{1,0:T(8,128)(2,1)S(1)} %bitcast.19, ...), custom_call_target="tpu_custom_call" | custom-call | tf_op jit(solution)/shard_map/attend_grads/pallas_call | solution.py:111
  78.9 19.2 %all_to_all.32.in_ref = bf16[16,2,64,256]{3,2,1,0:T(8,128)(2,1)S(1)} all-to-all(bf16[16,2,64,256]{3,2,1,0:T(8,128)(2,1)S(1)} %bitcast.17), channel_id=1, replica_groups=mesh['x'=4,'zs'=4,'zb'=2,'c'=2,'y'=4,'zh'=4] {'x','zb','c'}, dimensions={0} | all-to-all | bytes 2097152 | tf_op jit(solution)/shard_map/all_to_all | solution.py:219
  98.1 7.1 %all-to-all-start.2 = ((bf16[16,2,64,256]{3,2,1,0:T(8,128)(2,1)}), bf16[16,2,64,256]{3,2,1,0:T(8,128)(2,1)S(1)}, u32[]{:S(2)}, u32[]{:S(2)}) async-start(bf16[16,2,64,256]{3,2,1,0:T(8,128)(2,1)} %bitcast.9), calls=%async_computation.2 | async-start | bytes 2097152 | tf_op jit(solution)/shard_map/all_to_all | solution.py:219
  105.2 1.0 sum_parts.2
  106.2 2.7 %collective-permute-start.3 = (bf16[4,64,256]{2,1,0:T(8,128)(2,1)S(1)}, bf16[4,64,256]{2,1,0:T(8,128)(2,1)S(1)}, u32[]{:S(2)}, u32[]{:S(2)}) collective-permute-start(bf16[4,64,256]{2,1,0:T(8,128)(2,1)S(1)} %get-tuple-element.15), channel_id=1, source_target_pairs={{0,64},{4,68},{8,72},{12,76},{16,80},{20,84},{24,88},{28,92},{32,9... | collective-permute-start | bytes 393224 | tf_op jit(solution)/shard_map/ppermute | solution.py:43
  109.0 5.2 %collective-permute-start.4 = (bf16[4,64,256]{2,1,0:T(8,128)(2,1)S(1)}, bf16[4,64,256]{2,1,0:T(8,128)(2,1)S(1)}, u32[]{:S(2)}, u32[]{:S(2)}) collective-permute-start(bf16[4,64,256]{2,1,0:T(8,128)(2,1)S(1)} %get-tuple-element.16), channel_id=1, source_target_pairs={{0,195},{4,199},{8,203},{12,207},{16,211},{20,215},{24,219},{28,22... | collective-permute-start | bytes 393224 | tf_op jit(solution)/shard_map/ppermute | solution.py:43
  114.2 7.3 %all-to-all-done.2.in_ref = bf16[16,2,64,256]{3,2,1,0:T(8,128)(2,1)S(1)} async-done(((bf16[16,2,64,256]{3,2,1,0:T(8,128)(2,1)}), bf16[16,2,64,256]{3,2,1,0:T(8,128)(2,1)S(1)}, u32[]{:S(2)}, u32[]{:S(2)}) %all-to-all-start.2) | async-done | bytes 1048608 | tf_op jit(solution)/shard_map/all_to_all | solution.py:219
  121.5 0.0 collective-permute-done.3.refs_1_
  121.5 2.7 %collective-permute-done.4.refs_2_ = bf16[4,64,256]{2,1,0:T(8,128)(2,1)S(1)} collective-permute-done((bf16[4,64,256]{2,1,0:T(8,128)(2,1)S(1)}, bf16[4,64,256]{2,1,0:T(8,128)(2,1)S(1)}, u32[]{:S(2)}, u32[]{:S(2)}) %collective-permute-start.4) | collective-permute-done | bytes 131104 | tf_op jit(solution)/shard_map/ppermute | solution.py:43
  124.2 1.0 sum_parts.3
  125.2 5.2 %collective-permute-start.5 = (bf16[4,64,256]{2,1,0:T(8,128)(2,1)S(1)}, bf16[4,64,256]{2,1,0:T(8,128)(2,1)S(1)}, u32[]{:S(2)}, u32[]{:S(2)}) collective-permute-start(bf16[4,64,256]{2,1,0:T(8,128)(2,1)S(1)} %get-tuple-element.18), channel_id=1, source_target_pairs={{0,195},{4,199},{8,203},{12,207},{16,211},{20,215},{24,219},{28,22... | collective-permute-start | bytes 393224 | tf_op jit(solution)/shard_map/ppermute | solution.py:43
  130.4 5.3 %collective-permute-done.5 = bf16[4,64,256]{2,1,0:T(8,128)(2,1)S(1)} collective-permute-done((bf16[4,64,256]{2,1,0:T(8,128)(2,1)S(1)}, bf16[4,64,256]{2,1,0:T(8,128)(2,1)S(1)}, u32[]{:S(2)}, u32[]{:S(2)}) %collective-permute-start.5) | collective-permute-done | bytes 131104 | tf_op jit(solution)/shard_map/ppermute | solution.py:43
  135.8 47.7 %all_to_all.33 = bf16[16,16,256]{2,1,0:T(8,128)(2,1)S(1)} all-to-all(bf16[16,16,256]{2,1,0:T(8,128)(2,1)S(1)} %bitcast.23), channel_id=1, replica_groups=mesh['x'=4,'zs'=4,'zb'=2,'c'=2,'y'=4,'zh'=4] {'y','zh'}, dimensions={0} | all-to-all | bytes 262144 | tf_op jit(solution)/shard_map/all_to_all | solution.py:227
  183.5 0.6 copy.37
  184.1 0.6 copy.36
  (9 shorter events, 0.2 us)
Async XLA Ops:
  0.6 23.5 %copy-start = (s32[4,4,16]{2,1,0:T(4,128)S(1)}, s32[4,4,16]{2,1,0:T(4,128)}, u32[]{:S(2)}) copy-start(s32[4,4,16]{2,1,0:T(4,128)} %param.9) | copy-start | bytes 3076
  2.0 36.7 %collective-permute-start.2 = (bf16[4,64,256]{2,1,0:T(8,128)(2,1)S(1)}, bf16[4,64,256]{2,1,0:T(8,128)(2,1)S(1)}, u32[]{:S(2)}, u32[]{:S(2)}) collective-permute-start(bf16[4,64,256]{2,1,0:T(8,128)(2,1)S(1)} %pad_maximum_fusion.refs_0_.own_ref), channel_id=1, source_target_pairs={{0,128},{4,132},{8,136},{12,140},{16,144},{20,148},{24,152},{28,15... | collective-permute-start | bytes 393224 | tf_op jit(solution)/shard_map/ppermute | solution.py:43
  11.1 27.6 %collective-permute-start.1 = (bf16[4,64,256]{2,1,0:T(8,128)(2,1)S(1)}, bf16[4,64,256]{2,1,0:T(8,128)(2,1)S(1)}, u32[]{:S(2)}, u32[]{:S(2)}) collective-permute-start(bf16[4,64,256]{2,1,0:T(8,128)(2,1)S(1)} %pad_maximum_fusion.refs_0_.own_ref), channel_id=1, source_target_pairs={{0,195},{4,199},{8,203},{12,207},{16,211},{20,215},{24,219},{28,22... | collective-permute-start | bytes 393224 | tf_op jit(solution)/shard_map/ppermute | solution.py:43
  22.2 16.6 %collective-permute-start = (bf16[4,64,256]{2,1,0:T(8,128)(2,1)S(1)}, bf16[4,64,256]{2,1,0:T(8,128)(2,1)S(1)}, u32[]{:S(2)}, u32[]{:S(2)}) collective-permute-start(bf16[4,64,256]{2,1,0:T(8,128)(2,1)S(1)} %pad_maximum_fusion.refs_0_.own_ref), channel_id=1, source_target_pairs={{0,64},{4,68},{8,72},{12,76},{16,80},{20,84},{24,88},{28,92},{32,9... | collective-permute-start | bytes 393224 | tf_op jit(solution)/shard_map/ppermute | solution.py:43
  40.9 30.3 %copy-start.1 = (bf16[256,4,128]{2,1,0:T(4,128)(2,1)S(1)}, bf16[256,4,128]{2,1,0:T(4,128)(2,1)}, u32[]{:S(2)}) copy-start(bf16[256,4,128]{2,1,0:T(4,128)(2,1)} %param.5) | copy-start | bytes 786436
  40.9 30.3 %copy-start.2 = (bf16[256,4,128]{2,1,0:T(4,128)(2,1)S(1)}, bf16[256,4,128]{2,1,0:T(4,128)(2,1)}, u32[]{:S(2)}) copy-start(bf16[256,4,128]{2,1,0:T(4,128)(2,1)} %param.8) | copy-start | bytes 786436
  40.9 30.2 %all-to-all-start.1 = ((bf16[16,4,64,256]{3,2,1,0:T(8,128)(2,1)}), bf16[16,4,64,256]{3,2,1,0:T(8,128)(2,1)S(1)}, u32[]{:S(2)}, u32[]{:S(2)}) async-start(bf16[16,4,64,256]{3,2,1,0:T(8,128)(2,1)} %pick_blocks.1), calls=%async_computation.1 | async-start | bytes 4194304 | tf_op jit(solution)/shard_map/all_to_all | solution.py:208
  98.1 23.4 %all-to-all-start.2 = ((bf16[16,2,64,256]{3,2,1,0:T(8,128)(2,1)}), bf16[16,2,64,256]{3,2,1,0:T(8,128)(2,1)S(1)}, u32[]{:S(2)}, u32[]{:S(2)}) async-start(bf16[16,2,64,256]{3,2,1,0:T(8,128)(2,1)} %bitcast.9), calls=%async_computation.2 | async-start | bytes 2097152 | tf_op jit(solution)/shard_map/all_to_all | solution.py:219
  106.2 15.3 %collective-permute-start.3 = (bf16[4,64,256]{2,1,0:T(8,128)(2,1)S(1)}, bf16[4,64,256]{2,1,0:T(8,128)(2,1)S(1)}, u32[]{:S(2)}, u32[]{:S(2)}) collective-permute-start(bf16[4,64,256]{2,1,0:T(8,128)(2,1)S(1)} %get-tuple-element.15), channel_id=1, source_target_pairs={{0,64},{4,68},{8,72},{12,76},{16,80},{20,84},{24,88},{28,92},{32,9... | collective-permute-start | bytes 393224 | tf_op jit(solution)/shard_map/ppermute | solution.py:43
  109.0 15.2 %collective-permute-start.4 = (bf16[4,64,256]{2,1,0:T(8,128)(2,1)S(1)}, bf16[4,64,256]{2,1,0:T(8,128)(2,1)S(1)}, u32[]{:S(2)}, u32[]{:S(2)}) collective-permute-start(bf16[4,64,256]{2,1,0:T(8,128)(2,1)S(1)} %get-tuple-element.16), channel_id=1, source_target_pairs={{0,195},{4,199},{8,203},{12,207},{16,211},{20,215},{24,219},{28,22... | collective-permute-start | bytes 393224 | tf_op jit(solution)/shard_map/ppermute | solution.py:43
  125.2 10.5 %collective-permute-start.5 = (bf16[4,64,256]{2,1,0:T(8,128)(2,1)S(1)}, bf16[4,64,256]{2,1,0:T(8,128)(2,1)S(1)}, u32[]{:S(2)}, u32[]{:S(2)}) collective-permute-start(bf16[4,64,256]{2,1,0:T(8,128)(2,1)S(1)} %get-tuple-element.18), channel_id=1, source_target_pairs={{0,195},{4,199},{8,203},{12,207},{16,211},{20,215},{24,219},{28,22... | collective-permute-start | bytes 393224 | tf_op jit(solution)/shard_map/ppermute | solution.py:43

commit v9 on v7

--- a/solution.py
+++ b/solution.py
@@ -1,3 +1,5 @@
+import math
+
 import jax
 import jax.numpy as jnp
 from jax import lax
@@ -29,8 +31,9 @@
 
 
 def send(array, step):
+    sign = (1, -1) if abs(step) == ZS // 2 else (1, 1)
     pairs = [
-        (number(x, z, c, y), number(x, z + step * ZB, c, y))
+        (number(x, z, c, y), number(x, z + sign[c] * step * ZB, c, y))
         for x in range(NX)
         for z in range(NZ)
         for c in range(NC)
@@ -61,13 +64,13 @@
     k = k_ref[...]
     v = v_ref[...]
     nt = (((1,), (1,)), ((), ()))
-    scores = lax.dot_general(k, q, nt, preferred_element_type=F32) * factor
+    scores = lax.dot_general(k, q, nt, preferred_element_type=F32)
     key_row = lax.broadcasted_iota(jnp.int32, (BLK, rows), 0)
     token = lax.broadcasted_iota(jnp.int32, (BLK, rows), 1) // heads
     own = jnp.where(key_row <= token, scores[:BLK], NEG)
     far = scores[BLK:].reshape(KSEL - 1, BLK, rows) + bias_ref[0, 1:][:, None, :]
     scores = jnp.concatenate([own, far.reshape((KSEL - 1) * BLK, rows)], axis=0)
-    weights = jnp.exp(scores - jnp.max(scores, axis=0, keepdims=True))
+    weights = jnp.exp2((scores - jnp.max(scores, axis=0, keepdims=True)) * (factor * math.log2(math.e)))
     attend = weights * (1.0 / jnp.sum(weights, axis=0, keepdims=True))
     grad_prob = lax.dot_general(v, g, nt, preferred_element_type=F32)
     row_dot = jnp.sum(attend * grad_prob, axis=0, keepdims=True)
@@ -119,7 +122,7 @@
     out_ref = refs[-1]
     for place, near_ref in enumerate(refs[:-1]):
         for peer in range(PEERS):
-            slot = want_ref[peer, place]
+            slot = want_ref[peer * 8, place]
             out_ref[peer, place] = near_ref[jnp.maximum(slot, 0)]
 
 
@@ -145,7 +148,7 @@
     for place, out_ref in enumerate(out_refs):
         sum_ref[...] = jnp.zeros_like(sum_ref) if place else own_ref[...]
         for peer in range(PEERS):
-            slot = jnp.maximum(want_ref[peer, place], 0)
+            slot = jnp.maximum(want_ref[peer * 8, place], 0)
             sum_ref[slot] += in_ref[peer, place].astype(F32)
         out_ref[...] = sum_ref[...].astype(out_ref.dtype)
 
@@ -168,10 +171,6 @@
     )(want, parts, own_grads)
 
 
-def plus(a, b):
-    return (a.astype(F32) + b.astype(F32)).astype(BF16)
-
-
 def on_device(queries, key_states, values, grad_out, picked_blocks):
     tokens, heads, width = queries.shape
     blocks = tokens // BLK
@@ -190,11 +189,10 @@
     slots = jnp.where(live, peer * ZS + place, -1)
     match = slots[:, 1:, None] == jnp.arange(PEERS * ZS, dtype=jnp.int32)
     wanted = jnp.max(jnp.where(match, (picks % blocks)[:, 1:, None], -1), axis=(0, 1))
-    asked = lax.all_to_all(wanted.reshape(PEERS, ZS), SIDE, split_axis=0, concat_axis=0, tiled=True)
-
-    near = [own]
-    for away in AWAY[1:]:
-        near.append(send(near[max(len(near) - 2, 0)], 1 if away < 0 else -1))
+    wanted = jnp.pad(wanted.reshape(PEERS, 1, ZS), ((0, 0), (0, 7), (0, 128 - ZS)))
+    asked = lax.all_to_all(wanted, SIDE, split_axis=0, concat_axis=0, tiled=True).reshape(PEERS * 8, 128)
+
+    near = [own] + [send(own, -away) for away in AWAY[1:]]
     got = lax.all_to_all(pick_blocks(asked, near), SIDE, split_axis=0, concat_axis=0, tiled=True)
     got = got.reshape(PEERS * ZS, BLK, 2 * width)
     bias = jnp.where(live, 0.0, NEG).astype(F32)
@@ -205,9 +203,9 @@
     grad_queries = dq.reshape(tokens, heads, width)
 
     parts = lax.all_to_all(back.reshape(PEERS, ZS, BLK, 2 * width), SIDE, split_axis=0, concat_axis=0, tiled=True)
-    total, down1, up1, down2 = sum_parts(asked, parts, own_grads)
-    down = send(plus(send(down2, -1), down1), -1)
-    total = total + down.astype(F32) + send(up1, 1).astype(F32)
+    total, *sums = sum_parts(asked, parts, own_grads)
+    for away, held in reversed(list(zip(AWAY[1:], sums))):
+        total = total + send(held, away).astype(F32)
 
     pieces = total.astype(BF16).reshape(NY * ZH, tokens // (NY * ZH), 2 * width)
     pieces = lax.all_to_all(pieces, HEAD, split_axis=0, concat_axis=0, tiled=True)

time: 185 us -> 191 us (1.032)
  the two profiles are of different devices: /device:TPU:34 before, /device:TPU:32 now
where the time goes in v9:
time: 191 us; the launch traced here: 190 us
  blocking collectives  80.3 us (42%)
  starting transfers between devices  52.3 us (27%)
  waiting for transfers between devices  39.1 us (20%)
  Pallas kernels  11.7 us (6%)
  local copies, waits for them, and re-layouts  5.75 us (3%)
    all_to_all x1, blocking collectives, on_device(): lax.all_to_all(pieces, HEAD, split_axis=0, concat_axis=0, tiled=True)  49.5 us
    all_to_all x1, blocking collectives, on_device(): lax.all_to_all(back.reshape(PEERS, ZS, BLK, 2 * width), SIDE, split_axis=...  30.8 us
    ppermute x6, starting transfers between devices, send(): return lax.ppermute(array, AXES, pairs)  28.5 us
    all_to_all x1, waiting for transfers between devices, on_device(): lax.all_to_all(pick_blocks(asked, near), SIDE, split_axis=0, concat_axis=...  26.6 us
    all_to_all x1, starting transfers between devices, on_device(): lax.all_to_all(wanted, SIDE, split_axis=0, concat_axis=0, tiled=True)  15.4 us
    ppermute x6, waiting for transfers between devices, send(): return lax.ppermute(array, AXES, pairs)  12.4 us
    all_to_all x1, starting transfers between devices, on_device(): lax.all_to_all(pick_blocks(asked, near), SIDE, split_axis=0, concat_axis=...  8.35 us
    pallas_call x1, Pallas kernels, attend_grads(): pl.pallas_call(attend_body, grid_spec=pltpu.PrefetchScalarGridSpec(num_sc...  7.69 us
  transfers between devices with their start and end apart: 8, of which 6 were waited for; matrix products, arithmetic and copies ran while one was open for 1% of the time, Pallas kernels for 0%

profile of v9, /device:TPU:32, one launch (start us, length us, event | category | flops | bytes accessed | tf_op | source)
XLA Modules:
  0.0 190.1 jit_solution(4760333209787297003)
XLA Ops:
  0.6 0.0 copy-start
  0.7 0.7 copy-done
  1.4 0.1 slice.13
  1.5 0.1 slice.12
  1.5 0.1 copy.19
  1.6 0.1 copy.20
  1.7 0.1 select_reduce_fusion
  1.8 0.1 reshape.51
  1.9 0.7 pad.4.clone
  2.6 15.4 %all-to-all-start = ((s32[16,8,128]{2,1,0:T(8,128)}), s32[16,8,128]{2,1,0:T(8,128)S(1)}, u32[]{:S(2)}, u32[]{:S(2)}) async-start(s32[16,8,128]{2,1,0:T(8,128)} %pad.4.clone), calls=%async_computation | async-start | bytes 131072 | tf_op jit(solution)/shard_map/all_to_all | solution.py:193
  18.0 1.3 constant_dynamic-slice_fusion
  19.3 1.9 %collective-permute-start.2 = (bf16[4,64,256]{2,1,0:T(8,128)(2,1)S(1)}, bf16[4,64,256]{2,1,0:T(8,128)(2,1)S(1)}, u32[]{:S(2)}, u32[]{:S(2)}) collective-permute-start(bf16[4,64,256]{2,1,0:T(8,128)(2,1)S(1)} %pad_maximum_fusion.refs_0_.own_ref), channel_id=1, source_target_pairs={{0,128},{4,132},{8,136},{12,140},{16,147},{20,151},{24,155},{28,15... | collective-permute-start | bytes 393224 | tf_op jit(solution)/shard_map/ppermute | solution.py:42
  21.3 8.6 %collective-permute-start.1 = (bf16[4,64,256]{2,1,0:T(8,128)(2,1)S(1)}, bf16[4,64,256]{2,1,0:T(8,128)(2,1)S(1)}, u32[]{:S(2)}, u32[]{:S(2)}) collective-permute-start(bf16[4,64,256]{2,1,0:T(8,128)(2,1)S(1)} %pad_maximum_fusion.refs_0_.own_ref), channel_id=1, source_target_pairs={{0,195},{4,199},{8,203},{12,207},{16,211},{20,215},{24,219},{28,22... | collective-permute-start | bytes 393224 | tf_op jit(solution)/shard_map/ppermute | solution.py:42
  29.9 1.9 %collective-permute-start = (bf16[4,64,256]{2,1,0:T(8,128)(2,1)S(1)}, bf16[4,64,256]{2,1,0:T(8,128)(2,1)S(1)}, u32[]{:S(2)}, u32[]{:S(2)}) collective-permute-start(bf16[4,64,256]{2,1,0:T(8,128)(2,1)S(1)} %pad_maximum_fusion.refs_0_.own_ref), channel_id=1, source_target_pairs={{0,64},{4,68},{8,72},{12,76},{16,80},{20,84},{24,88},{28,92},{32,9... | collective-permute-start | bytes 393224 | tf_op jit(solution)/shard_map/ppermute | solution.py:42
  31.8 1.1 collective-permute-done.2.refs_3_
  32.9 5.2 %collective-permute-done.1.refs_2_ = bf16[4,64,256]{2,1,0:T(8,128)(2,1)S(1)} collective-permute-done((bf16[4,64,256]{2,1,0:T(8,128)(2,1)S(1)}, bf16[4,64,256]{2,1,0:T(8,128)(2,1)S(1)}, u32[]{:S(2)}, u32[]{:S(2)}) %collective-permute-start.1) | collective-permute-done | bytes 131104 | tf_op jit(solution)/shard_map/ppermute | solution.py:42
  38.1 1.9 collective-permute-done.refs_1_
  40.0 0.0 all-to-all-done
  40.0 1.8 pick_blocks.1
  41.7 0.0 copy-start.1
  41.8 1.3 copy-done.1
  43.1 0.0 copy-start.2
  43.1 0.0 copy-start.3
  43.1 8.3 %all-to-all-start.1 = ((bf16[16,4,64,256]{3,2,1,0:T(8,128)(2,1)}), bf16[16,4,64,256]{3,2,1,0:T(8,128)(2,1)S(1)}, u32[]{:S(2)}, u32[]{:S(2)}) async-start(bf16[16,4,64,256]{3,2,1,0:T(8,128)(2,1)} %copy-done.1), calls=%async_computation.1 | async-start | bytes 4194304 | tf_op jit(solution)/shard_map/all_to_all | solution.py:196
  51.4 26.6 %all-to-all-done.1 = bf16[16,4,64,256]{3,2,1,0:T(8,128)(2,1)S(1)} async-done(((bf16[16,4,64,256]{3,2,1,0:T(8,128)(2,1)}), bf16[16,4,64,256]{3,2,1,0:T(8,128)(2,1)S(1)}, u32[]{:S(2)}, u32[]{:S(2)}) %all-to-all-start.1) | async-done | bytes 2097184 | tf_op jit(solution)/shard_map/all_to_all | solution.py:196
  78.1 0.1 broadcast_in_dim.33.bias_ref
  78.1 0.0 copy-done.2
  78.1 0.0 copy-done.3
  78.2 7.7 %attend_grads.1 = (f32[1024,128]{1,0:T(8,128)}, f32[4,64,256]{2,1,0:T(8,128)S(1)}, bf16[64,64,256]{2,1,0:T(8,128)(2,1)S(1)}) custom-call(s32[4,16]{1,0:T(4,128)S(1)} %get-tuple-element.26.slot_ref, bf16[1024,128]{1,0:T(8,128)(2,1)S(1)} %bitcast.19, bf16[1024,128]{1,0:T(8,128)(2,1)S(1)} %bitcast.20, bf16[4,64,256]{2,1,0:T(8,128)(2,1)S(1)} %pad_maximum_fusion.refs_0_.own_ref, ...), custom_call_target="tpu_custom_call" | custom-call | tf_op jit(solution)/shard_map/attend_grads/pallas_call | solution.py:102
  85.8 30.8 %all_to_all.20.in_ref = bf16[16,4,64,256]{3,2,1,0:T(8,128)(2,1)S(1)} all-to-all(bf16[16,4,64,256]{3,2,1,0:T(8,128)(2,1)S(1)} %bitcast.16), channel_id=1, replica_groups=mesh['x'=4,'zs'=4,'zb'=2,'c'=2,'y'=4,'zh'=4] {'x','zb','c'}, dimensions={0} | all-to-all | bytes 4194304 | tf_op jit(solution)/shard_map/all_to_all | solution.py:205
  116.7 2.2 %sum_parts.1 = (f32[4,64,256]{2,1,0:T(8,128)S(1)}, bf16[4,64,256]{2,1,0:T(8,128)(2,1)S(1)}, bf16[4,64,256]{2,1,0:T(8,128)(2,1)S(1)}, bf16[4,64,256]{2,1,0:T(8,128)(2,1)S(1)}) custom-call(s32[128,128]{1,0:T(8,128)S(1)} %bitcast.18, bf16[16,4,64,256]{3,2,1,0:T(8,128)(2,1)S(1)} %all_to_all.20.in_ref, f32[4,64,256]{2,1,0:T(8,128)S(1)} %get-tuple-element.12.own_ref), custom_call_target="tpu_custom_call" | custom-call | tf_op jit(solution)/shard_map/sum_parts/pallas_call | solution.py:159
  118.9 8.1 %collective-permute-start.3 = (bf16[4,64,256]{2,1,0:T(8,128)(2,1)S(1)}, bf16[4,64,256]{2,1,0:T(8,128)(2,1)S(1)}, u32[]{:S(2)}, u32[]{:S(2)}) collective-permute-start(bf16[4,64,256]{2,1,0:T(8,128)(2,1)S(1)} %get-tuple-element.14), channel_id=1, source_target_pairs={{0,131},{4,135},{8,139},{12,143},{16,144},{20,148},{24,152},{28,15... | collective-permute-start | bytes 393224 | tf_op jit(solution)/shard_map/ppermute | solution.py:42
  127.1 1.9 %collective-permute-start.4 = (bf16[4,64,256]{2,1,0:T(8,128)(2,1)S(1)}, bf16[4,64,256]{2,1,0:T(8,128)(2,1)S(1)}, u32[]{:S(2)}, u32[]{:S(2)}) collective-permute-start(bf16[4,64,256]{2,1,0:T(8,128)(2,1)S(1)} %get-tuple-element.15), channel_id=1, source_target_pairs={{0,64},{4,68},{8,72},{12,76},{16,80},{20,84},{24,88},{28,92},{32,9... | collective-permute-start | bytes 393224 | tf_op jit(solution)/shard_map/ppermute | solution.py:42
  129.0 6.0 %collective-permute-start.5 = (bf16[4,64,256]{2,1,0:T(8,128)(2,1)S(1)}, bf16[4,64,256]{2,1,0:T(8,128)(2,1)S(1)}, u32[]{:S(2)}, u32[]{:S(2)}) collective-permute-start(bf16[4,64,256]{2,1,0:T(8,128)(2,1)S(1)} %get-tuple-element.16), channel_id=1, source_target_pairs={{0,195},{4,199},{8,203},{12,207},{16,211},{20,215},{24,219},{28,22... | collective-permute-start | bytes 393224 | tf_op jit(solution)/shard_map/ppermute | solution.py:42
  135.0 0.0 collective-permute-done.3
  135.0 1.7 collective-permute-done.4
  136.7 2.6 %collective-permute-done.5 = bf16[4,64,256]{2,1,0:T(8,128)(2,1)S(1)} collective-permute-done((bf16[4,64,256]{2,1,0:T(8,128)(2,1)S(1)}, bf16[4,64,256]{2,1,0:T(8,128)(2,1)S(1)}, u32[]{:S(2)}, u32[]{:S(2)}) %collective-permute-start.5) | collective-permute-done | bytes 131104 | tf_op jit(solution)/shard_map/ppermute | solution.py:42
  139.3 0.1 add_convert_fusion
  139.4 49.5 %all_to_all.21 = bf16[16,16,256]{2,1,0:T(8,128)(2,1)S(1)} all-to-all(bf16[16,16,256]{2,1,0:T(8,128)(2,1)S(1)} %bitcast.21), channel_id=1, replica_groups=mesh['x'=4,'zs'=4,'zb'=2,'c'=2,'y'=4,'zh'=4] {'y','zh'}, dimensions={0} | all-to-all | bytes 262144 | tf_op jit(solution)/shard_map/all_to_all | solution.py:211
  188.9 0.6 copy.23
  189.5 0.6 copy.22
  (8 shorter events, 0.1 us)
Async XLA Ops:
  0.6 0.7 copy-start
  2.6 37.4 %all-to-all-start = ((s32[16,8,128]{2,1,0:T(8,128)}), s32[16,8,128]{2,1,0:T(8,128)S(1)}, u32[]{:S(2)}, u32[]{:S(2)}) async-start(s32[16,8,128]{2,1,0:T(8,128)} %pad.4.clone), calls=%async_computation | async-start | bytes 131072 | tf_op jit(solution)/shard_map/all_to_all | solution.py:193
  19.3 13.6 %collective-permute-start.2 = (bf16[4,64,256]{2,1,0:T(8,128)(2,1)S(1)}, bf16[4,64,256]{2,1,0:T(8,128)(2,1)S(1)}, u32[]{:S(2)}, u32[]{:S(2)}) collective-permute-start(bf16[4,64,256]{2,1,0:T(8,128)(2,1)S(1)} %pad_maximum_fusion.refs_0_.own_ref), channel_id=1, source_target_pairs={{0,128},{4,132},{8,136},{12,140},{16,147},{20,151},{24,155},{28,15... | collective-permute-start | bytes 393224 | tf_op jit(solution)/shard_map/ppermute | solution.py:42
  21.3 16.9 %collective-permute-start.1 = (bf16[4,64,256]{2,1,0:T(8,128)(2,1)S(1)}, bf16[4,64,256]{2,1,0:T(8,128)(2,1)S(1)}, u32[]{:S(2)}, u32[]{:S(2)}) collective-permute-start(bf16[4,64,256]{2,1,0:T(8,128)(2,1)S(1)} %pad_maximum_fusion.refs_0_.own_ref), channel_id=1, source_target_pairs={{0,195},{4,199},{8,203},{12,207},{16,211},{20,215},{24,219},{28,22... | collective-permute-start | bytes 393224 | tf_op jit(solution)/shard_map/ppermute | solution.py:42
  29.9 10.1 %collective-permute-start = (bf16[4,64,256]{2,1,0:T(8,128)(2,1)S(1)}, bf16[4,64,256]{2,1,0:T(8,128)(2,1)S(1)}, u32[]{:S(2)}, u32[]{:S(2)}) collective-permute-start(bf16[4,64,256]{2,1,0:T(8,128)(2,1)S(1)} %pad_maximum_fusion.refs_0_.own_ref), channel_id=1, source_target_pairs={{0,64},{4,68},{8,72},{12,76},{16,80},{20,84},{24,88},{28,92},{32,9... | collective-permute-start | bytes 393224 | tf_op jit(solution)/shard_map/ppermute | solution.py:42
  41.7 1.3 copy-start.1
  43.1 35.1 %copy-start.2 = (bf16[256,4,128]{2,1,0:T(4,128)(2,1)S(1)}, bf16[256,4,128]{2,1,0:T(4,128)(2,1)}, u32[]{:S(2)}) copy-start(bf16[256,4,128]{2,1,0:T(4,128)(2,1)} %param.5) | copy-start | bytes 786436
  43.1 35.1 %copy-start.3 = (bf16[256,4,128]{2,1,0:T(4,128)(2,1)S(1)}, bf16[256,4,128]{2,1,0:T(4,128)(2,1)}, u32[]{:S(2)}) copy-start(bf16[256,4,128]{2,1,0:T(4,128)(2,1)} %param.8) | copy-start | bytes 786436
  43.1 35.0 %all-to-all-start.1 = ((bf16[16,4,64,256]{3,2,1,0:T(8,128)(2,1)}), bf16[16,4,64,256]{3,2,1,0:T(8,128)(2,1)S(1)}, u32[]{:S(2)}, u32[]{:S(2)}) async-start(bf16[16,4,64,256]{3,2,1,0:T(8,128)(2,1)} %copy-done.1), calls=%async_computation.1 | async-start | bytes 4194304 | tf_op jit(solution)/shard_map/all_to_all | solution.py:196
  118.9 16.1 %collective-permute-start.3 = (bf16[4,64,256]{2,1,0:T(8,128)(2,1)S(1)}, bf16[4,64,256]{2,1,0:T(8,128)(2,1)S(1)}, u32[]{:S(2)}, u32[]{:S(2)}) collective-permute-start(bf16[4,64,256]{2,1,0:T(8,128)(2,1)S(1)} %get-tuple-element.14), channel_id=1, source_target_pairs={{0,131},{4,135},{8,139},{12,143},{16,144},{20,148},{24,152},{28,15... | collective-permute-start | bytes 393224 | tf_op jit(solution)/shard_map/ppermute | solution.py:42
  127.1 9.6 %collective-permute-start.4 = (bf16[4,64,256]{2,1,0:T(8,128)(2,1)S(1)}, bf16[4,64,256]{2,1,0:T(8,128)(2,1)S(1)}, u32[]{:S(2)}, u32[]{:S(2)}) collective-permute-start(bf16[4,64,256]{2,1,0:T(8,128)(2,1)S(1)} %get-tuple-element.15), channel_id=1, source_target_pairs={{0,64},{4,68},{8,72},{12,76},{16,80},{20,84},{24,88},{28,92},{32,9... | collective-permute-start | bytes 393224 | tf_op jit(solution)/shard_map/ppermute | solution.py:42
  129.0 10.3 %collective-permute-start.5 = (bf16[4,64,256]{2,1,0:T(8,128)(2,1)S(1)}, bf16[4,64,256]{2,1,0:T(8,128)(2,1)S(1)}, u32[]{:S(2)}, u32[]{:S(2)}) collective-permute-start(bf16[4,64,256]{2,1,0:T(8,128)(2,1)S(1)} %get-tuple-element.16), channel_id=1, source_target_pairs={{0,195},{4,199},{8,203},{12,207},{16,211},{20,215},{24,219},{28,22... | collective-permute-start | bytes 393224 | tf_op jit(solution)/shard_map/ppermute | solution.py:42

commit v10 on v7

--- a/solution.py
+++ b/solution.py
@@ -1,3 +1,5 @@
+import math
+
 import jax
 import jax.numpy as jnp
 from jax import lax
@@ -39,35 +41,26 @@
     return lax.ppermute(array, AXES, pairs)
 
 
-def attend_body(slot_ref, q_ref, g_ref, own_ref, bias_ref, got_ref, dq_ref, down_ref, back_ref, k_ref, v_ref):
-    b = pl.program_id(0)
-    rows = q_ref.shape[0]
-    width = q_ref.shape[1]
+def attend_block(b, slot_ref, q, g, own_ref, bias_ref, got_ref, back_ref, k_ref, v_ref):
+    rows, width = q.shape
     heads = rows // BLK
     factor = width ** (-0.5)
-
-    @pl.when(b == 0)
-    def _():
-        back_ref[...] = jnp.zeros_like(back_ref)
-
-    k_ref[0:BLK, :] = own_ref[0, :, :width]
-    v_ref[0:BLK, :] = own_ref[0, :, width:]
+    k_ref[0:BLK, :] = own_ref[b, :, :width]
+    v_ref[0:BLK, :] = own_ref[b, :, width:]
     for j in range(1, KSEL):
         slot = jnp.maximum(slot_ref[b, j], 0)
         k_ref[j * BLK : (j + 1) * BLK, :] = got_ref[slot, :, :width]
         v_ref[j * BLK : (j + 1) * BLK, :] = got_ref[slot, :, width:]
-    q = q_ref[...]
-    g = g_ref[...]
     k = k_ref[...]
     v = v_ref[...]
     nt = (((1,), (1,)), ((), ()))
-    scores = lax.dot_general(k, q, nt, preferred_element_type=F32) * factor
+    scores = lax.dot_general(k, q, nt, preferred_element_type=F32)
     key_row = lax.broadcasted_iota(jnp.int32, (BLK, rows), 0)
     token = lax.broadcasted_iota(jnp.int32, (BLK, rows), 1) // heads
     own = jnp.where(key_row <= token, scores[:BLK], NEG)
-    far = scores[BLK:].reshape(KSEL - 1, BLK, rows) + bias_ref[0, 1:][:, None, :]
+    far = scores[BLK:].reshape(KSEL - 1, BLK, rows) + bias_ref[b, 1:][:, None, :]
     scores = jnp.concatenate([own, far.reshape((KSEL - 1) * BLK, rows)], axis=0)
-    weights = jnp.exp(scores - jnp.max(scores, axis=0, keepdims=True))
+    weights = jnp.exp2((scores - jnp.max(scores, axis=0, keepdims=True)) * (factor * math.log2(math.e)))
     attend = weights * (1.0 / jnp.sum(weights, axis=0, keepdims=True))
     grad_prob = lax.dot_general(v, g, nt, preferred_element_type=F32)
     row_dot = jnp.sum(attend * grad_prob, axis=0, keepdims=True)
@@ -75,42 +68,55 @@
     tn = (((0,), (0,)), ((), ()))
     nn = (((1,), (0,)), ((), ()))
     dq = lax.dot_general(k, dscore, tn, preferred_element_type=F32) * factor
-    dq_ref[...] = dq.T
     dk = lax.dot_general(dscore, q, nn, preferred_element_type=F32) * factor
     dv = lax.dot_general(attend.astype(BF16), g, nn, preferred_element_type=F32)
-    down_ref[0, :, :width] = dk[:BLK]
-    down_ref[0, :, width:] = dv[:BLK]
     for j in range(1, KSEL):
         slot = slot_ref[b, j]
-
-        @pl.when(slot >= 0)
-        def _():
-            back_ref[slot, :, :width] = dk[j * BLK : (j + 1) * BLK].astype(BF16)
-            back_ref[slot, :, width:] = dv[j * BLK : (j + 1) * BLK].astype(BF16)
+        slot = jnp.where(slot < 0, got_ref.shape[0], slot)
+        back_ref[slot, :, :width] = dk[j * BLK : (j + 1) * BLK].astype(BF16)
+        back_ref[slot, :, width:] = dv[j * BLK : (j + 1) * BLK].astype(BF16)
+    return dq.T, jnp.concatenate([dk[:BLK], dv[:BLK]], axis=1)
+
+
+def attend_body(slot_ref, q_ref, g_ref, own_ref, bias_ref, got_ref, dq_ref, down_ref, out_ref, k_ref, v_ref, back_ref):
+    blocks = own_ref.shape[0]
+    rows = q_ref.shape[0] // blocks
+    back_ref[...] = jnp.zeros_like(back_ref)
+    for b in range(blocks):
+        here = slice(b * rows, (b + 1) * rows)
+        dq_ref[here], down_ref[b] = attend_block(
+            b, slot_ref, q_ref[here], g_ref[here], own_ref, bias_ref, got_ref, back_ref, k_ref.at[b], v_ref.at[b]
+        )
+    out_ref[...] = back_ref[: got_ref.shape[0]]
 
 
 def attend_grads(slots, q_rows, g_rows, own, bias, got):
     blocks = slots.shape[0]
     total, width = q_rows.shape
-    rows = total // blocks
-    row_spec = pl.BlockSpec((rows, width), lambda b, s: (b, 0))
-    own_spec = pl.BlockSpec((1, BLK, 2 * width), lambda b, s: (b, 0, 0))
-    whole = pl.BlockSpec(got.shape, lambda b, s: (0, 0, 0))
+
+    def whole(shape):
+        return pl.BlockSpec(shape, lambda i, s: (0,) * len(shape))
+
+    outs = [
+        jax.ShapeDtypeStruct((total, width), F32),
+        jax.ShapeDtypeStruct((blocks, BLK, 2 * width), F32),
+        jax.ShapeDtypeStruct(got.shape, BF16),
+    ]
     return pl.pallas_call(
         attend_body,
         grid_spec=pltpu.PrefetchScalarGridSpec(
             num_scalar_prefetch=1,
-            grid=(blocks,),
-            in_specs=[row_spec, row_spec, own_spec, pl.BlockSpec((1, KSEL, rows), lambda b, s: (b, 0, 0)), whole],
-            out_specs=[row_spec, own_spec, whole],
-            scratch_shapes=[pltpu.VMEM((KSEL * BLK, width), BF16), pltpu.VMEM((KSEL * BLK, width), BF16)],
+            grid=(1,),
+            in_specs=[whole(array.shape) for array in (q_rows, g_rows, own, bias, got)],
+            out_specs=[whole(out.shape) for out in outs],
+            scratch_shapes=[
+                pltpu.VMEM((blocks, KSEL * BLK, width), BF16),
+                pltpu.VMEM((blocks, KSEL * BLK, width), BF16),
+                pltpu.VMEM((got.shape[0] + 1, BLK, 2 * width), BF16),
+            ],
         ),
-        out_shape=[
-            jax.ShapeDtypeStruct((total, width), F32),
-            jax.ShapeDtypeStruct((blocks, BLK, 2 * width), F32),
-            jax.ShapeDtypeStruct(got.shape, BF16),
-        ],
-        compiler_params=pltpu.CompilerParams(dimension_semantics=("arbitrary",), vmem_limit_bytes=48 * 2**20),
+        out_shape=outs,
+        compiler_params=pltpu.CompilerParams(vmem_limit_bytes=28 * 2**20),
         name="attend_grads",
     )(slots, q_rows, g_rows, own, bias, got)
 
@@ -190,7 +196,8 @@
     slots = jnp.where(live, peer * ZS + place, -1)
     match = slots[:, 1:, None] == jnp.arange(PEERS * ZS, dtype=jnp.int32)
     wanted = jnp.max(jnp.where(match, (picks % blocks)[:, 1:, None], -1), axis=(0, 1))
-    asked = lax.all_to_all(wanted.reshape(PEERS, ZS), SIDE, split_axis=0, concat_axis=0, tiled=True)
+    wanted = jnp.broadcast_to(wanted.reshape(PEERS, ZS, 1), (PEERS, ZS, 128))
+    asked = lax.all_to_all(wanted, SIDE, split_axis=0, concat_axis=0, tiled=True)[:, :, 0]
 
     near = [own]
     for away in AWAY[1:]:

time: 185 us -> 186 us (level)
  blocking collectives: 89.9 us -> 80.5 us
  waiting for transfers between devices: 36.5 us -> 43.8 us
  starting transfers between devices: 42.5 us -> 45.9 us
    all_to_all x0 -> x1, starting transfers between devices: none -> 12.8 us  [on_device(): lax.all_to_all(wanted, SIDE, split_axis=0, concat_axis=0, tiled=True)]
    all_to_all x1 -> x0, blocking collectives: 9.34 us -> none  [on_device(): lax.all_to_all(wanted.reshape(PEERS, ZS), SIDE, split_axis=0, concat_axis...]
    ppermute x6, starting transfers between devices: 36.5 us -> 27.2 us  [send(): return lax.ppermute(array, AXES, pairs)]
    ppermute x6, waiting for transfers between devices: 11.9 us -> 19.1 us  [send(): return lax.ppermute(array, AXES, pairs)]
  transfers between devices with their start and end apart: 7 -> 8, of which waited for: 5 -> 6; matrix products, arithmetic and copies ran while one was open for 0% -> 1% of each run, Pallas kernels for 0% -> 0%
where the time goes in v10:
time: 186 us; the launch traced here: 185 us
  blocking collectives  80.5 us (43%)
  starting transfers between devices  45.9 us (25%)
  waiting for transfers between devices  43.8 us (24%)
  Pallas kernels  9.98 us (5%)
  local copies, waits for them, and re-layouts  4.01 us (2%)
    all_to_all x1, blocking collectives, on_device(): lax.all_to_all(pieces, HEAD, split_axis=0, concat_axis=0, tiled=True)  50.1 us
    all_to_all x1, blocking collectives, on_device(): lax.all_to_all(back.reshape(PEERS, ZS, BLK, 2 * width), SIDE, split_axis=...  30.4 us
    ppermute x6, starting transfers between devices, send(): return lax.ppermute(array, AXES, pairs)  27.2 us
    all_to_all x1, waiting for transfers between devices, on_device(): lax.all_to_all(pick_blocks(asked, near), SIDE, split_axis=0, concat_axis=...  24.7 us
    ppermute x6, waiting for transfers between devices, send(): return lax.ppermute(array, AXES, pairs)  19.1 us
    all_to_all x1, starting transfers between devices, on_device(): lax.all_to_all(wanted, SIDE, split_axis=0, concat_axis=0, tiled=True)  12.8 us
    pallas_call x1, Pallas kernels, attend_grads(): pl.pallas_call(attend_body, grid_spec=pltpu.PrefetchScalarGridSpec(num_sc...  6.54 us
    all_to_all x1, starting transfers between devices, on_device(): lax.all_to_all(pick_blocks(asked, near), SIDE, split_axis=0, concat_axis=...  5.85 us
  transfers between devices with their start and end apart: 8, of which 6 were waited for; matrix products, arithmetic and copies ran while one was open for 1% of the time, Pallas kernels for 0%

profile of v10, /device:TPU:34, one launch (start us, length us, event | category | flops | bytes accessed | tf_op | source)
XLA Modules:
  0.0 185.2 jit_solution(17683452218557852103)
XLA Ops:
  0.6 0.0 copy-start
  0.7 1.3 constant_dynamic-slice_fusion
  2.0 5.2 %collective-permute-start = (bf16[4,64,256]{2,1,0:T(8,128)(2,1)S(1)}, bf16[4,64,256]{2,1,0:T(8,128)(2,1)S(1)}, u32[]{:S(2)}, u32[]{:S(2)}) collective-permute-start(bf16[4,64,256]{2,1,0:T(8,128)(2,1)S(1)} %pad_maximum_fusion.refs_0_.own_ref), channel_id=1, source_target_pairs={{0,64},{4,68},{8,72},{12,76},{16,80},{20,84},{24,88},{28,92},{32,9... | collective-permute-start | bytes 393224 | tf_op jit(solution)/shard_map/ppermute | solution.py:41
  7.2 0.0 copy-done
  7.3 0.1 slice.16
  7.4 0.1 slice.15
  7.4 0.1 copy.25
  7.5 0.1 copy.26
  7.6 0.1 select_reduce_fusion
  7.7 0.1 broadcast_in_dim.43
  7.8 0.7 broadcast_in_dim.44
  8.5 12.8 %all-to-all-start = ((s32[16,4,128]{2,1,0:T(4,128)}), s32[16,4,128]{2,1,0:T(4,128)S(1)}, u32[]{:S(2)}, u32[]{:S(2)}) async-start(s32[16,4,128]{2,1,0:T(4,128)} %broadcast_in_dim.44), calls=%async_computation | async-start | bytes 65536 | tf_op jit(solution)/shard_map/all_to_all | solution.py:200
  21.3 7.9 %collective-permute-start.1 = (bf16[4,64,256]{2,1,0:T(8,128)(2,1)S(1)}, bf16[4,64,256]{2,1,0:T(8,128)(2,1)S(1)}, u32[]{:S(2)}, u32[]{:S(2)}) collective-permute-start(bf16[4,64,256]{2,1,0:T(8,128)(2,1)S(1)} %pad_maximum_fusion.refs_0_.own_ref), channel_id=1, source_target_pairs={{0,195},{4,199},{8,203},{12,207},{16,211},{20,215},{24,219},{28,22... | collective-permute-start | bytes 393224 | tf_op jit(solution)/shard_map/ppermute | solution.py:41
  29.2 0.0 collective-permute-done.refs_1_
  29.2 1.9 %collective-permute-start.2 = (bf16[4,64,256]{2,1,0:T(8,128)(2,1)S(1)}, bf16[4,64,256]{2,1,0:T(8,128)(2,1)S(1)}, u32[]{:S(2)}, u32[]{:S(2)}) collective-permute-start(bf16[4,64,256]{2,1,0:T(8,128)(2,1)S(1)} %collective-permute-done.refs_1_), channel_id=1, source_target_pairs={{0,64},{4,68},{8,72},{12,76},{16,80},{20,84},{24,88},{28,92},{32,9... | collective-permute-start | bytes 393224 | tf_op jit(solution)/shard_map/ppermute | solution.py:41
  31.2 0.0 all-to-all-done
  31.2 0.1 copy.27
  31.3 0.1 copy.28.want_ref
  31.4 1.0 collective-permute-done.1.refs_2_
  32.3 9.0 %collective-permute-done.2.refs_3_ = bf16[4,64,256]{2,1,0:T(8,128)(2,1)S(1)} collective-permute-done((bf16[4,64,256]{2,1,0:T(8,128)(2,1)S(1)}, bf16[4,64,256]{2,1,0:T(8,128)(2,1)S(1)}, u32[]{:S(2)}, u32[]{:S(2)}) %collective-permute-start.2) | collective-permute-done | bytes 131104 | tf_op jit(solution)/shard_map/ppermute | solution.py:41
  41.3 2.1 %pick_blocks.1 = bf16[16,4,64,256]{3,2,1,0:T(8,128)(2,1)} custom-call(s32[16,4]{1,0:T(8,128)S(1)} %copy.28.want_ref, bf16[4,64,256]{2,1,0:T(8,128)(2,1)S(1)} %pad_maximum_fusion.refs_0_.own_ref, bf16[4,64,256]{2,1,0:T(8,128)(2,1)S(1)} %collective-permute-done.refs_1_, bf16[4,64,256]{2,1,0:T(8,128)(2,1)S(1)} %collective-permute-done.1.refs_2_, ...), custom_call_target="tpu_custom_call" | custom-call | tf_op jit(solution)/shard_map/pick_blocks/pallas_call | solution.py:135
  43.5 0.0 copy-start.1
  43.5 0.0 copy-start.2
  43.5 5.9 %all-to-all-start.1 = ((bf16[16,4,64,256]{3,2,1,0:T(8,128)(2,1)}), bf16[16,4,64,256]{3,2,1,0:T(8,128)(2,1)S(1)}, u32[]{:S(2)}, u32[]{:S(2)}) async-start(bf16[16,4,64,256]{3,2,1,0:T(8,128)(2,1)} %pick_blocks.1), calls=%async_computation.1 | async-start | bytes 4194304 | tf_op jit(solution)/shard_map/all_to_all | solution.py:205
  49.3 24.7 %all-to-all-done.1 = bf16[16,4,64,256]{3,2,1,0:T(8,128)(2,1)S(1)} async-done(((bf16[16,4,64,256]{3,2,1,0:T(8,128)(2,1)}), bf16[16,4,64,256]{3,2,1,0:T(8,128)(2,1)S(1)}, u32[]{:S(2)}, u32[]{:S(2)}) %all-to-all-start.1) | async-done | bytes 2097184 | tf_op jit(solution)/shard_map/all_to_all | solution.py:205
  74.0 0.1 broadcast_in_dim.40.bias_ref
  74.1 0.0 copy-done.1
  74.1 0.0 copy-done.2
  74.1 6.5 %attend_grads.1 = (f32[1024,128]{1,0:T(8,128)}, f32[4,64,256]{2,1,0:T(8,128)S(1)}, bf16[64,64,256]{2,1,0:T(8,128)(2,1)S(1)}) custom-call(s32[4,16]{1,0:T(4,128)S(1)} %get-tuple-element.26.slot_ref, bf16[1024,128]{1,0:T(8,128)(2,1)S(1)} %bitcast.17, bf16[1024,128]{1,0:T(8,128)(2,1)S(1)} %bitcast.18, bf16[4,64,256]{2,1,0:T(8,128)(2,1)S(1)} %pad_maximum_fusion.refs_0_.own_ref, ...), custom_call_target="tpu_custom_call" | custom-call | tf_op jit(solution)/shard_map/attend_grads/pallas_call | solution.py:105
  80.6 30.4 %all_to_all.20.in_ref = bf16[16,4,64,256]{3,2,1,0:T(8,128)(2,1)S(1)} all-to-all(bf16[16,4,64,256]{3,2,1,0:T(8,128)(2,1)S(1)} %bitcast.16), channel_id=1, replica_groups=mesh['x'=4,'zs'=4,'zb'=2,'c'=2,'y'=4,'zh'=4] {'x','zb','c'}, dimensions={0} | all-to-all | bytes 4194304 | tf_op jit(solution)/shard_map/all_to_all | solution.py:214
  111.0 1.3 sum_parts.1
  112.3 3.6 %collective-permute-start.3 = (bf16[4,64,256]{2,1,0:T(8,128)(2,1)S(1)}, bf16[4,64,256]{2,1,0:T(8,128)(2,1)S(1)}, u32[]{:S(2)}, u32[]{:S(2)}) collective-permute-start(bf16[4,64,256]{2,1,0:T(8,128)(2,1)S(1)} %get-tuple-element.14), channel_id=1, source_target_pairs={{0,195},{4,199},{8,203},{12,207},{16,211},{20,215},{24,219},{28,22... | collective-permute-start | bytes 393224 | tf_op jit(solution)/shard_map/ppermute | solution.py:41
  115.9 3.1 %collective-permute-start.5 = (bf16[4,64,256]{2,1,0:T(8,128)(2,1)S(1)}, bf16[4,64,256]{2,1,0:T(8,128)(2,1)S(1)}, u32[]{:S(2)}, u32[]{:S(2)}) collective-permute-start(bf16[4,64,256]{2,1,0:T(8,128)(2,1)S(1)} %get-tuple-element.16), channel_id=1, source_target_pairs={{0,64},{4,68},{8,72},{12,76},{16,80},{20,84},{24,88},{28,92},{32,9... | collective-permute-start | bytes 393224 | tf_op jit(solution)/shard_map/ppermute | solution.py:41
  119.0 3.4 %collective-permute-done.3 = bf16[4,64,256]{2,1,0:T(8,128)(2,1)S(1)} collective-permute-done((bf16[4,64,256]{2,1,0:T(8,128)(2,1)S(1)}, bf16[4,64,256]{2,1,0:T(8,128)(2,1)S(1)}, u32[]{:S(2)}, u32[]{:S(2)}) %collective-permute-start.3) | collective-permute-done | bytes 131104 | tf_op jit(solution)/shard_map/ppermute | solution.py:41
  122.5 5.5 %collective-permute-start.4 = (bf16[4,64,256]{2,1,0:T(8,128)(2,1)S(1)}, bf16[4,64,256]{2,1,0:T(8,128)(2,1)S(1)}, u32[]{:S(2)}, u32[]{:S(2)}) collective-permute-start(bf16[4,64,256]{2,1,0:T(8,128)(2,1)S(1)} %add_convert_fusion.1), channel_id=1, source_target_pairs={{0,195},{4,199},{8,203},{12,207},{16,211},{20,215},{24,219},{28,22... | collective-permute-start | bytes 393224 | tf_op jit(solution)/shard_map/ppermute | solution.py:41
  128.0 0.7 collective-permute-done.5
  128.7 5.0 %collective-permute-done.4 = bf16[4,64,256]{2,1,0:T(8,128)(2,1)S(1)} collective-permute-done((bf16[4,64,256]{2,1,0:T(8,128)(2,1)S(1)}, bf16[4,64,256]{2,1,0:T(8,128)(2,1)S(1)}, u32[]{:S(2)}, u32[]{:S(2)}) %collective-permute-start.4) | collective-permute-done | bytes 131104 | tf_op jit(solution)/shard_map/ppermute | solution.py:41
  133.7 0.1 add_convert_fusion
  133.8 50.1 %all_to_all.21 = bf16[16,16,256]{2,1,0:T(8,128)(2,1)S(1)} all-to-all(bf16[16,16,256]{2,1,0:T(8,128)(2,1)S(1)} %bitcast.19), channel_id=1, replica_groups=mesh['x'=4,'zs'=4,'zb'=2,'c'=2,'y'=4,'zh'=4] {'y','zh'}, dimensions={0} | all-to-all | bytes 262144 | tf_op jit(solution)/shard_map/all_to_all | solution.py:220
  183.9 0.6 copy.31
  184.6 0.6 copy.30
  (9 shorter events, 0.2 us)
Async XLA Ops:
  0.6 6.6 %copy-start = (s32[4,4,16]{2,1,0:T(4,128)S(1)}, s32[4,4,16]{2,1,0:T(4,128)}, u32[]{:S(2)}) copy-start(s32[4,4,16]{2,1,0:T(4,128)} %param.9) | copy-start | bytes 3076
  2.0 27.2 %collective-permute-start = (bf16[4,64,256]{2,1,0:T(8,128)(2,1)S(1)}, bf16[4,64,256]{2,1,0:T(8,128)(2,1)S(1)}, u32[]{:S(2)}, u32[]{:S(2)}) collective-permute-start(bf16[4,64,256]{2,1,0:T(8,128)(2,1)S(1)} %pad_maximum_fusion.refs_0_.own_ref), channel_id=1, source_target_pairs={{0,64},{4,68},{8,72},{12,76},{16,80},{20,84},{24,88},{28,92},{32,9... | collective-permute-start | bytes 393224 | tf_op jit(solution)/shard_map/ppermute | solution.py:41
  8.5 22.7 %all-to-all-start = ((s32[16,4,128]{2,1,0:T(4,128)}), s32[16,4,128]{2,1,0:T(4,128)S(1)}, u32[]{:S(2)}, u32[]{:S(2)}) async-start(s32[16,4,128]{2,1,0:T(4,128)} %broadcast_in_dim.44), calls=%async_computation | async-start | bytes 65536 | tf_op jit(solution)/shard_map/all_to_all | solution.py:200
  21.3 11.0 %collective-permute-start.1 = (bf16[4,64,256]{2,1,0:T(8,128)(2,1)S(1)}, bf16[4,64,256]{2,1,0:T(8,128)(2,1)S(1)}, u32[]{:S(2)}, u32[]{:S(2)}) collective-permute-start(bf16[4,64,256]{2,1,0:T(8,128)(2,1)S(1)} %pad_maximum_fusion.refs_0_.own_ref), channel_id=1, source_target_pairs={{0,195},{4,199},{8,203},{12,207},{16,211},{20,215},{24,219},{28,22... | collective-permute-start | bytes 393224 | tf_op jit(solution)/shard_map/ppermute | solution.py:41
  29.2 12.1 %collective-permute-start.2 = (bf16[4,64,256]{2,1,0:T(8,128)(2,1)S(1)}, bf16[4,64,256]{2,1,0:T(8,128)(2,1)S(1)}, u32[]{:S(2)}, u32[]{:S(2)}) collective-permute-start(bf16[4,64,256]{2,1,0:T(8,128)(2,1)S(1)} %collective-permute-done.refs_1_), channel_id=1, source_target_pairs={{0,64},{4,68},{8,72},{12,76},{16,80},{20,84},{24,88},{28,92},{32,9... | collective-permute-start | bytes 393224 | tf_op jit(solution)/shard_map/ppermute | solution.py:41
  43.5 30.6 %copy-start.1 = (bf16[256,4,128]{2,1,0:T(4,128)(2,1)S(1)}, bf16[256,4,128]{2,1,0:T(4,128)(2,1)}, u32[]{:S(2)}) copy-start(bf16[256,4,128]{2,1,0:T(4,128)(2,1)} %param.5) | copy-start | bytes 786436
  43.5 30.6 %copy-start.2 = (bf16[256,4,128]{2,1,0:T(4,128)(2,1)S(1)}, bf16[256,4,128]{2,1,0:T(4,128)(2,1)}, u32[]{:S(2)}) copy-start(bf16[256,4,128]{2,1,0:T(4,128)(2,1)} %param.8) | copy-start | bytes 786436
  43.5 30.5 %all-to-all-start.1 = ((bf16[16,4,64,256]{3,2,1,0:T(8,128)(2,1)}), bf16[16,4,64,256]{3,2,1,0:T(8,128)(2,1)S(1)}, u32[]{:S(2)}, u32[]{:S(2)}) async-start(bf16[16,4,64,256]{3,2,1,0:T(8,128)(2,1)} %pick_blocks.1), calls=%async_computation.1 | async-start | bytes 4194304 | tf_op jit(solution)/shard_map/all_to_all | solution.py:205
  112.3 10.2 %collective-permute-start.3 = (bf16[4,64,256]{2,1,0:T(8,128)(2,1)S(1)}, bf16[4,64,256]{2,1,0:T(8,128)(2,1)S(1)}, u32[]{:S(2)}, u32[]{:S(2)}) collective-permute-start(bf16[4,64,256]{2,1,0:T(8,128)(2,1)S(1)} %get-tuple-element.14), channel_id=1, source_target_pairs={{0,195},{4,199},{8,203},{12,207},{16,211},{20,215},{24,219},{28,22... | collective-permute-start | bytes 393224 | tf_op jit(solution)/shard_map/ppermute | solution.py:41
  115.9 12.8 %collective-permute-start.5 = (bf16[4,64,256]{2,1,0:T(8,128)(2,1)S(1)}, bf16[4,64,256]{2,1,0:T(8,128)(2,1)S(1)}, u32[]{:S(2)}, u32[]{:S(2)}) collective-permute-start(bf16[4,64,256]{2,1,0:T(8,128)(2,1)S(1)} %get-tuple-element.16), channel_id=1, source_target_pairs={{0,64},{4,68},{8,72},{12,76},{16,80},{20,84},{24,88},{28,92},{32,9... | collective-permute-start | bytes 393224 | tf_op jit(solution)/shard_map/ppermute | solution.py:41
  122.5 11.2 %collective-permute-start.4 = (bf16[4,64,256]{2,1,0:T(8,128)(2,1)S(1)}, bf16[4,64,256]{2,1,0:T(8,128)(2,1)S(1)}, u32[]{:S(2)}, u32[]{:S(2)}) collective-permute-start(bf16[4,64,256]{2,1,0:T(8,128)(2,1)S(1)} %add_convert_fusion.1), channel_id=1, source_target_pairs={{0,195},{4,199},{8,203},{12,207},{16,211},{20,215},{24,219},{28,22... | collective-permute-start | bytes 393224 | tf_op jit(solution)/shard_map/ppermute | solution.py:41

commit v11 on v10

--- a/solution.py
+++ b/solution.py
@@ -196,8 +196,7 @@
     slots = jnp.where(live, peer * ZS + place, -1)
     match = slots[:, 1:, None] == jnp.arange(PEERS * ZS, dtype=jnp.int32)
     wanted = jnp.max(jnp.where(match, (picks % blocks)[:, 1:, None], -1), axis=(0, 1))
-    wanted = jnp.broadcast_to(wanted.reshape(PEERS, ZS, 1), (PEERS, ZS, 128))
-    asked = lax.all_to_all(wanted, SIDE, split_axis=0, concat_axis=0, tiled=True)[:, :, 0]
+    asked = lax.all_to_all(wanted.reshape(PEERS, ZS), SIDE, split_axis=0, concat_axis=0, tiled=True)
 
     near = [own]
     for away in AWAY[1:]:

time: 186 us -> 183 us (0.984)
  blocking collectives: 80.5 us -> 89.7 us
  waiting for transfers between devices: 43.8 us -> 36.6 us
  starting transfers between devices: 45.9 us -> 42.5 us
    all_to_all x1 -> x0, starting transfers between devices: 12.8 us -> none  [on_device(): lax.all_to_all(wanted, SIDE, split_axis=0, concat_axis=0, tiled=True)]
    all_to_all x0 -> x1, blocking collectives: none -> 9.34 us  [on_device(): lax.all_to_all(wanted.reshape(PEERS, ZS), SIDE, split_axis=0, concat_axis...]
    ppermute x6, starting transfers between devices: 27.2 us -> 36.5 us  [send(): return lax.ppermute(array, AXES, pairs)]
    ppermute x6, waiting for transfers between devices: 19.1 us -> 11.9 us  [send(): return lax.ppermute(array, AXES, pairs)]
  transfers between devices with their start and end apart: 8 -> 7, of which waited for: 6 -> 5; matrix products, arithmetic and copies ran while one was open for 1% -> 0% of each run, Pallas kernels for 0% -> 0%
where the time goes in v11:
time: 183 us
  blocking collectives  89.7 us (49%)
  starting transfers between devices  42.5 us (23%)
  waiting for transfers between devices  36.6 us (20%)
  Pallas kernels  9.99 us (5%)
  local copies, waits for them, and re-layouts  3.11 us (2%)
    all_to_all x1, blocking collectives, on_device(): lax.all_to_all(pieces, HEAD, split_axis=0, concat_axis=0, tiled=True)  50 us
    ppermute x6, starting transfers between devices, send(): return lax.ppermute(array, AXES, pairs)  36.5 us
    all_to_all x1, blocking collectives, on_device(): lax.all_to_all(back.reshape(PEERS, ZS, BLK, 2 * width), SIDE, split_axis=...  30.3 us
    all_to_all x1, waiting for transfers between devices, on_device(): lax.all_to_all(pick_blocks(asked, near), SIDE, split_axis=0, concat_axis=...  24.7 us
    ppermute x6, waiting for transfers between devices, send(): return lax.ppermute(array, AXES, pairs)  11.9 us
    all_to_all x1, blocking collectives, on_device(): lax.all_to_all(wanted.reshape(PEERS, ZS), SIDE, split_axis=0, concat_axis...  9.34 us
    pallas_call x1, Pallas kernels, attend_grads(): pl.pallas_call(attend_body, grid_spec=pltpu.PrefetchScalarGridSpec(num_sc...  6.54 us
    all_to_all x1, starting transfers between devices, on_device(): lax.all_to_all(pick_blocks(asked, near), SIDE, split_axis=0, concat_axis=...  6.02 us
  transfers between devices with their start and end apart: 7, of which 5 were waited for; matrix products, arithmetic and copies ran while one was open for 0% of the time, Pallas kernels for 0%

profile of v11, /device:TPU:34, one launch (start us, length us, event | category | flops | bytes accessed | tf_op | source)
XLA Modules:
  0.0 182.9 jit_solution(2634211939725902383)
XLA Ops:
  0.6 0.0 copy-start
  0.7 1.3 constant_dynamic-slice_fusion
  2.0 5.2 %collective-permute-start = (bf16[4,64,256]{2,1,0:T(8,128)(2,1)S(1)}, bf16[4,64,256]{2,1,0:T(8,128)(2,1)S(1)}, u32[]{:S(2)}, u32[]{:S(2)}) collective-permute-start(bf16[4,64,256]{2,1,0:T(8,128)(2,1)S(1)} %pad_maximum_fusion.refs_0_.own_ref), channel_id=1, source_target_pairs={{0,64},{4,68},{8,72},{12,76},{16,80},{20,84},{24,88},{28,92},{32,9... | collective-permute-start | bytes 393224 | tf_op jit(solution)/shard_map/ppermute | solution.py:41
  7.2 15.0 %collective-permute-start.1 = (bf16[4,64,256]{2,1,0:T(8,128)(2,1)S(1)}, bf16[4,64,256]{2,1,0:T(8,128)(2,1)S(1)}, u32[]{:S(2)}, u32[]{:S(2)}) collective-permute-start(bf16[4,64,256]{2,1,0:T(8,128)(2,1)S(1)} %pad_maximum_fusion.refs_0_.own_ref), channel_id=1, source_target_pairs={{0,195},{4,199},{8,203},{12,207},{16,211},{20,215},{24,219},{28,22... | collective-permute-start | bytes 393224 | tf_op jit(solution)/shard_map/ppermute | solution.py:41
  22.2 0.0 copy-done
  22.2 4.3 %collective-permute-done.refs_1_ = bf16[4,64,256]{2,1,0:T(8,128)(2,1)S(1)} collective-permute-done((bf16[4,64,256]{2,1,0:T(8,128)(2,1)S(1)}, bf16[4,64,256]{2,1,0:T(8,128)(2,1)S(1)}, u32[]{:S(2)}, u32[]{:S(2)}) %collective-permute-start) | collective-permute-done | bytes 131104 | tf_op jit(solution)/shard_map/ppermute | solution.py:41
  26.5 1.9 %collective-permute-start.2 = (bf16[4,64,256]{2,1,0:T(8,128)(2,1)S(1)}, bf16[4,64,256]{2,1,0:T(8,128)(2,1)S(1)}, u32[]{:S(2)}, u32[]{:S(2)}) collective-permute-start(bf16[4,64,256]{2,1,0:T(8,128)(2,1)S(1)} %collective-permute-done.refs_1_), channel_id=1, source_target_pairs={{0,64},{4,68},{8,72},{12,76},{16,80},{20,84},{24,88},{28,92},{32,9... | collective-permute-start | bytes 393224 | tf_op jit(solution)/shard_map/ppermute | solution.py:41
  28.5 0.1 slice.13
  28.6 0.1 slice.12
  28.6 0.1 copy.26
  28.7 0.1 copy.27
  28.8 0.1 select_reduce_fusion
  29.0 0.1 all_to_all.16
  29.0 9.3 %all_to_all.26 = s32[16,1,4]{2,1,0:T(1,128)S(1)} all-to-all(s32[16,1,4]{2,1,0:T(1,128)S(1)} %bitcast.25), channel_id=1, replica_groups=mesh['x'=4,'zs'=4,'zb'=2,'c'=2,'y'=4,'zh'=4] {'x','zb','c'}, dimensions={0} | all-to-all | bytes 512 | tf_op jit(solution)/shard_map/all_to_all | solution.py:199
  38.4 0.0 collective-permute-done.1.refs_2_
  38.4 0.0 collective-permute-done.2.refs_3_
  38.4 2.1 %pick_blocks.1 = bf16[16,4,64,256]{3,2,1,0:T(8,128)(2,1)} custom-call(s32[16,4]{1,0:T(8,128)S(1)} %bitcast.19, bf16[4,64,256]{2,1,0:T(8,128)(2,1)S(1)} %pad_maximum_fusion.refs_0_.own_ref, bf16[4,64,256]{2,1,0:T(8,128)(2,1)S(1)} %collective-permute-done.refs_1_, bf16[4,64,256]{2,1,0:T(8,128)(2,1)S(1)} %collective-permute-done.1.refs_2_, ...), custom_call_target="tpu_custom_call" | custom-call | tf_op jit(solution)/shard_map/pick_blocks/pallas_call | solution.py:135
  40.5 0.0 copy-start.1
  40.5 0.0 copy-start.2
  40.5 6.0 %all-to-all-start.1 = ((bf16[16,4,64,256]{3,2,1,0:T(8,128)(2,1)}), bf16[16,4,64,256]{3,2,1,0:T(8,128)(2,1)S(1)}, u32[]{:S(2)}, u32[]{:S(2)}) async-start(bf16[16,4,64,256]{3,2,1,0:T(8,128)(2,1)} %pick_blocks.1), calls=%async_computation.1 | async-start | bytes 4194304 | tf_op jit(solution)/shard_map/all_to_all | solution.py:204
  46.6 24.7 %all-to-all-done.1 = bf16[16,4,64,256]{3,2,1,0:T(8,128)(2,1)S(1)} async-done(((bf16[16,4,64,256]{3,2,1,0:T(8,128)(2,1)}), bf16[16,4,64,256]{3,2,1,0:T(8,128)(2,1)S(1)}, u32[]{:S(2)}, u32[]{:S(2)}) %all-to-all-start.1) | async-done | bytes 2097184 | tf_op jit(solution)/shard_map/all_to_all | solution.py:204
  71.2 0.1 broadcast_in_dim.33.bias_ref
  71.3 0.0 copy-done.1
  71.3 0.0 copy-done.2
  71.3 6.5 %attend_grads.1 = (f32[1024,128]{1,0:T(8,128)}, f32[4,64,256]{2,1,0:T(8,128)S(1)}, bf16[64,64,256]{2,1,0:T(8,128)(2,1)S(1)}) custom-call(s32[4,16]{1,0:T(4,128)S(1)} %get-tuple-element.26.slot_ref, bf16[1024,128]{1,0:T(8,128)(2,1)S(1)} %bitcast.17, bf16[1024,128]{1,0:T(8,128)(2,1)S(1)} %bitcast.18, bf16[4,64,256]{2,1,0:T(8,128)(2,1)S(1)} %pad_maximum_fusion.refs_0_.own_ref, ...), custom_call_target="tpu_custom_call" | custom-call | tf_op jit(solution)/shard_map/attend_grads/pallas_call | solution.py:105
  77.9 30.3 %all_to_all.27.in_ref = bf16[16,4,64,256]{3,2,1,0:T(8,128)(2,1)S(1)} all-to-all(bf16[16,4,64,256]{3,2,1,0:T(8,128)(2,1)S(1)} %bitcast.16), channel_id=1, replica_groups=mesh['x'=4,'zs'=4,'zb'=2,'c'=2,'y'=4,'zh'=4] {'x','zb','c'}, dimensions={0} | all-to-all | bytes 4194304 | tf_op jit(solution)/shard_map/all_to_all | solution.py:213
  108.2 1.3 sum_parts.1
  109.5 6.0 %collective-permute-start.3 = (bf16[4,64,256]{2,1,0:T(8,128)(2,1)S(1)}, bf16[4,64,256]{2,1,0:T(8,128)(2,1)S(1)}, u32[]{:S(2)}, u32[]{:S(2)}) collective-permute-start(bf16[4,64,256]{2,1,0:T(8,128)(2,1)S(1)} %get-tuple-element.14), channel_id=1, source_target_pairs={{0,195},{4,199},{8,203},{12,207},{16,211},{20,215},{24,219},{28,22... | collective-permute-start | bytes 393224 | tf_op jit(solution)/shard_map/ppermute | solution.py:41
  115.5 1.9 %collective-permute-start.5 = (bf16[4,64,256]{2,1,0:T(8,128)(2,1)S(1)}, bf16[4,64,256]{2,1,0:T(8,128)(2,1)S(1)}, u32[]{:S(2)}, u32[]{:S(2)}) collective-permute-start(bf16[4,64,256]{2,1,0:T(8,128)(2,1)S(1)} %get-tuple-element.16), channel_id=1, source_target_pairs={{0,64},{4,68},{8,72},{12,76},{16,80},{20,84},{24,88},{28,92},{32,9... | collective-permute-start | bytes 393224 | tf_op jit(solution)/shard_map/ppermute | solution.py:41
  117.5 3.2 %collective-permute-done.3 = bf16[4,64,256]{2,1,0:T(8,128)(2,1)S(1)} collective-permute-done((bf16[4,64,256]{2,1,0:T(8,128)(2,1)S(1)}, bf16[4,64,256]{2,1,0:T(8,128)(2,1)S(1)}, u32[]{:S(2)}, u32[]{:S(2)}) %collective-permute-start.3) | collective-permute-done | bytes 131104 | tf_op jit(solution)/shard_map/ppermute | solution.py:41
  120.7 6.5 %collective-permute-start.4 = (bf16[4,64,256]{2,1,0:T(8,128)(2,1)S(1)}, bf16[4,64,256]{2,1,0:T(8,128)(2,1)S(1)}, u32[]{:S(2)}, u32[]{:S(2)}) collective-permute-start(bf16[4,64,256]{2,1,0:T(8,128)(2,1)S(1)} %add_convert_fusion.1), channel_id=1, source_target_pairs={{0,195},{4,199},{8,203},{12,207},{16,211},{20,215},{24,219},{28,22... | collective-permute-start | bytes 393224 | tf_op jit(solution)/shard_map/ppermute | solution.py:41
  127.2 1.1 collective-permute-done.5
  128.3 3.2 %collective-permute-done.4 = bf16[4,64,256]{2,1,0:T(8,128)(2,1)S(1)} collective-permute-done((bf16[4,64,256]{2,1,0:T(8,128)(2,1)S(1)}, bf16[4,64,256]{2,1,0:T(8,128)(2,1)S(1)}, u32[]{:S(2)}, u32[]{:S(2)}) %collective-permute-start.4) | collective-permute-done | bytes 131104 | tf_op jit(solution)/shard_map/ppermute | solution.py:41
  131.6 0.1 add_convert_fusion
  131.6 50.0 %all_to_all.28 = bf16[16,16,256]{2,1,0:T(8,128)(2,1)S(1)} all-to-all(bf16[16,16,256]{2,1,0:T(8,128)(2,1)S(1)} %bitcast.21), channel_id=1, replica_groups=mesh['x'=4,'zs'=4,'zb'=2,'c'=2,'y'=4,'zh'=4] {'y','zh'}, dimensions={0} | all-to-all | bytes 262144 | tf_op jit(solution)/shard_map/all_to_all | solution.py:219
  181.7 0.6 copy.33
  182.3 0.6 copy.32
  (9 shorter events, 0.2 us)
Async XLA Ops:
  0.6 21.6 %copy-start = (s32[4,4,16]{2,1,0:T(4,128)S(1)}, s32[4,4,16]{2,1,0:T(4,128)}, u32[]{:S(2)}) copy-start(s32[4,4,16]{2,1,0:T(4,128)} %param.9) | copy-start | bytes 3076
  2.0 24.5 %collective-permute-start = (bf16[4,64,256]{2,1,0:T(8,128)(2,1)S(1)}, bf16[4,64,256]{2,1,0:T(8,128)(2,1)S(1)}, u32[]{:S(2)}, u32[]{:S(2)}) collective-permute-start(bf16[4,64,256]{2,1,0:T(8,128)(2,1)S(1)} %pad_maximum_fusion.refs_0_.own_ref), channel_id=1, source_target_pairs={{0,64},{4,68},{8,72},{12,76},{16,80},{20,84},{24,88},{28,92},{32,9... | collective-permute-start | bytes 393224 | tf_op jit(solution)/shard_map/ppermute | solution.py:41
  7.2 31.2 %collective-permute-start.1 = (bf16[4,64,256]{2,1,0:T(8,128)(2,1)S(1)}, bf16[4,64,256]{2,1,0:T(8,128)(2,1)S(1)}, u32[]{:S(2)}, u32[]{:S(2)}) collective-permute-start(bf16[4,64,256]{2,1,0:T(8,128)(2,1)S(1)} %pad_maximum_fusion.refs_0_.own_ref), channel_id=1, source_target_pairs={{0,195},{4,199},{8,203},{12,207},{16,211},{20,215},{24,219},{28,22... | collective-permute-start | bytes 393224 | tf_op jit(solution)/shard_map/ppermute | solution.py:41
  26.5 11.8 %collective-permute-start.2 = (bf16[4,64,256]{2,1,0:T(8,128)(2,1)S(1)}, bf16[4,64,256]{2,1,0:T(8,128)(2,1)S(1)}, u32[]{:S(2)}, u32[]{:S(2)}) collective-permute-start(bf16[4,64,256]{2,1,0:T(8,128)(2,1)S(1)} %collective-permute-done.refs_1_), channel_id=1, source_target_pairs={{0,64},{4,68},{8,72},{12,76},{16,80},{20,84},{24,88},{28,92},{32,9... | collective-permute-start | bytes 393224 | tf_op jit(solution)/shard_map/ppermute | solution.py:41
  40.5 30.8 %copy-start.1 = (bf16[256,4,128]{2,1,0:T(4,128)(2,1)S(1)}, bf16[256,4,128]{2,1,0:T(4,128)(2,1)}, u32[]{:S(2)}) copy-start(bf16[256,4,128]{2,1,0:T(4,128)(2,1)} %param.5) | copy-start | bytes 786436
  40.5 30.8 %copy-start.2 = (bf16[256,4,128]{2,1,0:T(4,128)(2,1)S(1)}, bf16[256,4,128]{2,1,0:T(4,128)(2,1)}, u32[]{:S(2)}) copy-start(bf16[256,4,128]{2,1,0:T(4,128)(2,1)} %param.8) | copy-start | bytes 786436
  40.5 30.7 %all-to-all-start.1 = ((bf16[16,4,64,256]{3,2,1,0:T(8,128)(2,1)}), bf16[16,4,64,256]{3,2,1,0:T(8,128)(2,1)S(1)}, u32[]{:S(2)}, u32[]{:S(2)}) async-start(bf16[16,4,64,256]{3,2,1,0:T(8,128)(2,1)} %pick_blocks.1), calls=%async_computation.1 | async-start | bytes 4194304 | tf_op jit(solution)/shard_map/all_to_all | solution.py:204
  109.5 11.2 %collective-permute-start.3 = (bf16[4,64,256]{2,1,0:T(8,128)(2,1)S(1)}, bf16[4,64,256]{2,1,0:T(8,128)(2,1)S(1)}, u32[]{:S(2)}, u32[]{:S(2)}) collective-permute-start(bf16[4,64,256]{2,1,0:T(8,128)(2,1)S(1)} %get-tuple-element.14), channel_id=1, source_target_pairs={{0,195},{4,199},{8,203},{12,207},{16,211},{20,215},{24,219},{28,22... | collective-permute-start | bytes 393224 | tf_op jit(solution)/shard_map/ppermute | solution.py:41
  115.5 12.8 %collective-permute-start.5 = (bf16[4,64,256]{2,1,0:T(8,128)(2,1)S(1)}, bf16[4,64,256]{2,1,0:T(8,128)(2,1)S(1)}, u32[]{:S(2)}, u32[]{:S(2)}) collective-permute-start(bf16[4,64,256]{2,1,0:T(8,128)(2,1)S(1)} %get-tuple-element.16), channel_id=1, source_target_pairs={{0,64},{4,68},{8,72},{12,76},{16,80},{20,84},{24,88},{28,92},{32,9... | collective-permute-start | bytes 393224 | tf_op jit(solution)/shard_map/ppermute | solution.py:41
  120.7 10.8 %collective-permute-start.4 = (bf16[4,64,256]{2,1,0:T(8,128)(2,1)S(1)}, bf16[4,64,256]{2,1,0:T(8,128)(2,1)S(1)}, u32[]{:S(2)}, u32[]{:S(2)}) collective-permute-start(bf16[4,64,256]{2,1,0:T(8,128)(2,1)S(1)} %add_convert_fusion.1), channel_id=1, source_target_pairs={{0,195},{4,199},{8,203},{12,207},{16,211},{20,215},{24,219},{28,22... | collective-permute-start | bytes 393224 | tf_op jit(solution)/shard_map/ppermute | solution.py:41

commit v12 on v11

--- a/solution.py
+++ b/solution.py
@@ -178,6 +178,21 @@
     return (a.astype(F32) + b.astype(F32)).astype(BF16)
 
 
+def heads_body(in_ref, key_ref, value_ref):
+    width = key_ref.shape[2]
+    for y in range(NY):
+        total = in_ref[y * ZH].astype(F32)
+        for zh in range(1, ZH):
+            total += in_ref[y * ZH + zh].astype(F32)
+        key_ref[:, y, :] = total[:, :width]
+        value_ref[:, y, :] = total[:, width:]
+
+
+def sum_heads(pieces, width):
+    out = jax.ShapeDtypeStruct((pieces.shape[1], NY, width), F32)
+    return pl.pallas_call(heads_body, out_shape=[out, out], name="sum_heads")(pieces)
+
+
 def on_device(queries, key_states, values, grad_out, picked_blocks):
     tokens, heads, width = queries.shape
     blocks = tokens // BLK
@@ -217,9 +232,7 @@
 
     pieces = total.astype(BF16).reshape(NY * ZH, tokens // (NY * ZH), 2 * width)
     pieces = lax.all_to_all(pieces, HEAD, split_axis=0, concat_axis=0, tiled=True)
-    summed = pieces.astype(F32).reshape(NY, ZH, tokens // (NY * ZH), 2 * width).sum(axis=1)
-    summed = summed.transpose(1, 0, 2)
-    return (grad_queries, summed[:, :, :width], summed[:, :, width:])
+    return (grad_queries, *sum_heads(pieces, width))
 
 
 def solution(mesh):

time: 183 us -> 184 us (level)
  no operation moved by 1% of the time
where the time goes in v12:
time: 184 us
  blocking collectives  90.7 us (49%)
  starting transfers between devices  42.5 us (23%)
  waiting for transfers between devices  36.6 us (20%)
  Pallas kernels  11.5 us (6%)
  local copies, waits for them, and re-layouts  1.85 us (1%)
    all_to_all x1, blocking collectives, on_device(): lax.all_to_all(pieces, HEAD, split_axis=0, concat_axis=0, tiled=True)  51 us
    ppermute x6, starting transfers between devices, send(): return lax.ppermute(array, AXES, pairs)  36.5 us
    all_to_all x1, blocking collectives, on_device(): lax.all_to_all(back.reshape(PEERS, ZS, BLK, 2 * width), SIDE, split_axis=...  30.3 us
    all_to_all x1, waiting for transfers between devices, on_device(): lax.all_to_all(pick_blocks(asked, near), SIDE, split_axis=0, concat_axis=...  24.7 us
    ppermute x6, waiting for transfers between devices, send(): return lax.ppermute(array, AXES, pairs)  11.9 us
    all_to_all x1, blocking collectives, on_device(): lax.all_to_all(wanted.reshape(PEERS, ZS), SIDE, split_axis=0, concat_axis...  9.34 us
    pallas_call x1, Pallas kernels, attend_grads(): pl.pallas_call(attend_body, grid_spec=pltpu.PrefetchScalarGridSpec(num_sc...  6.54 us
    all_to_all x1, starting transfers between devices, on_device(): lax.all_to_all(pick_blocks(asked, near), SIDE, split_axis=0, concat_axis=...  6.02 us
  transfers between devices with their start and end apart: 7, of which 5 were waited for; matrix products, arithmetic and copies ran while one was open for 0% of the time, Pallas kernels for 0%

profile of v12, /device:TPU:34, one launch (start us, length us, event | category | flops | bytes accessed | tf_op | source)
XLA Modules:
  0.0 184.2 jit_solution(12081860534918526226)
XLA Ops:
  0.6 0.0 copy-start
  0.7 1.3 constant_dynamic-slice_fusion
  2.0 5.2 %collective-permute-start = (bf16[4,64,256]{2,1,0:T(8,128)(2,1)S(1)}, bf16[4,64,256]{2,1,0:T(8,128)(2,1)S(1)}, u32[]{:S(2)}, u32[]{:S(2)}) collective-permute-start(bf16[4,64,256]{2,1,0:T(8,128)(2,1)S(1)} %pad_maximum_fusion.refs_0_.own_ref), channel_id=1, source_target_pairs={{0,64},{4,68},{8,72},{12,76},{16,80},{20,84},{24,88},{28,92},{32,9... | collective-permute-start | bytes 393224 | tf_op jit(solution)/shard_map/ppermute | solution.py:41
  7.2 15.0 %collective-permute-start.1 = (bf16[4,64,256]{2,1,0:T(8,128)(2,1)S(1)}, bf16[4,64,256]{2,1,0:T(8,128)(2,1)S(1)}, u32[]{:S(2)}, u32[]{:S(2)}) collective-permute-start(bf16[4,64,256]{2,1,0:T(8,128)(2,1)S(1)} %pad_maximum_fusion.refs_0_.own_ref), channel_id=1, source_target_pairs={{0,195},{4,199},{8,203},{12,207},{16,211},{20,215},{24,219},{28,22... | collective-permute-start | bytes 393224 | tf_op jit(solution)/shard_map/ppermute | solution.py:41
  22.2 0.0 copy-done
  22.2 4.3 %collective-permute-done.refs_1_ = bf16[4,64,256]{2,1,0:T(8,128)(2,1)S(1)} collective-permute-done((bf16[4,64,256]{2,1,0:T(8,128)(2,1)S(1)}, bf16[4,64,256]{2,1,0:T(8,128)(2,1)S(1)}, u32[]{:S(2)}, u32[]{:S(2)}) %collective-permute-start) | collective-permute-done | bytes 131104 | tf_op jit(solution)/shard_map/ppermute | solution.py:41
  26.5 1.9 %collective-permute-start.2 = (bf16[4,64,256]{2,1,0:T(8,128)(2,1)S(1)}, bf16[4,64,256]{2,1,0:T(8,128)(2,1)S(1)}, u32[]{:S(2)}, u32[]{:S(2)}) collective-permute-start(bf16[4,64,256]{2,1,0:T(8,128)(2,1)S(1)} %collective-permute-done.refs_1_), channel_id=1, source_target_pairs={{0,64},{4,68},{8,72},{12,76},{16,80},{20,84},{24,88},{28,92},{32,9... | collective-permute-start | bytes 393224 | tf_op jit(solution)/shard_map/ppermute | solution.py:41
  28.5 0.1 slice.7
  28.6 0.1 slice.6
  28.6 0.1 copy.24
  28.7 0.1 copy.25
  28.8 0.1 select_reduce_fusion
  29.0 0.1 all_to_all.16
  29.0 9.3 %all_to_all.26 = s32[16,1,4]{2,1,0:T(1,128)S(1)} all-to-all(s32[16,1,4]{2,1,0:T(1,128)S(1)} %bitcast.20), channel_id=1, replica_groups=mesh['x'=4,'zs'=4,'zb'=2,'c'=2,'y'=4,'zh'=4] {'x','zb','c'}, dimensions={0} | all-to-all | bytes 512 | tf_op jit(solution)/shard_map/all_to_all | solution.py:214
  38.4 0.0 collective-permute-done.1.refs_2_
  38.4 0.0 collective-permute-done.2.refs_3_
  38.4 2.1 %pick_blocks.1 = bf16[16,4,64,256]{3,2,1,0:T(8,128)(2,1)} custom-call(s32[16,4]{1,0:T(8,128)S(1)} %bitcast.15, bf16[4,64,256]{2,1,0:T(8,128)(2,1)S(1)} %pad_maximum_fusion.refs_0_.own_ref, bf16[4,64,256]{2,1,0:T(8,128)(2,1)S(1)} %collective-permute-done.refs_1_, bf16[4,64,256]{2,1,0:T(8,128)(2,1)S(1)} %collective-permute-done.1.refs_2_, ...), custom_call_target="tpu_custom_call" | custom-call | tf_op jit(solution)/shard_map/pick_blocks/pallas_call | solution.py:135
  40.5 0.0 copy-start.1
  40.5 0.0 copy-start.2
  40.5 6.0 %all-to-all-start.1 = ((bf16[16,4,64,256]{3,2,1,0:T(8,128)(2,1)}), bf16[16,4,64,256]{3,2,1,0:T(8,128)(2,1)S(1)}, u32[]{:S(2)}, u32[]{:S(2)}) async-start(bf16[16,4,64,256]{3,2,1,0:T(8,128)(2,1)} %pick_blocks.1), calls=%async_computation.1 | async-start | bytes 4194304 | tf_op jit(solution)/shard_map/all_to_all | solution.py:219
  46.6 24.7 %all-to-all-done.1 = bf16[16,4,64,256]{3,2,1,0:T(8,128)(2,1)S(1)} async-done(((bf16[16,4,64,256]{3,2,1,0:T(8,128)(2,1)}), bf16[16,4,64,256]{3,2,1,0:T(8,128)(2,1)S(1)}, u32[]{:S(2)}, u32[]{:S(2)}) %all-to-all-start.1) | async-done | bytes 2097184 | tf_op jit(solution)/shard_map/all_to_all | solution.py:219
  71.2 0.1 broadcast_in_dim.33.bias_ref
  71.3 0.0 copy-done.1
  71.3 0.0 copy-done.2
  71.3 6.5 %attend_grads.1 = (f32[1024,128]{1,0:T(8,128)}, f32[4,64,256]{2,1,0:T(8,128)S(1)}, bf16[64,64,256]{2,1,0:T(8,128)(2,1)S(1)}) custom-call(s32[4,16]{1,0:T(4,128)S(1)} %get-tuple-element.22.slot_ref, bf16[1024,128]{1,0:T(8,128)(2,1)S(1)} %bitcast.13, bf16[1024,128]{1,0:T(8,128)(2,1)S(1)} %bitcast.14, bf16[4,64,256]{2,1,0:T(8,128)(2,1)S(1)} %pad_maximum_fusion.refs_0_.own_ref, ...), custom_call_target="tpu_custom_call" | custom-call | tf_op jit(solution)/shard_map/attend_grads/pallas_call | solution.py:105
  77.9 30.3 %all_to_all.27.in_ref = bf16[16,4,64,256]{3,2,1,0:T(8,128)(2,1)S(1)} all-to-all(bf16[16,4,64,256]{3,2,1,0:T(8,128)(2,1)S(1)} %bitcast.12), channel_id=1, replica_groups=mesh['x'=4,'zs'=4,'zb'=2,'c'=2,'y'=4,'zh'=4] {'x','zb','c'}, dimensions={0} | all-to-all | bytes 4194304 | tf_op jit(solution)/shard_map/all_to_all | solution.py:228
  108.2 1.3 sum_parts.1
  109.5 6.0 %collective-permute-start.3 = (bf16[4,64,256]{2,1,0:T(8,128)(2,1)S(1)}, bf16[4,64,256]{2,1,0:T(8,128)(2,1)S(1)}, u32[]{:S(2)}, u32[]{:S(2)}) collective-permute-start(bf16[4,64,256]{2,1,0:T(8,128)(2,1)S(1)} %get-tuple-element.16), channel_id=1, source_target_pairs={{0,195},{4,199},{8,203},{12,207},{16,211},{20,215},{24,219},{28,22... | collective-permute-start | bytes 393224 | tf_op jit(solution)/shard_map/ppermute | solution.py:41
  115.5 1.9 %collective-permute-start.5 = (bf16[4,64,256]{2,1,0:T(8,128)(2,1)S(1)}, bf16[4,64,256]{2,1,0:T(8,128)(2,1)S(1)}, u32[]{:S(2)}, u32[]{:S(2)}) collective-permute-start(bf16[4,64,256]{2,1,0:T(8,128)(2,1)S(1)} %get-tuple-element.18), channel_id=1, source_target_pairs={{0,64},{4,68},{8,72},{12,76},{16,80},{20,84},{24,88},{28,92},{32,9... | collective-permute-start | bytes 393224 | tf_op jit(solution)/shard_map/ppermute | solution.py:41
  117.5 3.2 %collective-permute-done.3 = bf16[4,64,256]{2,1,0:T(8,128)(2,1)S(1)} collective-permute-done((bf16[4,64,256]{2,1,0:T(8,128)(2,1)S(1)}, bf16[4,64,256]{2,1,0:T(8,128)(2,1)S(1)}, u32[]{:S(2)}, u32[]{:S(2)}) %collective-permute-start.3) | collective-permute-done | bytes 131104 | tf_op jit(solution)/shard_map/ppermute | solution.py:41
  120.7 6.5 %collective-permute-start.4 = (bf16[4,64,256]{2,1,0:T(8,128)(2,1)S(1)}, bf16[4,64,256]{2,1,0:T(8,128)(2,1)S(1)}, u32[]{:S(2)}, u32[]{:S(2)}) collective-permute-start(bf16[4,64,256]{2,1,0:T(8,128)(2,1)S(1)} %add_convert_fusion.1), channel_id=1, source_target_pairs={{0,195},{4,199},{8,203},{12,207},{16,211},{20,215},{24,219},{28,22... | collective-permute-start | bytes 393224 | tf_op jit(solution)/shard_map/ppermute | solution.py:41
  127.2 1.1 collective-permute-done.5
  128.3 3.2 %collective-permute-done.4 = bf16[4,64,256]{2,1,0:T(8,128)(2,1)S(1)} collective-permute-done((bf16[4,64,256]{2,1,0:T(8,128)(2,1)S(1)}, bf16[4,64,256]{2,1,0:T(8,128)(2,1)S(1)}, u32[]{:S(2)}, u32[]{:S(2)}) %collective-permute-start.4) | collective-permute-done | bytes 131104 | tf_op jit(solution)/shard_map/ppermute | solution.py:41
  131.5 0.1 add_convert_fusion
  131.6 51.0 %all_to_all.28.in_ref = bf16[16,16,256]{2,1,0:T(8,128)(2,1)} all-to-all(bf16[16,16,256]{2,1,0:T(8,128)(2,1)S(1)} %bitcast.17), channel_id=1, replica_groups=mesh['x'=4,'zs'=4,'zb'=2,'c'=2,'y'=4,'zh'=4] {'y','zh'}, dimensions={0} | all-to-all | bytes 262144 | tf_op jit(solution)/shard_map/all_to_all | solution.py:234
  182.6 1.6 sum_heads.1
  (7 shorter events, 0.1 us)
Async XLA Ops:
  0.6 21.6 %copy-start = (s32[4,4,16]{2,1,0:T(4,128)S(1)}, s32[4,4,16]{2,1,0:T(4,128)}, u32[]{:S(2)}) copy-start(s32[4,4,16]{2,1,0:T(4,128)} %param.9) | copy-start | bytes 3076
  2.0 24.5 %collective-permute-start = (bf16[4,64,256]{2,1,0:T(8,128)(2,1)S(1)}, bf16[4,64,256]{2,1,0:T(8,128)(2,1)S(1)}, u32[]{:S(2)}, u32[]{:S(2)}) collective-permute-start(bf16[4,64,256]{2,1,0:T(8,128)(2,1)S(1)} %pad_maximum_fusion.refs_0_.own_ref), channel_id=1, source_target_pairs={{0,64},{4,68},{8,72},{12,76},{16,80},{20,84},{24,88},{28,92},{32,9... | collective-permute-start | bytes 393224 | tf_op jit(solution)/shard_map/ppermute | solution.py:41
  7.2 31.2 %collective-permute-start.1 = (bf16[4,64,256]{2,1,0:T(8,128)(2,1)S(1)}, bf16[4,64,256]{2,1,0:T(8,128)(2,1)S(1)}, u32[]{:S(2)}, u32[]{:S(2)}) collective-permute-start(bf16[4,64,256]{2,1,0:T(8,128)(2,1)S(1)} %pad_maximum_fusion.refs_0_.own_ref), channel_id=1, source_target_pairs={{0,195},{4,199},{8,203},{12,207},{16,211},{20,215},{24,219},{28,22... | collective-permute-start | bytes 393224 | tf_op jit(solution)/shard_map/ppermute | solution.py:41
  26.5 11.8 %collective-permute-start.2 = (bf16[4,64,256]{2,1,0:T(8,128)(2,1)S(1)}, bf16[4,64,256]{2,1,0:T(8,128)(2,1)S(1)}, u32[]{:S(2)}, u32[]{:S(2)}) collective-permute-start(bf16[4,64,256]{2,1,0:T(8,128)(2,1)S(1)} %collective-permute-done.refs_1_), channel_id=1, source_target_pairs={{0,64},{4,68},{8,72},{12,76},{16,80},{20,84},{24,88},{28,92},{32,9... | collective-permute-start | bytes 393224 | tf_op jit(solution)/shard_map/ppermute | solution.py:41
  40.5 30.8 %copy-start.1 = (bf16[256,4,128]{2,1,0:T(4,128)(2,1)S(1)}, bf16[256,4,128]{2,1,0:T(4,128)(2,1)}, u32[]{:S(2)}) copy-start(bf16[256,4,128]{2,1,0:T(4,128)(2,1)} %param.5) | copy-start | bytes 786436
  40.5 30.8 %copy-start.2 = (bf16[256,4,128]{2,1,0:T(4,128)(2,1)S(1)}, bf16[256,4,128]{2,1,0:T(4,128)(2,1)}, u32[]{:S(2)}) copy-start(bf16[256,4,128]{2,1,0:T(4,128)(2,1)} %param.8) | copy-start | bytes 786436
  40.5 30.7 %all-to-all-start.1 = ((bf16[16,4,64,256]{3,2,1,0:T(8,128)(2,1)}), bf16[16,4,64,256]{3,2,1,0:T(8,128)(2,1)S(1)}, u32[]{:S(2)}, u32[]{:S(2)}) async-start(bf16[16,4,64,256]{3,2,1,0:T(8,128)(2,1)} %pick_blocks.1), calls=%async_computation.1 | async-start | bytes 4194304 | tf_op jit(solution)/shard_map/all_to_all | solution.py:219
  109.5 11.2 %collective-permute-start.3 = (bf16[4,64,256]{2,1,0:T(8,128)(2,1)S(1)}, bf16[4,64,256]{2,1,0:T(8,128)(2,1)S(1)}, u32[]{:S(2)}, u32[]{:S(2)}) collective-permute-start(bf16[4,64,256]{2,1,0:T(8,128)(2,1)S(1)} %get-tuple-element.16), channel_id=1, source_target_pairs={{0,195},{4,199},{8,203},{12,207},{16,211},{20,215},{24,219},{28,22... | collective-permute-start | bytes 393224 | tf_op jit(solution)/shard_map/ppermute | solution.py:41
  115.5 12.8 %collective-permute-start.5 = (bf16[4,64,256]{2,1,0:T(8,128)(2,1)S(1)}, bf16[4,64,256]{2,1,0:T(8,128)(2,1)S(1)}, u32[]{:S(2)}, u32[]{:S(2)}) collective-permute-start(bf16[4,64,256]{2,1,0:T(8,128)(2,1)S(1)} %get-tuple-element.18), channel_id=1, source_target_pairs={{0,64},{4,68},{8,72},{12,76},{16,80},{20,84},{24,88},{28,92},{32,9... | collective-permute-start | bytes 393224 | tf_op jit(solution)/shard_map/ppermute | solution.py:41
  120.7 10.8 %collective-permute-start.4 = (bf16[4,64,256]{2,1,0:T(8,128)(2,1)S(1)}, bf16[4,64,256]{2,1,0:T(8,128)(2,1)S(1)}, u32[]{:S(2)}, u32[]{:S(2)}) collective-permute-start(bf16[4,64,256]{2,1,0:T(8,128)(2,1)S(1)} %add_convert_fusion.1), channel_id=1, source_target_pairs={{0,195},{4,199},{8,203},{12,207},{16,211},{20,215},{24,219},{28,22... | collective-permute-start | bytes 393224 | tf_op jit(solution)/shard_map/ppermute | solution.py:41
